TPU v7x, 32 devices: a whole 2x2x4 slice. The times are simulated.
32 devices in a mesh: dev: 32 (over z, y, x, core).
Axes of the slice: x: 2, y: 2, z: 4, core: 2. Of those that a mesh axis runs over, the one named last changes fastest.
Arguments:
- tokens: bfloat16 [12288, 576], P('dev'), may hold values from -8 to 8
- positions: int32 [12288], P('dev'), may hold values from 0 to 383, as said below
- gain_attn: float32 [576], replicated, may hold values from 0.1 to 1.9
- w_query: bfloat16 [331776], P('dev'), may hold values from -2 to 2
- w_kv: bfloat16 [221184], P('dev'), may hold values from -2 to 2
- w_out: bfloat16 [331776], P('dev'), may hold values from -1.5 to 1.5
- gain_ffn: float32 [576], replicated, may hold values from 0.1 to 1.9
- w_gate_up: bfloat16 [1769472], P('dev'), may hold values from -0.25 to 0.25
- w_down: bfloat16 [884736], P('dev'), may hold values from -0.15625 to 0.15625
- cotangent: bfloat16 [12288, 576], P('dev'), may hold values from -16 to 16
Outputs:
- mixed: bfloat16 [12288, 576], P('dev')
- d_tokens: float32 [12288, 576], P('dev')
- d_gain_attn: float32 [576], replicated
- d_query: float32 [331776], P('dev')
- d_kv: float32 [221184], P('dev')
- d_out: float32 [331776], P('dev')
- d_gain_ffn: float32 [576], replicated
- d_gate_up: float32 [1769472], P('dev')
- d_down: float32 [884736], P('dev')
Inputs may be any that keep to these rules, and one draw needn't show every extreme that they name: positions count 0 at a document's first token and rise by one along it; documents lie end to end, so token t's document begins at token t - positions[t]; token 0 has position 0; some document has exactly 384 tokens.
All inputs are finite; a program needn't handle non-finite values.
Results may differ from a plain program's by a relative error of at most 0.012.
Values may be sent and summed in bfloat16 or wider, within the bound.
No kernel may reach another device: no remote copies, remote signals or barrier semaphores. Data moves between devices by JAX's collectives and lax.ppermute only.
A program may use at most 128 MiB of HBM per device.

v0:
```python
import math

import jax
import jax.numpy as jnp
from jax import lax
from jax.experimental import pallas as pl
from jax.experimental.pallas import tpu as pltpu
from jax.sharding import PartitionSpec as P

D = 576
H = 9
KVH = 3
HD = 64
FF = 1536


norm_epsilon = 1e-05
theta_base = 100000.0


def passed_along(value, axis, steps):
    count = lax.axis_size(axis)
    first, last = (max(0, -steps), min(count, count - steps))
    return lax.ppermute(value, axis, [(source, source + steps) for source in range(first, last)])


def link_masks(count):
    bits = [1 << b for b in range(count.bit_length() - 1)]
    if count == 32:
        bits = [1, 2, 4, 8, 24]
    return bits[0], bits[1:]


def swapped(value, mask):
    count = lax.axis_size("dev")
    return lax.ppermute(value, "dev", [(i, i ^ mask) for i in range(count)])


def color_orders(count, colors):
    first, rest = link_masks(count)
    if colors == 1:
        return [rest + [first]]
    step = len(rest) // colors
    return [rest[c * step :] + rest[: c * step] + [first] for c in range(colors)]


def slot_masks(order):
    slots = [0]
    for mask in order:
        slots = slots + [s ^ mask for s in slots]
    return slots


def cut_rows(rows, colors):
    edges = [rows * c // colors for c in range(colors + 1)]
    return list(zip(edges[:-1], edges[1:]))


def gather_all(block, colors):
    count = lax.axis_size("dev")
    me = lax.axis_index("dev")
    orders = color_orders(count, colors)
    held = [block[a:b][None] for a, b in cut_rows(block.shape[0], colors)]
    for t in range(len(orders[0])):
        got = [swapped(h, order[t]) for h, order in zip(held, orders)]
        held = [jnp.concatenate([h, g], axis=0) for h, g in zip(held, got)]
    whole = []
    for h, order in zip(held, orders):
        slots = slot_masks(order)
        where = [0] * count
        for place, mask in enumerate(slots):
            where[mask] = place
        index = jnp.asarray(where, jnp.int32)[me ^ jnp.arange(count, dtype=jnp.int32)]
        whole.append(jnp.take(h, index, axis=0, mode="clip"))
    return jnp.concatenate(whole, axis=1)


def scatter_sum(parts, colors):
    count = lax.axis_size("dev")
    me = lax.axis_index("dev")
    orders = color_orders(count, colors)
    held = []
    for (a, b), order in zip(cut_rows(parts.shape[1], colors), orders):
        slots = jnp.asarray(slot_masks(order), jnp.int32)
        held.append(jnp.take(parts[:, a:b], me ^ slots, axis=0, mode="clip"))
    for t in range(len(orders[0])):
        half = held[0].shape[0] // 2
        masks = [order[-1 - t] for order in orders]
        got = [swapped(h[half:].astype(jnp.bfloat16), m) for h, m in zip(held, masks)]
        held = [h[:half].astype(jnp.float32) + g.astype(jnp.float32) for h, g in zip(held, got)]
    return jnp.concatenate([h[0] for h in held], axis=0)


def sum_all(value):
    first, rest = link_masks(lax.axis_size("dev"))
    for mask in [first] + rest:
        value = value + swapped(value, mask)
    return value


def norm_forward(values, scale_gain):
    inverse = lax.rsqrt(jnp.mean(values * values, axis=-1, keepdims=True) + norm_epsilon)
    return (values * inverse * scale_gain, inverse)


def norm_backward(grad_output, values, inverse, scale_gain):
    unit_rows = values * inverse
    scaled = grad_output * scale_gain
    grad_gain = jnp.sum(grad_output * unit_rows, axis=0)
    grad_input = inverse * (
        scaled - unit_rows * jnp.mean(scaled * unit_rows, axis=-1, keepdims=True)
    )
    return (grad_input, grad_gain)


def rope_angles(position_block):
    half_dim = HD // 2
    frequency = jnp.exp(
        jnp.arange(half_dim, dtype=jnp.float32) * (-2.0 * math.log(theta_base) / HD)
    )
    angles = position_block.astype(jnp.float32)[:, None] * frequency[None, :]
    return (jnp.cos(angles)[:, None, :], jnp.sin(angles)[:, None, :])


def rotate(values, cos_table, sin_table):
    half_dim = values.shape[-1] // 2
    first_half = values[..., :half_dim]
    second_half = values[..., half_dim:]
    return jnp.concatenate(
        [
            first_half * cos_table - second_half * sin_table,
            second_half * cos_table + first_half * sin_table,
        ],
        axis=-1,
    )


def project_heads(normed, query_mat, keyval_mat, cos_table, sin_table):
    row_count = normed.shape[0]
    queries = jnp.dot(normed, query_mat, preferred_element_type=jnp.float32).reshape(
        row_count, H, HD
    )
    keyvals = jnp.dot(normed, keyval_mat, preferred_element_type=jnp.float32)
    keys_rot = rotate(
        keyvals[:, : KVH * HD].reshape(row_count, KVH, HD), cos_table, sin_table
    ).reshape(row_count, KVH * HD)
    query_rot = (
        rotate(queries, cos_table, sin_table).reshape(row_count, H * HD).astype(jnp.bfloat16)
    )
    keyval_rot = jnp.concatenate([keys_rot, keyvals[:, KVH * HD :]], axis=1).astype(jnp.bfloat16)
    return (query_rot, keyval_rot)


def window_mask(position_block, row_count):
    query_at = jnp.arange(row_count, dtype=jnp.int32)[:, None] + row_count
    key_at = jnp.arange(2 * row_count, dtype=jnp.int32)[None, :]
    return (key_at <= query_at) & (key_at >= query_at - position_block[:, None])


def masked_scores(query_group, key_group, allowed):
    scale_factor = 1.0 / math.sqrt(HD)
    scores = (
        jnp.einsum("tqd,wd->qtw", query_group, key_group, preferred_element_type=jnp.float32)
        * scale_factor
    )
    return jnp.where(allowed[None], scores, -1e30)


def attend_forward(query_rot, window, allowed):
    row_count = query_rot.shape[0]
    grouped = H // KVH
    queries = query_rot.reshape(row_count, H, HD)
    outputs = []
    totals = []
    for group_index in range(KVH):
        query_group = queries[:, group_index * grouped : (group_index + 1) * grouped]
        key_group = window[:, group_index * HD : (group_index + 1) * HD]
        value_group = window[:, (KVH + group_index) * HD : (KVH + group_index + 1) * HD]
        scores = masked_scores(query_group, key_group, allowed)
        highest = jnp.max(scores, axis=-1, keepdims=True)
        log_total = highest + jnp.log(jnp.sum(jnp.exp(scores - highest), axis=-1, keepdims=True))
        probability = jnp.exp(scores - log_total).astype(jnp.bfloat16)
        head_out = jnp.einsum(
            "qtw,wd->tqd", probability, value_group, preferred_element_type=jnp.float32
        )
        outputs.append(head_out.astype(jnp.bfloat16))
        totals.append(log_total)
    return (jnp.concatenate(outputs, axis=1).reshape(row_count, H * HD), totals)


def attend_backward(query_rot, window, allowed, attended, grad_attended, totals):
    row_count = query_rot.shape[0]
    grouped = H // KVH
    scale_factor = 1.0 / math.sqrt(HD)
    queries = query_rot.reshape(row_count, H, HD)
    attended_heads = attended.reshape(row_count, H, HD)
    grad_heads = grad_attended.reshape(row_count, H, HD)
    query_grads = []
    key_grads = []
    value_grads = []
    for group_index in range(KVH):
        head_slice = slice(group_index * grouped, (group_index + 1) * grouped)
        query_group = queries[:, head_slice]
        key_group = window[:, group_index * HD : (group_index + 1) * HD]
        value_group = window[:, (KVH + group_index) * HD : (KVH + group_index + 1) * HD]
        scores = masked_scores(query_group, key_group, allowed)
        probability = jnp.exp(scores - totals[group_index])
        grad_group = grad_heads[:, head_slice]
        row_delta = jnp.sum(
            grad_group.astype(jnp.float32) * attended_heads[:, head_slice].astype(jnp.float32),
            axis=-1,
        )
        grad_prob = jnp.einsum(
            "tqd,wd->qtw", grad_group, value_group, preferred_element_type=jnp.float32
        )
        grad_scores = (probability * (grad_prob - row_delta.T[:, :, None]) * scale_factor).astype(
            jnp.bfloat16
        )
        query_grads.append(
            jnp.einsum("qtw,wd->tqd", grad_scores, key_group, preferred_element_type=jnp.float32)
        )
        key_grads.append(
            jnp.einsum("qtw,tqd->wd", grad_scores, query_group, preferred_element_type=jnp.float32)
        )
        value_grads.append(
            jnp.einsum(
                "qtw,tqd->wd",
                probability.astype(jnp.bfloat16),
                grad_group,
                preferred_element_type=jnp.float32,
            )
        )
    return (jnp.concatenate(query_grads, axis=1), jnp.concatenate(key_grads + value_grads, axis=1))


def shards_general(
    tokens, positions, gain_attn, w_query, w_kv, w_out, gain_ffn, w_gate_up, w_down, cotangent
):
    row_count = tokens.shape[0]
    width_kv = 2 * KVH * HD
    count = lax.axis_size("dev")
    attn_sizes = [w_query.shape[0], w_kv.shape[0], w_out.shape[0]]
    ffn_sizes = [w_gate_up.shape[0], w_down.shape[0]]
    attn_all = gather_all(jnp.concatenate([w_query, w_kv, w_out]).reshape(-1, 128), 2)
    attn_all = attn_all.reshape(count, -1)
    query_mat = attn_all[:, : attn_sizes[0]].reshape(D, H * HD)
    keyval_mat = attn_all[:, attn_sizes[0] : attn_sizes[0] + attn_sizes[1]].reshape(D, width_kv)
    out_mat = attn_all[:, attn_sizes[0] + attn_sizes[1] :].reshape(H * HD, D)
    ffn_all = gather_all(jnp.concatenate([w_gate_up, w_down]).reshape(-1, 128), 4)
    ffn_all = ffn_all.reshape(count, -1)
    gate_up_mat = ffn_all[:, : ffn_sizes[0]].reshape(D, 2 * FF)
    down_mat = ffn_all[:, ffn_sizes[0] :].reshape(FF, D)
    inputs = tokens.astype(jnp.float32)
    normed_attn, inverse_attn = norm_forward(inputs, gain_attn)
    normed_attn = normed_attn.astype(jnp.bfloat16)
    cos_table, sin_table = rope_angles(positions)
    query_rot, keyval_rot = project_heads(normed_attn, query_mat, keyval_mat, cos_table, sin_table)
    near_keys = passed_along(keyval_rot, "dev", 1)
    window = jnp.concatenate([near_keys, keyval_rot], axis=0)
    allowed = window_mask(positions, row_count)
    attended, totals = attend_forward(query_rot, window, allowed)
    residual = inputs + jnp.dot(attended, out_mat, preferred_element_type=jnp.float32)
    normed_ffn, inverse_ffn = norm_forward(residual, gain_ffn)
    normed_ffn = normed_ffn.astype(jnp.bfloat16)
    gate_up = jnp.dot(normed_ffn, gate_up_mat, preferred_element_type=jnp.float32)
    gate_part = gate_up[:, :FF]
    up_part = gate_up[:, FF:]
    activated = (jax.nn.silu(gate_part) * up_part).astype(jnp.bfloat16)
    mixed = (residual + jnp.dot(activated, down_mat, preferred_element_type=jnp.float32)).astype(
        jnp.bfloat16
    )
    grad_act = jnp.dot(cotangent, down_mat.T, preferred_element_type=jnp.float32)
    sigmoid_gate = jax.nn.sigmoid(gate_part)
    grad_gate_up_act = jnp.concatenate(
        [
            grad_act * up_part * sigmoid_gate * (1.0 + gate_part * (1.0 - sigmoid_gate)),
            grad_act * jax.nn.silu(gate_part),
        ],
        axis=1,
    ).astype(jnp.bfloat16)
    grad_down = jnp.dot(activated.T, cotangent, preferred_element_type=jnp.float32)
    grad_gate_up = jnp.dot(normed_ffn.T, grad_gate_up_act, preferred_element_type=jnp.float32)
    grad_normed_ffn = jnp.dot(grad_gate_up_act, gate_up_mat.T, preferred_element_type=jnp.float32)
    grad_norm_ffn, grad_gain_ffn = norm_backward(grad_normed_ffn, residual, inverse_ffn, gain_ffn)
    grad_residual = cotangent.astype(jnp.float32) + grad_norm_ffn
    grad_residual_b = grad_residual.astype(jnp.bfloat16)
    grad_out = jnp.dot(attended.T, grad_residual_b, preferred_element_type=jnp.float32)
    grad_attended = jnp.dot(grad_residual_b, out_mat.T, preferred_element_type=jnp.float32).astype(
        jnp.bfloat16
    )
    grad_query_rot, grad_window = attend_backward(
        query_rot, window, allowed, attended, grad_attended, totals
    )
    back_near = passed_along(grad_window[:row_count].astype(jnp.bfloat16), "dev", -1).astype(jnp.float32)
    grad_keyval_rot = grad_window[row_count:] + back_near
    key_part = rotate(
        grad_keyval_rot[:, : KVH * HD].reshape(row_count, KVH, HD), cos_table, -sin_table
    ).reshape(row_count, KVH * HD)
    grad_keyval_act = jnp.concatenate([key_part, grad_keyval_rot[:, KVH * HD :]], axis=1).astype(
        jnp.bfloat16
    )
    grad_query_act = (
        rotate(grad_query_rot, cos_table, -sin_table)
        .reshape(row_count, H * HD)
        .astype(jnp.bfloat16)
    )
    grad_query = jnp.dot(normed_attn.T, grad_query_act, preferred_element_type=jnp.float32)
    grad_keyval = jnp.dot(normed_attn.T, grad_keyval_act, preferred_element_type=jnp.float32)
    grad_normed_attn = jnp.dot(
        grad_query_act, query_mat.T, preferred_element_type=jnp.float32
    ) + jnp.dot(grad_keyval_act, keyval_mat.T, preferred_element_type=jnp.float32)
    grad_input, grad_gain_attn = norm_backward(grad_normed_attn, inputs, inverse_attn, gain_attn)
    token_grads = grad_residual + grad_input
    ffn_parts = jnp.concatenate(
        [
            grad_gate_up.reshape(count, -1).astype(jnp.bfloat16),
            grad_down.reshape(count, -1).astype(jnp.bfloat16),
            grad_out.reshape(count, -1).astype(jnp.bfloat16),
        ],
        axis=1,
    )
    ffn_parts = jnp.pad(ffn_parts, ((0, 0), (0, -ffn_parts.shape[1] % 128)))
    ffn_share = scatter_sum(ffn_parts.reshape(count, -1, 128), 4).reshape(-1)
    share_gate_up = ffn_share[: ffn_sizes[0]]
    share_down = ffn_share[ffn_sizes[0] : ffn_sizes[0] + ffn_sizes[1]]
    share_out = ffn_share[ffn_sizes[0] + ffn_sizes[1] : sum(ffn_sizes) + attn_sizes[2]]
    attn_parts = jnp.concatenate(
        [
            grad_query.reshape(count, -1).astype(jnp.bfloat16),
            grad_keyval.reshape(count, -1).astype(jnp.bfloat16),
        ],
        axis=1,
    )
    attn_rows = attn_parts.shape[1]
    attn_parts = jnp.pad(attn_parts, ((0, 0), (0, -attn_rows % 128)))
    attn_share = scatter_sum(attn_parts.reshape(count, -1, 128), 2).reshape(-1)
    share_query = attn_share[: attn_sizes[0]]
    share_keyval = attn_share[attn_sizes[0] : attn_sizes[0] + attn_sizes[1]]
    gain_sums = sum_all(jnp.stack([grad_gain_attn, grad_gain_ffn]))
    gain_attn_sum = gain_sums[0]
    gain_ffn_sum = gain_sums[1]
    return (
        mixed,
        token_grads,
        gain_attn_sum,
        share_query,
        share_keyval,
        share_out,
        gain_ffn_sum,
        share_gate_up,
        share_down,
    )


PAD = 24
CHUNK = 128
bf16 = jnp.bfloat16
f32 = jnp.float32


def dot_nn(a, b):
    return lax.dot_general(a, b, (((1,), (0,)), ((), ())), preferred_element_type=f32)


def dot_nt(a, b):
    return lax.dot_general(a, b, (((1,), (1,)), ((), ())), preferred_element_type=f32)


def split_two(value):
    high = value.astype(bf16)
    return high, (value - high.astype(f32)).astype(bf16)


def spread_wide(source_row):
    rows = lax.broadcasted_iota(jnp.int32, (D, source_row.shape[1]), 0)
    return jnp.where(rows == source_row, 1.0, 0.0).astype(bf16)


def spread_tall(source_col):
    lanes = lax.broadcasted_iota(jnp.int32, (source_col.shape[0], D), 1)
    return jnp.where(lanes == source_col, 1.0, 0.0).astype(bf16)


def turn(a, b, cos_table, sin_table):
    return a * cos_table - b * sin_table, b * cos_table + a * sin_table


def project_kernel(tok, gain, cos, sin, src_a, src_b, wa0, wa1, wb0, wb1, q_out, kv_out):
    x = tok[...].astype(f32)
    inverse = lax.rsqrt(jnp.mean(x * x, axis=0, keepdims=True) + norm_epsilon)
    normed = (x * inverse * gain[...]).astype(bf16).T
    cos_table, sin_table = cos[...], sin[...]
    wa = jnp.concatenate([wa0[...], wa1[...]], axis=0)
    wb = jnp.concatenate([wb0[...], wb1[...]], axis=0)
    wide_a = dot_nn(normed, spread_wide(src_a[...])).astype(bf16)
    wide_b = dot_nn(normed, spread_wide(src_b[...])).astype(bf16)
    qk = dot_nn(wide_a, wa).T
    v = dot_nn(wide_b, wb).T[H * HD :]
    half = HD // 2
    for h in range(H + KVH):
        a = qk[h * HD : h * HD + half]
        b = qk[h * HD + half : (h + 1) * HD]
        ra, rb = turn(a, b, cos_table, sin_table)
        out, row = (q_out, h * HD) if h < H else (kv_out, (h - H) * HD)
        out[row : row + half, :] = ra.astype(bf16)
        out[row + half : row + HD, :] = rb.astype(bf16)
    kv_out[KVH * HD :, :] = v.astype(bf16)


def attend_kernel(q, near, own, pos, prob_out, att_out):
    tokens = q.shape[1]
    group = H // KVH
    scale = 1.0 / math.sqrt(HD)
    span = tokens + CHUNK
    rows = lax.broadcasted_iota(jnp.int32, (span, CHUNK), 0)
    lanes = lax.broadcasted_iota(jnp.int32, (span, CHUNK), 1) + tokens
    for g in range(KVH):
        kw = jnp.concatenate(
            [near[g * HD : (g + 1) * HD, :], own[g * HD : (g + 1) * HD, :]], axis=1
        ).T
        low = (KVH + g) * HD
        vw = jnp.concatenate([near[low : low + HD, :], own[low : low + HD, :]], axis=1)
        for c in range(tokens // CHUNK):
            base = c * CHUNK
            position = pos[:, base : base + CHUNK]
            allowed = (rows <= lanes) & (rows >= lanes - position)
            for i in range(group):
                h = g * group + i
                qh = q[h * HD : (h + 1) * HD, base : base + CHUNK]
                scores = dot_nn(kw[base : base + span], qh) * scale
                scores = jnp.where(allowed, scores, -1e30)
                highest = jnp.max(scores, axis=0, keepdims=True)
                e = jnp.exp(scores - highest)
                total = jnp.sum(e, axis=0, keepdims=True)
                p = (e * (1.0 / total)).astype(bf16)
                prob_out[g, c, :, i * CHUNK : (i + 1) * CHUNK] = p
                att_out[h * HD : (h + 1) * HD, base : base + CHUNK] = dot_nn(
                    vw[:, base : base + span], p
                ).astype(bf16)


def attend_back_kernel(
    q, near, own, prob, att, grad_att, cos, sin, dq_out, dnear_out, down_out, dk, dv
):
    tokens = q.shape[1]
    group = H // KVH
    scale = 1.0 / math.sqrt(HD)
    span = tokens + CHUNK
    half = HD // 2
    for g in range(KVH):
        low = (KVH + g) * HD
        kw = jnp.concatenate(
            [near[g * HD : (g + 1) * HD, :], own[g * HD : (g + 1) * HD, :]], axis=1
        )
        vw = jnp.concatenate([near[low : low + HD, :], own[low : low + HD, :]], axis=1).T
        dk[...] = jnp.zeros_like(dk)
        dv[...] = jnp.zeros_like(dv)
        for c in range(tokens // CHUNK):
            base = c * CHUNK
            cut = slice(base, base + CHUNK)
            heads = [g * group + i for i in range(group)]
            q_all = jnp.concatenate([q[h * HD : (h + 1) * HD, cut] for h in heads], axis=1)
            g_all = jnp.concatenate([grad_att[h * HD : (h + 1) * HD, cut] for h in heads], axis=1)
            a_all = jnp.concatenate([att[h * HD : (h + 1) * HD, cut] for h in heads], axis=1)
            delta = jnp.sum(g_all.astype(f32) * a_all.astype(f32), axis=0, keepdims=True)
            p = prob[g, c]
            grad_prob = dot_nn(vw[base : base + span], g_all)
            ds = (p.astype(f32) * (grad_prob - delta) * scale).astype(bf16)
            dq = dot_nn(kw[:, base : base + span], ds)
            dk[:, base : base + span] += dot_nt(q_all, ds)
            dv[:, base : base + span] += dot_nt(g_all, p)
            for i, h in enumerate(heads):
                part = dq[:, i * CHUNK : (i + 1) * CHUNK]
                ra, rb = turn(part[:half], part[half:], cos[:, cut], -sin[:, cut])
                dq_out[h * HD : h * HD + half, cut] = ra.astype(bf16)
                dq_out[h * HD + half : (h + 1) * HD, cut] = rb.astype(bf16)
        dnear_out[g * HD : (g + 1) * HD, :] = dk[:, :tokens].astype(bf16)
        dnear_out[low : low + HD, :] = dv[:, :tokens].astype(bf16)
        down_out[g * HD : (g + 1) * HD, :] = dk[:, tokens:]
        down_out[low : low + HD, :] = dv[:, tokens:]


def feed_kernel(
    slots,
    att,
    tok,
    cot,
    gain,
    src_b,
    src_g,
    src_u,
    src_d,
    wb0,
    wb1,
    wg0,
    wg1,
    wu0,
    wu1,
    wd0,
    wd1,
    mixed_out,
    gres_out,
    gatt_out,
    dgain_out,
    dg_out,
    du_out,
    dd_out,
    wd,
    act,
    dgate,
    dup,
    wide_g,
    wide_u,
):
    count = slots.shape[0]
    rows_d = FF // count
    for p in range(count):
        half, at = (wd0, p) if p < count // 2 else (wd1, p - count // 2)
        target = pl.multiple_of(slots[p] * rows_d, rows_d)
        wd[pl.ds(target, rows_d), :] = half[at * rows_d : (at + 1) * rows_d, :]
    wb = jnp.concatenate([wb0[...], wb1[...]], axis=0)
    spread_b = spread_wide(src_b[...])
    spread_g = spread_wide(src_g[...])
    spread_u = spread_wide(src_u[...])
    cot_tok = cot[...].T
    att_wide = dot_nn(att[...].T, spread_b).astype(bf16)
    residual = tok[...].astype(f32).T + dot_nn(att_wide, wb)[:, :D]
    inverse = lax.rsqrt(jnp.mean(residual * residual, axis=-1, keepdims=True) + norm_epsilon)
    normed = (residual * inverse * gain[...]).astype(bf16)
    wide_g[...] = dot_nn(normed, spread_g).astype(bf16)
    wide_u[...] = dot_nn(normed, spread_u).astype(bf16)
    block = 256

    def ff_step(j, carry):
        cut = pl.ds(pl.multiple_of(j * block, block), block)
        gate = dot_nn(wide_g[...], jnp.concatenate([wg0[:, cut], wg1[:, cut]], axis=0))
        up = dot_nn(wide_u[...], jnp.concatenate([wu0[:, cut], wu1[:, cut]], axis=0))
        grad_act = dot_nt(cot_tok, wd[cut, :])
        sig = jax.nn.sigmoid(gate)
        silu = gate * sig
        act[:, cut] = (silu * up).astype(bf16)
        dgate[:, cut] = (grad_act * up * sig * (1.0 + gate * (1.0 - sig))).astype(bf16)
        dup[:, cut] = (grad_act * silu).astype(bf16)
        return carry

    lax.fori_loop(0, FF // block, ff_step, 0)
    mixed = residual + dot_nn(act[...], wd[...])
    mixed_out[...] = mixed.T.astype(bf16)
    dn_g = dot_nt(dgate[...], jnp.concatenate([wg0[...], wg1[...]], axis=0))
    dn_u = dot_nt(dup[...], jnp.concatenate([wu0[...], wu1[...]], axis=0))
    grad_normed = sum(dot_nt(part, spread_g) for part in split_two(dn_g)) + sum(
        dot_nt(part, spread_u) for part in split_two(dn_u)
    )
    unit = residual * inverse
    scaled = grad_normed * gain[...]
    dgain_out[...] = jnp.sum(grad_normed * unit, axis=0, keepdims=True)
    grad_res = cot_tok.astype(f32) + inverse * (
        scaled - unit * jnp.mean(scaled * unit, axis=-1, keepdims=True)
    )
    gres_out[...] = grad_res.T
    grad_res_b = grad_res.astype(bf16)
    gatt_wide = dot_nt(wb[:, :D], grad_res_b).astype(bf16)
    gatt_out[...] = dot_nn(spread_b, gatt_wide).astype(bf16)
    dg_out[...] = dot_nn(wide_g[...].T, dgate[...]).astype(bf16)
    du_out[...] = dot_nn(wide_u[...].T, dup[...]).astype(bf16)
    d_out = dot_nn(dot_nn(spread_tall(src_d[...]), att[...]).astype(bf16), grad_res_b).astype(bf16)
    wd[...] = dot_nn(act[...].T, cot_tok).astype(bf16)
    rows_all = rows_d + PAD
    for p in range(count):
        source = pl.multiple_of(slots[p] * rows_d, rows_d)
        dd_out[p * rows_all : p * rows_all + rows_d, :] = wd[pl.ds(source, rows_d), :]
        dd_out[p * rows_all + rows_d : (p + 1) * rows_all, :] = d_out[p * PAD : (p + 1) * PAD]


def finish_kernel(
    dq,
    own,
    back,
    tok,
    gain,
    cos,
    sin,
    gres,
    src_a,
    src_b,
    tall_a,
    tall_b,
    wa0,
    wa1,
    wb0,
    wb1,
    dtok_out,
    dgain_out,
    da_out,
    dv_out,
):
    x = tok[...].astype(f32)
    inverse = lax.rsqrt(jnp.mean(x * x, axis=0, keepdims=True) + norm_epsilon)
    unit = x * inverse
    normed = (unit * gain[...]).astype(bf16)
    total = own[...] + back[...].astype(f32)
    half = HD // 2
    parts = [dq[...]]
    for g in range(KVH):
        ra, rb = turn(
            total[g * HD : g * HD + half],
            total[g * HD + half : (g + 1) * HD],
            cos[...],
            -sin[...],
        )
        parts += [ra.astype(bf16), rb.astype(bf16)]
    dqk = jnp.concatenate(parts, axis=0)
    dv = total[KVH * HD :].astype(bf16)
    wa = jnp.concatenate([wa0[...], wa1[...]], axis=0)
    wb = jnp.concatenate([wb0[...], wb1[...]], axis=0)
    dvx = jnp.concatenate([jnp.zeros((H * HD, dv.shape[1]), bf16), dv], axis=0)
    dn_a = dot_nn(wa, dqk)
    dn_b = dot_nn(wb, dvx)
    spread_a = spread_wide(src_a[...])
    spread_b = spread_wide(src_b[...])
    grad_normed = sum(dot_nn(spread_a, part) for part in split_two(dn_a)) + sum(
        dot_nn(spread_b, part) for part in split_two(dn_b)
    )
    scaled = grad_normed * gain[...]
    dgain_out[...] = jnp.sum(grad_normed * unit, axis=1, keepdims=True)
    dtok_out[...] = gres[...] + inverse * (
        scaled - unit * jnp.mean(scaled * unit, axis=0, keepdims=True)
    )
    wide_a = dot_nn(spread_tall(tall_a[...]), normed).astype(bf16)
    wide_b = dot_nn(spread_tall(tall_b[...]), normed).astype(bf16)
    da_out[...] = dot_nt(wide_a, dqk).astype(bf16)
    dv_out[...] = dot_nt(wide_b, dv).astype(bf16)


def call_whole(kernel, outs, operands, scratch=(), scalars=()):
    vmem = pl.BlockSpec(memory_space=pltpu.VMEM)
    smem = pl.BlockSpec(memory_space=pltpu.SMEM)
    return pl.pallas_call(
        kernel,
        out_shape=[jax.ShapeDtypeStruct(s, d) for s, d in outs],
        in_specs=[smem] * len(scalars) + [vmem] * len(operands),
        out_specs=[vmem] * len(outs),
        scratch_shapes=list(scratch),
        compiler_params=pltpu.CompilerParams(vmem_limit_bytes=60 * 1024 * 1024),
    )(*scalars, *operands)


def doubled(streams, orders):
    held = list(streams)
    got = None
    for t in range(len(orders[0])):
        got = [swapped(h, order[t]) for h, order in zip(held, orders)]
        if t < len(orders[0]) - 1:
            held = [jnp.concatenate([h, g], axis=0) for h, g in zip(held, got)]
    return list(zip(held, got))


def halved(streams, orders):
    held = list(streams)
    for t in range(len(orders[0])):
        half = held[0].shape[0] // 2
        halves = [h.shape[0] // 2 for h in held]
        got = [
            swapped(h[k:].astype(bf16), order[-1 - t])
            for h, k, order in zip(held, halves, orders)
        ]
        held = [h[:k].astype(f32) + g.astype(f32) for h, k, g in zip(held, halves, got)]
    return held


def sources(order, count, per_slot):
    me = lax.axis_index("dev")
    owner = me ^ jnp.asarray(slot_masks(order), jnp.int32)
    inner = jnp.arange(PAD, dtype=jnp.int32)[None, :]
    value = jnp.where(inner < per_slot, owner[:, None] * per_slot + inner, -1)
    return value.reshape(-1)


def padded_rows(value):
    return jnp.pad(value, ((0, PAD - value.shape[0]), (0, 0)))


def shards(
    tokens, positions, gain_attn, w_query, w_kv, w_out, gain_ffn, w_gate_up, w_down, cotangent
):
    count = lax.axis_size("dev")
    me = lax.axis_index("dev")
    row_count = tokens.shape[0]
    per = D // count
    per_d = FF // count
    first, rest = link_masks(count)
    order_of = [rest[k:] + rest[:k] + [first] for k in range(len(rest))]
    ord_a, ord_b = order_of[0], order_of[2]
    ord_g, ord_u, ord_d = order_of[1], order_of[2], order_of[3]
    src_a, src_b = sources(ord_a, count, per), sources(ord_b, count, per)
    src_g, src_u = sources(ord_g, count, per), sources(ord_u, count, per)
    src_d = sources(ord_d, count, per)
    slots = me ^ jnp.asarray(slot_masks(ord_d), jnp.int32)
    w_qs, w_kvs = w_query.reshape(per, H * HD), w_kv.reshape(per, 2 * KVH * HD)
    w_gs = w_gate_up.reshape(per, 2 * FF)
    kv_cut = KVH * HD
    stream_a = padded_rows(jnp.concatenate([w_qs, w_kvs[:, :kv_cut]], axis=1))
    stream_b = padded_rows(jnp.concatenate([w_out.reshape(per, D), w_kvs[:, kv_cut:]], axis=1))
    (wa0, wa1), (wb0, wb1) = doubled([stream_a, stream_b], [ord_a, ord_b])
    stream_g, stream_u = padded_rows(w_gs[:, :FF]), padded_rows(w_gs[:, FF:])
    stream_d = w_down.reshape(per_d, D)
    (wg0, wg1), (wu0, wu1), (wd0, wd1) = doubled(
        [stream_g, stream_u, stream_d], [ord_g, ord_u, ord_d]
    )
    half_dim = HD // 2
    frequency = jnp.exp(jnp.arange(half_dim, dtype=f32) * (-2.0 * math.log(theta_base) / HD))
    angles = frequency[:, None] * positions.astype(f32)[None, :]
    cos, sin = jnp.cos(angles), jnp.sin(angles)
    tok_t, cot_t = tokens.T, cotangent.T
    gain_col = gain_attn.reshape(D, 1)
    q_t, kv_t = call_whole(
        project_kernel,
        [((H * HD, row_count), bf16), ((2 * kv_cut, row_count), bf16)],
        [tok_t, gain_col, cos, sin, src_a[None], src_b[None], wa0, wa1, wb0, wb1],
    )
    near = passed_along(kv_t, "dev", 1)
    chunks = row_count // CHUNK
    prob, att_t = call_whole(
        attend_kernel,
        [
            ((KVH, chunks, row_count + CHUNK, H // KVH * CHUNK), bf16),
            ((H * HD, row_count), bf16),
        ],
        [q_t, near, kv_t, positions[None]],
    )
    wide = count * PAD
    mixed_t, gres_t, gatt_t, dgain_ffn, dg, du, dd = call_whole(
        feed_kernel,
        [
            ((D, row_count), bf16),
            ((D, row_count), f32),
            ((H * HD, row_count), bf16),
            ((1, D), f32),
            ((wide, FF), bf16),
            ((wide, FF), bf16),
            ((count * (per_d + PAD), D), bf16),
        ],
        [
            att_t,
            tok_t,
            cot_t,
            gain_ffn[None],
            src_b[None],
            src_g[None],
            src_u[None],
            src_d[:, None],
            wb0,
            wb1,
            wg0,
            wg1,
            wu0,
            wu1,
            wd0,
            wd1,
        ],
        scratch=[
            pltpu.VMEM((FF, D), bf16),
            pltpu.VMEM((row_count, FF), bf16),
            pltpu.VMEM((row_count, FF), bf16),
            pltpu.VMEM((row_count, FF), bf16),
            pltpu.VMEM((row_count, wide), bf16),
            pltpu.VMEM((row_count, wide), bf16),
        ],
        scalars=[slots],
    )
    share_g, share_u, share_d = halved([dg, du, dd], [ord_g, ord_u, ord_d])
    dq_t, dnear, down = call_whole(
        attend_back_kernel,
        [
            ((H * HD, row_count), bf16),
            ((2 * kv_cut, row_count), bf16),
            ((2 * kv_cut, row_count), f32),
        ],
        [q_t, near, kv_t, prob, att_t, gatt_t, cos, sin],
        scratch=[pltpu.VMEM((HD, 2 * row_count), f32)] * 2,
    )
    back = passed_along(dnear, "dev", -1)
    dtok_t, dgain_attn, da, dv = call_whole(
        finish_kernel,
        [
            ((D, row_count), f32),
            ((D, 1), f32),
            ((wide, H * HD + kv_cut), bf16),
            ((wide, kv_cut), bf16),
        ],
        [
            dq_t,
            down,
            back,
            tok_t,
            gain_col,
            cos,
            sin,
            gres_t,
            src_a[None],
            src_b[None],
            src_a[:, None],
            src_b[:, None],
            wa0,
            wa1,
            wb0,
            wb1,
        ],
    )
    share_a, share_v = halved([da, dv], [ord_a, ord_b])
    gain_sums = sum_all(jnp.concatenate([dgain_attn.reshape(1, D), dgain_ffn], axis=0))
    share_kv = jnp.concatenate([share_a[:per, H * HD :], share_v[:per]], axis=1)
    share_gu = jnp.concatenate([share_g[:per], share_u[:per]], axis=1)
    return (
        mixed_t.T,
        dtok_t.T,
        gain_sums[0],
        share_a[:per, : H * HD].reshape(-1),
        share_kv.reshape(-1),
        share_d[per_d : per_d + per].reshape(-1),
        gain_sums[1],
        share_gu.reshape(-1),
        share_d[:per_d].reshape(-1),
    )


def fits_whole_rows(count):
    per = D // count
    return D % count == 0 and FF % count == 0 and (FF // count) % 16 == 0 and 16 <= per <= PAD


def solution(mesh):
    in_specs = (
        P("dev", None),
        P("dev"),
        P(),
        P("dev"),
        P("dev"),
        P("dev"),
        P(),
        P("dev"),
        P("dev"),
        P("dev", None),
    )
    out_specs = (
        P("dev", None),
        P("dev", None),
        P(),
        P("dev"),
        P("dev"),
        P("dev"),
        P(),
        P("dev"),
        P("dev"),
    )
    return jax.shard_map(
        shards if fits_whole_rows(mesh.shape["dev"]) else shards_general, mesh=mesh, in_specs=in_specs, out_specs=out_specs, check_vma=False)
```

profile of v0, /device:TPU:0, one launch (start us, length us, event | category | flops | bytes accessed | tf_op | source)
XLA Modules:
  0.0 264.4 jit_solution(4236014248078375123)
XLA Ops:
  2.5 3.1 %collective-permute-start.5 = (bf16[24,768]{1,0:T(8,128)(2,1)S(1)}, bf16[24,768]{1,0:T(8,128)(2,1)S(1)}, u32[]{:S(2)}, u32[]{:S(2)}) collective-permute-start(bf16[24,768]{1,0:T(8,128)(2,1)S(1)} %get-tuple-element.48), channel_id=1, source_target_pairs={{0,8},{1,9},{2,10},{3,11},{4,12},{5,13},{6,14},{7,15},{8,0},{9,1},... | collective-permute-start | bytes 110600 | tf_op jit(solution)/shard_map/ppermute | solution.py:36
  6.4 1.5 collective-permute-start
  10.6 1.5 collective-permute-start.11
  12.3 3.7 %collective-permute-start.21 = (bf16[48,576]{1,0:T(8,128)(2,1)S(1)}, bf16[48,576]{1,0:T(8,128)(2,1)S(1)}, u32[]{:S(2)}, u32[]{:S(2)}) collective-permute-start(bf16[48,576]{1,0:T(8,128)(2,1)S(1)} %reshape.332), channel_id=1, source_target_pairs={{0,24},{1,25},{2,26},{3,27},{4,28},{5,29},{6,30},{7,31},{8,16},{9,... | collective-permute-start | bytes 165896 | tf_op jit(solution)/shard_map/ppermute | solution.py:36
  19.1 3.7 %collective-permute-start.17 = (bf16[48,1536]{1,0:T(8,128)(2,1)S(1)}, bf16[48,1536]{1,0:T(8,128)(2,1)S(1)}, u32[]{:S(2)}, u32[]{:S(2)}) collective-permute-start(bf16[48,1536]{1,0:T(8,128)(2,1)S(1)} %pad_maximum_fusion.12), channel_id=1, source_target_pairs={{0,24},{1,25},{2,26},{3,27},{4,28},{5,29},{6,30},{7,31},{8,16},{9,... | collective-permute-start | bytes 442376 | tf_op jit(solution)/shard_map/ppermute | solution.py:36
  24.2 1.6 collective-permute-start.7
  25.7 2.1 collective-permute-start.2
  30.0 2.5 collective-permute-start.13
  37.0 1.2 collective-permute-start.19
  38.2 3.6 %collective-permute-done.13 = bf16[96,1536]{1,0:T(8,128)(2,1)S(1)} collective-permute-done((bf16[96,1536]{1,0:T(8,128)(2,1)S(1)}, bf16[96,1536]{1,0:T(8,128)(2,1)S(1)}, u32[]{:S(2)}, u32[]{:S(2)}) %collective-permute-start.13) | collective-permute-done | bytes 294944 | tf_op jit(solution)/shard_map/ppermute | solution.py:36
  41.8 1.4 collective-permute-start.14
  44.8 7.8 %collective-permute-done.19 = bf16[192,1536]{1,0:T(8,128)(2,1)S(1)} collective-permute-done((bf16[192,1536]{1,0:T(8,128)(2,1)S(1)}, bf16[192,1536]{1,0:T(8,128)(2,1)S(1)}, u32[]{:S(2)}, u32[]{:S(2)}) %collective-permute-start.19) | collective-permute-done | bytes 589856 | tf_op jit(solution)/shard_map/ppermute | solution.py:36
  55.1 1.3 copy.31
  61.2 4.8 %shard_map.223 = (bf16[576,384]{1,0:T(8,128)(2,1)}, bf16[384,384]{1,0:T(8,128)(2,1)}) custom-call(bf16[576,384]{1,0:T(8,128)(2,1)} %bitcast.4, f32[576,1]{1,0:T(8,128)} %reshape.339.gain, f32[32,384]{1,0:T(8,128)} %get-tuple-element.60.cos, f32[32,384]{1,0:T(8,128)} %get-tuple-element.59.sin, s32[1,768]{1,0:T(1,128)} %select_n.87.src_a, ...), custom_call_target="tpu_custom_call" | custom-call | tf_op jit(solution)/shard_map/pallas_call | solution.py:638
  65.9 2.5 collective-permute-start.10
  71.8 12.1 %shard_map.224 = (bf16[3,3,512,384]{3,2,1,0:T(8,128)(2,1)}, bf16[576,384]{1,0:T(8,128)(2,1)}) custom-call(bf16[576,384]{1,0:T(8,128)(2,1)} %get-tuple-element.27.q, bf16[384,384]{1,0:T(8,128)(2,1)} %copy-done.14, bf16[384,384]{1,0:T(8,128)(2,1)} %get-tuple-element.28.own, s32[1,384]{1,0:T(1,128)} %broadcast_in_dim.56.pos), custom_call_target="tpu_custom_call" | custom-call | tf_op jit(solution)/shard_map/pallas_call | solution.py:638
  84.0 2.2 copy.33.wd1
  86.2 24.6 %shard_map.225 = (bf16[576,384]{1,0:T(8,128)(2,1)}, f32[576,384]{1,0:T(8,128)}, bf16[576,384]{1,0:T(8,128)(2,1)}, f32[1,576]{1,0:T(1,128)}, bf16[768,1536]{1,0:T...) custom-call(s32[32]{0:T(128)} %get-tuple-element.66.slots, bf16[576,384]{1,0:T(8,128)(2,1)} %get-tuple-element.29.att, ...), custom_call_target="tpu_custom_call" | custom-call | tf_op jit(solution)/shard_map/pallas_call | solution.py:638
  110.8 8.6 %shard_map.226 = (bf16[576,384]{1,0:T(8,128)(2,1)}, bf16[384,384]{1,0:T(8,128)(2,1)}, f32[384,384]{1,0:T(8,128)}) custom-call(bf16[576,384]{1,0:T(8,128)(2,1)} %get-tuple-element.27.q, bf16[384,384]{1,0:T(8,128)(2,1)} %copy-done.14, bf16[384,384]{1,0:T(8,128)(2,1)} %get-tuple-element.28.own, bf16[3,3,512,384]{3,2,1,0:T(8,128)(2,1)} %get-tuple-element.31.prob, ...), custom_call_target="tpu_custom_call" | custom-call | tf_op jit(solution)/shard_map/pallas_call | solution.py:638
  119.3 1.3 collective-permute-start.26
  122.4 1.5 collective-permute-done.26.back
  124.7 9.3 %shard_map.227 = (f32[576,384]{1,0:T(8,128)}, f32[576,1]{1,0:T(8,128)}, bf16[768,768]{1,0:T(8,128)(2,1)}, bf16[768,192]{1,0:T(8,128)(2,1)}) custom-call(bf16[576,384]{1,0:T(8,128)(2,1)} %get-tuple-element.33.dq, f32[384,384]{1,0:T(8,128)} %get-tuple-element.34.own, bf16[384,384]{1,0:T(8,128)(2,1)} %copy-done.16, bf16[576,384]{1,0:T(8,128)(2,1)} %bitcast.6, ...), custom_call_target="tpu_custom_call" | custom-call | tf_op jit(solution)/shard_map/pallas_call | solution.py:638
  134.0 1.6 slice.227
  135.6 5.7 %collective-permute-start.37 = (bf16[384,192]{1,0:T(8,128)(2,1)}, bf16[384,192]{1,0:T(8,128)(2,1)}, u32[]{:S(2)}, u32[]{:S(2)}) collective-permute-start(bf16[384,192]{1,0:T(8,128)(2,1)} %slice.227), channel_id=1, source_target_pairs={{0,1},{1,0},{2,3},{3,2},{4,5},{5,4},{6,7},{7,6},{8,9},{9,8},{10,11... | collective-permute-start | bytes 442376 | tf_op jit(solution)/shard_map/ppermute | solution.py:36
  141.3 1.1 slice.250
  143.1 1.3 reduce
  145.4 1.5 collective-permute-start.38
  147.0 3.7 %collective-permute-done.38 = bf16[192,192]{1,0:T(8,128)(2,1)S(1)} collective-permute-done((bf16[192,192]{1,0:T(8,128)(2,1)S(1)}, bf16[192,192]{1,0:T(8,128)(2,1)S(1)}, u32[]{:S(2)}, u32[]{:S(2)}) %collective-permute-start.38) | collective-permute-done | bytes 73760 | tf_op jit(solution)/shard_map/ppermute | solution.py:36
  150.7 9.3 %collective-permute-start.39 = (bf16[96,192]{1,0:T(8,128)(2,1)S(1)}, bf16[96,192]{1,0:T(8,128)(2,1)S(1)}, u32[]{:S(2)}, u32[]{:S(2)}) collective-permute-start(bf16[96,192]{1,0:T(8,128)(2,1)S(1)} %slice.394), channel_id=1, source_target_pairs={{0,2},{1,3},{2,0},{3,1},{4,6},{5,7},{6,4},{7,5},{8,10},{9,11},{10,... | collective-permute-start | bytes 110600 | tf_op jit(solution)/shard_map/ppermute | solution.py:36
  160.1 2.0 collective-permute-done.39
  163.7 1.8 collective-permute-start.29
  165.5 1.9 collective-permute-done.29
  167.4 1.4 collective-permute-start.30
  168.8 2.2 collective-permute-done.30
  171.0 2.3 collective-permute-start.31
  173.3 1.2 slice.261
  174.6 1.4 copy.37
  176.7 1.4 convert_add_fusion.3
  178.1 2.2 collective-permute-start.33
  181.6 7.8 %collective-permute-done.33 = bf16[192,768]{1,0:T(8,128)(2,1)S(1)} collective-permute-done((bf16[192,768]{1,0:T(8,128)(2,1)S(1)}, bf16[192,768]{1,0:T(8,128)(2,1)S(1)}, u32[]{:S(2)}, u32[]{:S(2)}) %collective-permute-start.33) | collective-permute-done | bytes 294944 | tf_op jit(solution)/shard_map/ppermute | solution.py:36
  189.4 6.2 %collective-permute-start.34 = (bf16[96,768]{1,0:T(8,128)(2,1)S(1)}, bf16[96,768]{1,0:T(8,128)(2,1)S(1)}, u32[]{:S(2)}, u32[]{:S(2)}) collective-permute-start(bf16[96,768]{1,0:T(8,128)(2,1)S(1)} %slice.388), channel_id=1, source_target_pairs={{0,8},{1,9},{2,10},{3,11},{4,12},{5,13},{6,14},{7,15},{8,0},{9,1},... | collective-permute-start | bytes 442376 | tf_op jit(solution)/shard_map/ppermute | solution.py:36
  195.7 1.7 convert_add_fusion.2
  197.5 1.7 collective-permute-start.48
  199.9 1.7 collective-permute-start.35
  201.6 1.6 convert_add_fusion.1
  205.2 1.6 copy.38
  207.7 1.5 collective-permute-start.36
  209.3 2.1 convert_add_fusion
  212.3 1.8 collective-permute-start.43
  215.5 1.4 reshape.335
  216.9 1.5 reshape.334
  218.4 1.7 slice_add_fusion.2
  220.2 2.7 %collective-permute-start.49 = (bf16[96,1536]{1,0:T(8,128)(2,1)S(1)}, bf16[96,1536]{1,0:T(8,128)(2,1)S(1)}, u32[]{:S(2)}, u32[]{:S(2)}) collective-permute-start(bf16[96,1536]{1,0:T(8,128)(2,1)S(1)} %slice.383), channel_id=1, source_target_pairs={{0,24},{1,25},{2,26},{3,27},{4,28},{5,29},{6,30},{7,31},{8,16},{9,... | collective-permute-start | bytes 884744 | tf_op jit(solution)/shard_map/ppermute | solution.py:36
  222.9 1.2 slice_add_fusion.1
  224.4 6.4 %collective-permute-done.43 = bf16[576,576]{1,0:T(8,128)(2,1)} collective-permute-done((bf16[576,576]{1,0:T(8,128)(2,1)}, bf16[576,576]{1,0:T(8,128)(2,1)}, u32[]{:S(2)}, u32[]{:S(2)}) %collective-permute-start.43) | collective-permute-done | bytes 663584 | tf_op jit(solution)/shard_map/ppermute | solution.py:36
  230.9 1.2 slice_add_fusion
  232.2 1.8 collective-permute-start.44
  234.0 4.6 %collective-permute-done.49 = bf16[96,1536]{1,0:T(8,128)(2,1)S(1)} collective-permute-done((bf16[96,1536]{1,0:T(8,128)(2,1)S(1)}, bf16[96,1536]{1,0:T(8,128)(2,1)S(1)}, u32[]{:S(2)}, u32[]{:S(2)}) %collective-permute-start.49) | collective-permute-done | bytes 294944 | tf_op jit(solution)/shard_map/ppermute | solution.py:36
  239.4 4.5 %collective-permute-done.50 = bf16[48,1536]{1,0:T(8,128)(2,1)S(1)} collective-permute-done((bf16[48,1536]{1,0:T(8,128)(2,1)S(1)}, bf16[48,1536]{1,0:T(8,128)(2,1)S(1)}, u32[]{:S(2)}, u32[]{:S(2)}) %collective-permute-start.50) | collective-permute-done | bytes 147488 | tf_op jit(solution)/shard_map/ppermute | solution.py:36
  243.9 4.1 %collective-permute-start.51 = (bf16[24,1536]{1,0:T(8,128)(2,1)S(1)}, bf16[24,1536]{1,0:T(8,128)(2,1)S(1)}, u32[]{:S(2)}, u32[]{:S(2)}) collective-permute-start(bf16[24,1536]{1,0:T(8,128)(2,1)S(1)} %slice.392), channel_id=1, source_target_pairs={{0,4},{1,5},{2,6},{3,7},{4,0},{5,1},{6,2},{7,3},{8,12},{9,13},{10,... | collective-permute-start | bytes 221192 | tf_op jit(solution)/shard_map/ppermute | solution.py:36
  248.2 2.2 collective-permute-done.51
  250.6 1.9 collective-permute-done.56
  252.6 3.5 %collective-permute-done.45 = bf16[144,576]{1,0:T(8,128)(2,1)S(1)} collective-permute-done((bf16[144,576]{1,0:T(8,128)(2,1)S(1)}, bf16[144,576]{1,0:T(8,128)(2,1)S(1)}, u32[]{:S(2)}, u32[]{:S(2)}) %collective-permute-start.45) | collective-permute-done | bytes 165920 | tf_op jit(solution)/shard_map/ppermute | solution.py:36
  257.0 5.6 %collective-permute-done.46 = bf16[72,576]{1,0:T(8,128)(2,1)S(1)} collective-permute-done((bf16[72,576]{1,0:T(8,128)(2,1)S(1)}, bf16[72,576]{1,0:T(8,128)(2,1)S(1)}, u32[]{:S(2)}, u32[]{:S(2)}) %collective-permute-start.46) | collective-permute-done | bytes 82976 | tf_op jit(solution)/shard_map/ppermute | solution.py:36
  (250 shorter events, 47.0 us)
Async XLA Ops:
  0.7 15.9 %copy-start.26 = (s32[32]{0:T(128)S(1)}, s32[32]{0:T(128)}, u32[]{:S(2)}) copy-start(s32[32]{0:T(128)} %constant.22.clone) | copy-start | bytes 388
  0.7 15.9 %copy-start.23 = (s32[32]{0:T(128)S(1)}, s32[32]{0:T(128)}, u32[]{:S(2)}) copy-start(s32[32]{0:T(128)} %constant.23.clone) | copy-start | bytes 388
  0.7 15.8 %copy-start.24 = (s32[32]{0:T(128)S(1)}, s32[32]{0:T(128)}, u32[]{:S(2)}) copy-start(s32[32]{0:T(128)} %constant.24.clone) | copy-start | bytes 388
  2.5 14.1 %collective-permute-start.5 = (bf16[24,768]{1,0:T(8,128)(2,1)S(1)}, bf16[24,768]{1,0:T(8,128)(2,1)S(1)}, u32[]{:S(2)}, u32[]{:S(2)}) collective-permute-start(bf16[24,768]{1,0:T(8,128)(2,1)S(1)} %get-tuple-element.48), channel_id=1, source_target_pairs={{0,8},{1,9},{2,10},{3,11},{4,12},{5,13},{6,14},{7,15},{8,0},{9,1},... | collective-permute-start | bytes 110600 | tf_op jit(solution)/shard_map/ppermute | solution.py:36
  6.4 10.5 %collective-permute-start = (bf16[24,768]{1,0:T(8,128)(2,1)S(1)}, bf16[24,768]{1,0:T(8,128)(2,1)S(1)}, u32[]{:S(2)}, u32[]{:S(2)}) collective-permute-start(bf16[24,768]{1,0:T(8,128)(2,1)S(1)} %get-tuple-element.50), channel_id=1, source_target_pairs={{0,2},{1,3},{2,0},{3,1},{4,6},{5,7},{6,4},{7,5},{8,10},{9,11},{10,... | collective-permute-start | bytes 110600 | tf_op jit(solution)/shard_map/ppermute | solution.py:36
  9.5 9.5 %collective-permute-start.16 = (bf16[24,1536]{1,0:T(8,128)(2,1)S(1)}, bf16[24,1536]{1,0:T(8,128)(2,1)S(1)}, u32[]{:S(2)}, u32[]{:S(2)}) collective-permute-start(bf16[24,1536]{1,0:T(8,128)(2,1)S(1)} %get-tuple-element.53), channel_id=1, source_target_pairs={{0,8},{1,9},{2,10},{3,11},{4,12},{5,13},{6,14},{7,15},{8,0},{9,1},... | collective-permute-start | bytes 221192 | tf_op jit(solution)/shard_map/ppermute | solution.py:36
  10.6 12.2 %collective-permute-start.11 = (bf16[24,1536]{1,0:T(8,128)(2,1)S(1)}, bf16[24,1536]{1,0:T(8,128)(2,1)S(1)}, u32[]{:S(2)}, u32[]{:S(2)}) collective-permute-start(bf16[24,1536]{1,0:T(8,128)(2,1)S(1)} %get-tuple-element.55), channel_id=1, source_target_pairs={{0,4},{1,5},{2,6},{3,7},{4,0},{5,1},{6,2},{7,3},{8,12},{9,13},{10,... | collective-permute-start | bytes 221192 | tf_op jit(solution)/shard_map/ppermute | solution.py:36
  12.3 6.2 %collective-permute-start.21 = (bf16[48,576]{1,0:T(8,128)(2,1)S(1)}, bf16[48,576]{1,0:T(8,128)(2,1)S(1)}, u32[]{:S(2)}, u32[]{:S(2)}) collective-permute-start(bf16[48,576]{1,0:T(8,128)(2,1)S(1)} %reshape.332), channel_id=1, source_target_pairs={{0,24},{1,25},{2,26},{3,27},{4,28},{5,29},{6,30},{7,31},{8,16},{9,... | collective-permute-start | bytes 165896 | tf_op jit(solution)/shard_map/ppermute | solution.py:36
  16.6 7.6 %collective-permute-start.6 = (bf16[48,768]{1,0:T(8,128)(2,1)S(1)}, bf16[48,768]{1,0:T(8,128)(2,1)S(1)}, u32[]{:S(2)}, u32[]{:S(2)}) collective-permute-start(bf16[48,768]{1,0:T(8,128)(2,1)S(1)} %pad_maximum_fusion.15), channel_id=1, source_target_pairs={{0,24},{1,25},{2,26},{3,27},{4,28},{5,29},{6,30},{7,31},{8,16},{9,... | collective-permute-start | bytes 221192 | tf_op jit(solution)/shard_map/ppermute | solution.py:36
  16.9 8.8 %collective-permute-start.1 = (bf16[48,768]{1,0:T(8,128)(2,1)S(1)}, bf16[48,768]{1,0:T(8,128)(2,1)S(1)}, u32[]{:S(2)}, u32[]{:S(2)}) collective-permute-start(bf16[48,768]{1,0:T(8,128)(2,1)S(1)} %pad_maximum_fusion.14), channel_id=1, source_target_pairs={{0,4},{1,5},{2,6},{3,7},{4,0},{5,1},{6,2},{7,3},{8,12},{9,13},{10,... | collective-permute-start | bytes 221192 | tf_op jit(solution)/shard_map/ppermute | solution.py:36
  18.5 9.4 %collective-permute-start.22 = (bf16[96,576]{1,0:T(8,128)(2,1)S(1)}, bf16[96,576]{1,0:T(8,128)(2,1)S(1)}, u32[]{:S(2)}, u32[]{:S(2)}) collective-permute-start(bf16[96,576]{1,0:T(8,128)(2,1)S(1)} %pad_maximum_fusion.13), channel_id=1, source_target_pairs={{0,2},{1,3},{2,0},{3,1},{4,6},{5,7},{6,4},{7,5},{8,10},{9,11},{10,... | collective-permute-start | bytes 331784 | tf_op jit(solution)/shard_map/ppermute | solution.py:36
  19.1 9.4 %collective-permute-start.17 = (bf16[48,1536]{1,0:T(8,128)(2,1)S(1)}, bf16[48,1536]{1,0:T(8,128)(2,1)S(1)}, u32[]{:S(2)}, u32[]{:S(2)}) collective-permute-start(bf16[48,1536]{1,0:T(8,128)(2,1)S(1)} %pad_maximum_fusion.12), channel_id=1, source_target_pairs={{0,24},{1,25},{2,26},{3,27},{4,28},{5,29},{6,30},{7,31},{8,16},{9,... | collective-permute-start | bytes 442376 | tf_op jit(solution)/shard_map/ppermute | solution.py:36
  22.8 7.2 %collective-permute-start.12 = (bf16[48,1536]{1,0:T(8,128)(2,1)S(1)}, bf16[48,1536]{1,0:T(8,128)(2,1)S(1)}, u32[]{:S(2)}, u32[]{:S(2)}) collective-permute-start(bf16[48,1536]{1,0:T(8,128)(2,1)S(1)} %pad_maximum_fusion.11), channel_id=1, source_target_pairs={{0,8},{1,9},{2,10},{3,11},{4,12},{5,13},{6,14},{7,15},{8,0},{9,1},... | collective-permute-start | bytes 442376 | tf_op jit(solution)/shard_map/ppermute | solution.py:36
  24.2 9.8 %collective-permute-start.7 = (bf16[96,768]{1,0:T(8,128)(2,1)S(1)}, bf16[96,768]{1,0:T(8,128)(2,1)S(1)}, u32[]{:S(2)}, u32[]{:S(2)}) collective-permute-start(bf16[96,768]{1,0:T(8,128)(2,1)S(1)} %pad_maximum_fusion.10), channel_id=1, source_target_pairs={{0,2},{1,3},{2,0},{3,1},{4,6},{5,7},{6,4},{7,5},{8,10},{9,11},{10,... | collective-permute-start | bytes 442376 | tf_op jit(solution)/shard_map/ppermute | solution.py:36
  25.7 9.2 %collective-permute-start.2 = (bf16[96,768]{1,0:T(8,128)(2,1)S(1)}, bf16[96,768]{1,0:T(8,128)(2,1)S(1)}, u32[]{:S(2)}, u32[]{:S(2)}) collective-permute-start(bf16[96,768]{1,0:T(8,128)(2,1)S(1)} %pad_maximum_fusion.9), channel_id=1, source_target_pairs={{0,8},{1,9},{2,10},{3,11},{4,12},{5,13},{6,14},{7,15},{8,0},{9,1},... | collective-permute-start | bytes 442376 | tf_op jit(solution)/shard_map/ppermute | solution.py:36
  27.9 8.9 %collective-permute-start.23 = (bf16[192,576]{1,0:T(8,128)(2,1)S(1)}, bf16[192,576]{1,0:T(8,128)(2,1)S(1)}, u32[]{:S(2)}, u32[]{:S(2)}) collective-permute-start(bf16[192,576]{1,0:T(8,128)(2,1)S(1)} %pad_maximum_fusion.8), channel_id=1, source_target_pairs={{0,4},{1,5},{2,6},{3,7},{4,0},{5,1},{6,2},{7,3},{8,12},{9,13},{10,... | collective-permute-start | bytes 663560 | tf_op jit(solution)/shard_map/ppermute | solution.py:36
  28.6 8.4 %collective-permute-start.18 = (bf16[96,1536]{1,0:T(8,128)(2,1)S(1)}, bf16[96,1536]{1,0:T(8,128)(2,1)S(1)}, u32[]{:S(2)}, u32[]{:S(2)}) collective-permute-start(bf16[96,1536]{1,0:T(8,128)(2,1)S(1)} %pad_maximum_fusion.6), channel_id=1, source_target_pairs={{0,2},{1,3},{2,0},{3,1},{4,6},{5,7},{6,4},{7,5},{8,10},{9,11},{10,... | collective-permute-start | bytes 884744 | tf_op jit(solution)/shard_map/ppermute | solution.py:36
  30.0 11.7 %collective-permute-start.13 = (bf16[96,1536]{1,0:T(8,128)(2,1)S(1)}, bf16[96,1536]{1,0:T(8,128)(2,1)S(1)}, u32[]{:S(2)}, u32[]{:S(2)}) collective-permute-start(bf16[96,1536]{1,0:T(8,128)(2,1)S(1)} %pad_maximum_fusion.5), channel_id=1, source_target_pairs={{0,24},{1,25},{2,26},{3,27},{4,28},{5,29},{6,30},{7,31},{8,16},{9,... | collective-permute-start | bytes 884744 | tf_op jit(solution)/shard_map/ppermute | solution.py:36
  34.0 10.8 %collective-permute-start.8 = (bf16[192,768]{1,0:T(8,128)(2,1)S(1)}, bf16[192,768]{1,0:T(8,128)(2,1)S(1)}, u32[]{:S(2)}, u32[]{:S(2)}) collective-permute-start(bf16[192,768]{1,0:T(8,128)(2,1)S(1)} %pad_maximum_fusion.4), channel_id=1, source_target_pairs={{0,4},{1,5},{2,6},{3,7},{4,0},{5,1},{6,2},{7,3},{8,12},{9,13},{10,... | collective-permute-start | bytes 884744 | tf_op jit(solution)/shard_map/ppermute | solution.py:36
  35.0 19.9 %collective-permute-start.3 = (bf16[192,768]{1,0:T(8,128)(2,1)S(1)}, bf16[192,768]{1,0:T(8,128)(2,1)S(1)}, u32[]{:S(2)}, u32[]{:S(2)}) collective-permute-start(bf16[192,768]{1,0:T(8,128)(2,1)S(1)} %pad_maximum_fusion.3), channel_id=1, source_target_pairs={{0,24},{1,25},{2,26},{3,27},{4,28},{5,29},{6,30},{7,31},{8,16},{9,... | collective-permute-start | bytes 884744 | tf_op jit(solution)/shard_map/ppermute | solution.py:36
  36.8 18.2 %collective-permute-start.24 = (bf16[384,576]{1,0:T(8,128)(2,1)S(1)}, bf16[384,576]{1,0:T(8,128)(2,1)S(1)}, u32[]{:S(2)}, u32[]{:S(2)}) collective-permute-start(bf16[384,576]{1,0:T(8,128)(2,1)S(1)} %pad_maximum_fusion.2), channel_id=1, source_target_pairs={{0,8},{1,9},{2,10},{3,11},{4,12},{5,13},{6,14},{7,15},{8,0},{9,1},... | collective-permute-start | bytes 1327112 | tf_op jit(solution)/shard_map/ppermute | solution.py:36
  37.0 15.6 %collective-permute-start.19 = (bf16[192,1536]{1,0:T(8,128)(2,1)S(1)}, bf16[192,1536]{1,0:T(8,128)(2,1)S(1)}, u32[]{:S(2)}, u32[]{:S(2)}) collective-permute-start(bf16[192,1536]{1,0:T(8,128)(2,1)S(1)} %pad_maximum_fusion.1), channel_id=1, source_target_pairs={{0,4},{1,5},{2,6},{3,7},{4,0},{5,1},{6,2},{7,3},{8,12},{9,13},{10,... | collective-permute-start | bytes 1769480 | tf_op jit(solution)/shard_map/ppermute | solution.py:36
  41.8 11.7 %collective-permute-start.14 = (bf16[192,1536]{1,0:T(8,128)(2,1)S(1)}, bf16[192,1536]{1,0:T(8,128)(2,1)S(1)}, u32[]{:S(2)}, u32[]{:S(2)}) collective-permute-start(bf16[192,1536]{1,0:T(8,128)(2,1)S(1)} %pad_maximum_fusion), channel_id=1, source_target_pairs={{0,2},{1,3},{2,0},{3,1},{4,6},{5,7},{6,4},{7,5},{8,10},{9,11},{10,... | collective-permute-start | bytes 1769480 | tf_op jit(solution)/shard_map/ppermute | solution.py:36
  44.8 15.3 %collective-permute-start.9 = (bf16[384,768]{1,0:T(8,128)(2,1)S(1)}, bf16[384,768]{1,0:T(8,128)(2,1)S(1)}, u32[]{:S(2)}, u32[]{:S(2)}) collective-permute-start(bf16[384,768]{1,0:T(8,128)(2,1)S(1)} %constant_dynamic-update-slice_fusion.5.wb0), channel_id=1, source_target_pairs={{0,1},{1,0},{2,3},{3,2},{4,5},{5,4},{6,7},{7,6},{8,9},{9,8},{10,11... | collective-permute-start | bytes 1769480 | tf_op jit(solution)/shard_map/ppermute | solution.py:36
  53.5 32.7 %collective-permute-start.20 = (bf16[384,1536]{1,0:T(8,128)(2,1)}, bf16[384,1536]{1,0:T(8,128)(2,1)}, u32[]{:S(2)}, u32[]{:S(2)}) collective-permute-start(bf16[384,1536]{1,0:T(8,128)(2,1)} %constant_dynamic-update-slice_fusion.15.wu0), channel_id=1, source_target_pairs={{0,1},{1,0},{2,3},{3,2},{4,5},{5,4},{6,7},{7,6},{8,9},{9,8},{10,11... | collective-permute-start | bytes 3538952 | tf_op jit(solution)/shard_map/ppermute | solution.py:36
  54.4 31.8 %collective-permute-start.15 = (bf16[384,1536]{1,0:T(8,128)(2,1)}, bf16[384,1536]{1,0:T(8,128)(2,1)}, u32[]{:S(2)}, u32[]{:S(2)}) collective-permute-start(bf16[384,1536]{1,0:T(8,128)(2,1)} %constant_dynamic-update-slice_fusion.10.wg0), channel_id=1, source_target_pairs={{0,1},{1,0},{2,3},{3,2},{4,5},{5,4},{6,7},{7,6},{8,9},{9,8},{10,11... | collective-permute-start | bytes 3538952 | tf_op jit(solution)/shard_map/ppermute | solution.py:36
  54.9 5.2 %collective-permute-start.4 = (bf16[384,768]{1,0:T(8,128)(2,1)S(1)}, bf16[384,768]{1,0:T(8,128)(2,1)S(1)}, u32[]{:S(2)}, u32[]{:S(2)}) collective-permute-start(bf16[384,768]{1,0:T(8,128)(2,1)S(1)} %constant_dynamic-update-slice_fusion.wa0), channel_id=1, source_target_pairs={{0,1},{1,0},{2,3},{3,2},{4,5},{5,4},{6,7},{7,6},{8,9},{9,8},{10,11... | collective-permute-start | bytes 1769480 | tf_op jit(solution)/shard_map/ppermute | solution.py:36
  56.4 27.6 %collective-permute-start.25 = (bf16[768,576]{0,1:T(8,128)(2,1)}, bf16[768,576]{0,1:T(8,128)(2,1)}, u32[]{:S(2)}, u32[]{:S(2)}) collective-permute-start(bf16[768,576]{0,1:T(8,128)(2,1)} %copy.31), channel_id=1, source_target_pairs={{0,1},{1,0},{2,3},{3,2},{4,5},{5,4},{6,7},{7,6},{8,9},{9,8},{10,11... | collective-permute-start | bytes 2654216 | tf_op jit(solution)/shard_map/ppermute | solution.py:36
  65.9 5.2 %collective-permute-start.10 = (bf16[384,384]{1,0:T(8,128)(2,1)}, bf16[384,384]{1,0:T(8,128)(2,1)S(1)}, u32[]{:S(2)}, u32[]{:S(2)}) collective-permute-start(bf16[384,384]{1,0:T(8,128)(2,1)} %get-tuple-element.28.own), channel_id=1, source_target_pairs={{0,1},{1,2},{2,3},{3,4},{4,5},{5,6},{6,7},{7,8},{8,9},{9,10},{10,1... | collective-permute-start | bytes 884744 | tf_op jit(solution)/shard_map/ppermute | solution.py:24
  119.3 4.6 %collective-permute-start.26 = (bf16[384,384]{1,0:T(8,128)(2,1)}, bf16[384,384]{1,0:T(8,128)(2,1)S(1)}, u32[]{:S(2)}, u32[]{:S(2)}) collective-permute-start(bf16[384,384]{1,0:T(8,128)(2,1)} %get-tuple-element.35), channel_id=1, source_target_pairs={{1,0},{2,1},{3,2},{4,3},{5,4},{6,5},{7,6},{8,7},{9,8},{10,9},{11,1... | collective-permute-start | bytes 884744 | tf_op jit(solution)/shard_map/ppermute | solution.py:24
  124.7 16.6 %copy-start.11 = (bf16[768,1536]{1,0:T(8,128)(2,1)S(1)}, bf16[768,1536]{1,0:T(8,128)(2,1)}, u32[]{:S(2)}) copy-start(bf16[768,1536]{1,0:T(8,128)(2,1)} %get-tuple-element.43) | copy-start | bytes 7077892
  135.6 8.8 %collective-permute-start.37 = (bf16[384,192]{1,0:T(8,128)(2,1)}, bf16[384,192]{1,0:T(8,128)(2,1)}, u32[]{:S(2)}, u32[]{:S(2)}) collective-permute-start(bf16[384,192]{1,0:T(8,128)(2,1)} %slice.227), channel_id=1, source_target_pairs={{0,1},{1,0},{2,3},{3,2},{4,5},{5,4},{6,7},{7,6},{8,9},{9,8},{10,11... | collective-permute-start | bytes 442376 | tf_op jit(solution)/shard_map/ppermute | solution.py:36
  142.4 53.2 %collective-permute-start.47 = (bf16[384,1536]{1,0:T(8,128)(2,1)}, bf16[384,1536]{1,0:T(8,128)(2,1)}, u32[]{:S(2)}, u32[]{:S(2)}) collective-permute-start(bf16[384,1536]{1,0:T(8,128)(2,1)} %slice.250), channel_id=1, source_target_pairs={{0,1},{1,0},{2,3},{3,2},{4,5},{5,4},{6,7},{7,6},{8,9},{9,8},{10,11... | collective-permute-start | bytes 3538952 | tf_op jit(solution)/shard_map/ppermute | solution.py:36
  143.0 30.3 %copy-start.9 = (bf16[768,1536]{1,0:T(8,128)(2,1)S(1)}, bf16[768,1536]{1,0:T(8,128)(2,1)}, u32[]{:S(2)}) copy-start(bf16[768,1536]{1,0:T(8,128)(2,1)} %get-tuple-element.44) | copy-start | bytes 7077892
  143.0 33.6 %collective-permute-start.32 = (bf16[384,768]{1,0:T(8,128)(2,1)S(1)}, bf16[384,768]{1,0:T(8,128)(2,1)}, u32[]{:S(2)}, u32[]{:S(2)}) collective-permute-start(bf16[384,768]{1,0:T(8,128)(2,1)S(1)} %slice.215), channel_id=1, source_target_pairs={{0,1},{1,0},{2,3},{3,2},{4,5},{5,4},{6,7},{7,6},{8,9},{9,8},{10,11... | collective-permute-start | bytes 1769480 | tf_op jit(solution)/shard_map/ppermute | solution.py:36
  145.4 5.2 %collective-permute-start.38 = (bf16[192,192]{1,0:T(8,128)(2,1)S(1)}, bf16[192,192]{1,0:T(8,128)(2,1)S(1)}, u32[]{:S(2)}, u32[]{:S(2)}) collective-permute-start(bf16[192,192]{1,0:T(8,128)(2,1)S(1)} %slice.389), channel_id=1, source_target_pairs={{0,4},{1,5},{2,6},{3,7},{4,0},{5,1},{6,2},{7,3},{8,12},{9,13},{10,... | collective-permute-start | bytes 221192 | tf_op jit(solution)/shard_map/ppermute | solution.py:36
  146.9 13.1 %collective-permute-start.27 = (f32[2,576]{1,0:T(2,128)S(1)}, f32[2,576]{1,0:T(2,128)S(1)}, u32[]{:S(2)}, u32[]{:S(2)}) collective-permute-start(f32[2,576]{1,0:T(2,128)S(1)} %pad_maximum_fusion.17), channel_id=1, source_target_pairs={{0,1},{1,0},{2,3},{3,2},{4,5},{5,4},{6,7},{7,6},{8,9},{9,8},{10,11... | collective-permute-start | bytes 13832 | tf_op jit(solution)/shard_map/ppermute | solution.py:36
  150.6 23.8 %copy-start.6 = (bf16[2304,576]{1,0:T(8,128)(2,1)S(1)}, bf16[2304,576]{1,0:T(8,128)(2,1)}, u32[]{:S(2)}) copy-start(bf16[2304,576]{1,0:T(8,128)(2,1)} %get-tuple-element.42) | copy-start | bytes 7962628
  150.7 11.4 %collective-permute-start.39 = (bf16[96,192]{1,0:T(8,128)(2,1)S(1)}, bf16[96,192]{1,0:T(8,128)(2,1)S(1)}, u32[]{:S(2)}, u32[]{:S(2)}) collective-permute-start(bf16[96,192]{1,0:T(8,128)(2,1)S(1)} %slice.394), channel_id=1, source_target_pairs={{0,2},{1,3},{2,0},{3,1},{4,6},{5,7},{6,4},{7,5},{8,10},{9,11},{10,... | collective-permute-start | bytes 110600 | tf_op jit(solution)/shard_map/ppermute | solution.py:36
  160.0 3.7 %collective-permute-start.28 = (f32[2,576]{1,0:T(2,128)S(1)}, f32[2,576]{1,0:T(2,128)S(1)}, u32[]{:S(2)}, u32[]{:S(2)}) collective-permute-start(f32[2,576]{1,0:T(2,128)S(1)} %fusion.6), channel_id=1, source_target_pairs={{0,2},{1,3},{2,0},{3,1},{4,6},{5,7},{6,4},{7,5},{8,10},{9,11},{10,... | collective-permute-start | bytes 13832 | tf_op jit(solution)/shard_map/ppermute | solution.py:36
  162.1 14.5 %collective-permute-start.40 = (bf16[48,192]{1,0:T(8,128)(2,1)S(1)}, bf16[48,192]{1,0:T(8,128)(2,1)S(1)}, u32[]{:S(2)}, u32[]{:S(2)}) collective-permute-start(bf16[48,192]{1,0:T(8,128)(2,1)S(1)} %slice.396), channel_id=1, source_target_pairs={{0,24},{1,25},{2,26},{3,27},{4,28},{5,29},{6,30},{7,31},{8,16},{9,... | collective-permute-start | bytes 55304 | tf_op jit(solution)/shard_map/ppermute | solution.py:36
  163.7 3.7 %collective-permute-start.29 = (f32[2,576]{1,0:T(2,128)S(1)}, f32[2,576]{1,0:T(2,128)S(1)}, u32[]{:S(2)}, u32[]{:S(2)}) collective-permute-start(f32[2,576]{1,0:T(2,128)S(1)} %fusion.13), channel_id=1, source_target_pairs={{0,4},{1,5},{2,6},{3,7},{4,0},{5,1},{6,2},{7,3},{8,12},{9,13},{10,... | collective-permute-start | bytes 13832 | tf_op jit(solution)/shard_map/ppermute | solution.py:36
  167.4 3.6 %collective-permute-start.30 = (f32[2,576]{1,0:T(2,128)S(1)}, f32[2,576]{1,0:T(2,128)S(1)}, u32[]{:S(2)}, u32[]{:S(2)}) collective-permute-start(f32[2,576]{1,0:T(2,128)S(1)} %add.236), channel_id=1, source_target_pairs={{0,8},{1,9},{2,10},{3,11},{4,12},{5,13},{6,14},{7,15},{8,0},{9,1},... | collective-permute-start | bytes 13832 | tf_op jit(solution)/shard_map/ppermute | solution.py:36
  171.0 5.4 %collective-permute-start.31 = (f32[2,576]{1,0:T(2,128)S(1)}, f32[2,576]{1,0:T(2,128)S(1)}, u32[]{:S(2)}, u32[]{:S(2)}) collective-permute-start(f32[2,576]{1,0:T(2,128)S(1)} %add.237), channel_id=1, source_target_pairs={{0,24},{1,25},{2,26},{3,27},{4,28},{5,29},{6,30},{7,31},{8,16},{9,... | collective-permute-start | bytes 13832 | tf_op jit(solution)/shard_map/ppermute | solution.py:36
  174.5 27.2 %collective-permute-start.52 = (bf16[384,1536]{1,0:T(8,128)(2,1)}, bf16[384,1536]{1,0:T(8,128)(2,1)}, u32[]{:S(2)}, u32[]{:S(2)}) collective-permute-start(bf16[384,1536]{1,0:T(8,128)(2,1)} %slice.261), channel_id=1, source_target_pairs={{0,1},{1,0},{2,3},{3,2},{4,5},{5,4},{6,7},{7,6},{8,9},{9,8},{10,11... | collective-permute-start | bytes 3538952 | tf_op jit(solution)/shard_map/ppermute | solution.py:36
  176.4 28.8 %collective-permute-start.42 = (bf16[1152,576]{0,1:T(8,128)(2,1)S(1)}, bf16[1152,576]{0,1:T(8,128)(2,1)S(1)}, u32[]{:S(2)}, u32[]{:S(2)}) collective-permute-start(bf16[1152,576]{0,1:T(8,128)(2,1)S(1)} %copy.37), channel_id=1, source_target_pairs={{0,1},{1,0},{2,3},{3,2},{4,5},{5,4},{6,7},{7,6},{8,9},{9,8},{10,11... | collective-permute-start | bytes 3981320 | tf_op jit(solution)/shard_map/ppermute | solution.py:36
  176.6 4.4 %collective-permute-start.41 = (bf16[24,192]{1,0:T(8,128)(2,1)S(1)}, bf16[24,192]{1,0:T(8,128)(2,1)S(1)}, u32[]{:S(2)}, u32[]{:S(2)}) collective-permute-start(bf16[24,192]{1,0:T(8,128)(2,1)S(1)} %slice.397), channel_id=1, source_target_pairs={{0,8},{1,9},{2,10},{3,11},{4,12},{5,13},{6,14},{7,15},{8,0},{9,1},... | collective-permute-start | bytes 27656 | tf_op jit(solution)/shard_map/ppermute | solution.py:36
  178.0 17.6 %copy-start.12 = (bf16[768,1536]{1,0:T(8,128)(2,1)S(1)}, bf16[768,1536]{1,0:T(8,128)(2,1)}, u32[]{:S(2)}) copy-start(bf16[768,1536]{1,0:T(8,128)(2,1)} %get-tuple-element.43) | copy-start | bytes 7077892
  178.1 11.3 %collective-permute-start.33 = (bf16[192,768]{1,0:T(8,128)(2,1)S(1)}, bf16[192,768]{1,0:T(8,128)(2,1)S(1)}, u32[]{:S(2)}, u32[]{:S(2)}) collective-permute-start(bf16[192,768]{1,0:T(8,128)(2,1)S(1)} %slice.384), channel_id=1, source_target_pairs={{0,24},{1,25},{2,26},{3,27},{4,28},{5,29},{6,30},{7,31},{8,16},{9,... | collective-permute-start | bytes 884744 | tf_op jit(solution)/shard_map/ppermute | solution.py:36
  189.4 9.8 %collective-permute-start.34 = (bf16[96,768]{1,0:T(8,128)(2,1)S(1)}, bf16[96,768]{1,0:T(8,128)(2,1)S(1)}, u32[]{:S(2)}, u32[]{:S(2)}) collective-permute-start(bf16[96,768]{1,0:T(8,128)(2,1)S(1)} %slice.388), channel_id=1, source_target_pairs={{0,8},{1,9},{2,10},{3,11},{4,12},{5,13},{6,14},{7,15},{8,0},{9,1},... | collective-permute-start | bytes 442376 | tf_op jit(solution)/shard_map/ppermute | solution.py:36
  197.5 20.9 %collective-permute-start.48 = (bf16[192,1536]{1,0:T(8,128)(2,1)S(1)}, bf16[192,1536]{1,0:T(8,128)(2,1)}, u32[]{:S(2)}, u32[]{:S(2)}) collective-permute-start(bf16[192,1536]{1,0:T(8,128)(2,1)S(1)} %slice.380), channel_id=1, source_target_pairs={{0,2},{1,3},{2,0},{3,1},{4,6},{5,7},{6,4},{7,5},{8,10},{9,11},{10,... | collective-permute-start | bytes 1769480 | tf_op jit(solution)/shard_map/ppermute | solution.py:36
  199.9 6.9 %collective-permute-start.35 = (bf16[48,768]{1,0:T(8,128)(2,1)}, bf16[48,768]{1,0:T(8,128)(2,1)}, u32[]{:S(2)}, u32[]{:S(2)}) collective-permute-start(bf16[48,768]{1,0:T(8,128)(2,1)} %slice.393), channel_id=1, source_target_pairs={{0,4},{1,5},{2,6},{3,7},{4,0},{5,1},{6,2},{7,3},{8,12},{9,13},{10,... | collective-permute-start | bytes 221192 | tf_op jit(solution)/shard_map/ppermute | solution.py:36
  204.9 18.0 %collective-permute-start.53 = (bf16[192,1536]{1,0:T(8,128)(2,1)}, bf16[192,1536]{1,0:T(8,128)(2,1)}, u32[]{:S(2)}, u32[]{:S(2)}) collective-permute-start(bf16[192,1536]{1,0:T(8,128)(2,1)} %slice.379), channel_id=1, source_target_pairs={{0,4},{1,5},{2,6},{3,7},{4,0},{5,1},{6,2},{7,3},{8,12},{9,13},{10,... | collective-permute-start | bytes 1769480 | tf_op jit(solution)/shard_map/ppermute | solution.py:36
  207.7 6.4 %collective-permute-start.36 = (bf16[24,768]{1,0:T(8,128)(2,1)S(1)}, bf16[24,768]{1,0:T(8,128)(2,1)S(1)}, u32[]{:S(2)}, u32[]{:S(2)}) collective-permute-start(bf16[24,768]{1,0:T(8,128)(2,1)S(1)} %slice.395), channel_id=1, source_target_pairs={{0,2},{1,3},{2,0},{3,1},{4,6},{5,7},{6,4},{7,5},{8,10},{9,11},{10,... | collective-permute-start | bytes 110600 | tf_op jit(solution)/shard_map/ppermute | solution.py:36
  212.3 18.5 %collective-permute-start.43 = (bf16[576,576]{1,0:T(8,128)(2,1)}, bf16[576,576]{1,0:T(8,128)(2,1)}, u32[]{:S(2)}, u32[]{:S(2)}) collective-permute-start(bf16[576,576]{1,0:T(8,128)(2,1)} %slice.378), channel_id=1, source_target_pairs={{0,8},{1,9},{2,10},{3,11},{4,12},{5,13},{6,14},{7,15},{8,0},{9,1},... | collective-permute-start | bytes 1990664 | tf_op jit(solution)/shard_map/ppermute | solution.py:36
  220.2 18.4 %collective-permute-start.49 = (bf16[96,1536]{1,0:T(8,128)(2,1)S(1)}, bf16[96,1536]{1,0:T(8,128)(2,1)S(1)}, u32[]{:S(2)}, u32[]{:S(2)}) collective-permute-start(bf16[96,1536]{1,0:T(8,128)(2,1)S(1)} %slice.383), channel_id=1, source_target_pairs={{0,24},{1,25},{2,26},{3,27},{4,28},{5,29},{6,30},{7,31},{8,16},{9,... | collective-permute-start | bytes 884744 | tf_op jit(solution)/shard_map/ppermute | solution.py:36
  224.1 14.7 %collective-permute-start.54 = (bf16[96,1536]{1,0:T(8,128)(2,1)S(1)}, bf16[96,1536]{1,0:T(8,128)(2,1)S(1)}, u32[]{:S(2)}, u32[]{:S(2)}) collective-permute-start(bf16[96,1536]{1,0:T(8,128)(2,1)S(1)} %slice.382), channel_id=1, source_target_pairs={{0,2},{1,3},{2,0},{3,1},{4,6},{5,7},{6,4},{7,5},{8,10},{9,11},{10,... | collective-permute-start | bytes 884744 | tf_op jit(solution)/shard_map/ppermute | solution.py:36
  232.2 18.2 %collective-permute-start.44 = (bf16[288,576]{1,0:T(8,128)(2,1)S(1)}, bf16[288,576]{1,0:T(8,128)(2,1)S(1)}, u32[]{:S(2)}, u32[]{:S(2)}) collective-permute-start(bf16[288,576]{1,0:T(8,128)(2,1)S(1)} %slice.381), channel_id=1, source_target_pairs={{0,4},{1,5},{2,6},{3,7},{4,0},{5,1},{6,2},{7,3},{8,12},{9,13},{10,... | collective-permute-start | bytes 995336 | tf_op jit(solution)/shard_map/ppermute | solution.py:36
  238.7 5.2 %collective-permute-start.50 = (bf16[48,1536]{1,0:T(8,128)(2,1)S(1)}, bf16[48,1536]{1,0:T(8,128)(2,1)S(1)}, u32[]{:S(2)}, u32[]{:S(2)}) collective-permute-start(bf16[48,1536]{1,0:T(8,128)(2,1)S(1)} %slice.387), channel_id=1, source_target_pairs={{0,8},{1,9},{2,10},{3,11},{4,12},{5,13},{6,14},{7,15},{8,0},{9,1},... | collective-permute-start | bytes 442376 | tf_op jit(solution)/shard_map/ppermute | solution.py:36
  238.8 9.2 %collective-permute-start.55 = (bf16[48,1536]{1,0:T(8,128)(2,1)S(1)}, bf16[48,1536]{1,0:T(8,128)(2,1)S(1)}, u32[]{:S(2)}, u32[]{:S(2)}) collective-permute-start(bf16[48,1536]{1,0:T(8,128)(2,1)S(1)} %slice.386), channel_id=1, source_target_pairs={{0,24},{1,25},{2,26},{3,27},{4,28},{5,29},{6,30},{7,31},{8,16},{9,... | collective-permute-start | bytes 442376 | tf_op jit(solution)/shard_map/ppermute | solution.py:36
  243.9 6.4 %collective-permute-start.51 = (bf16[24,1536]{1,0:T(8,128)(2,1)S(1)}, bf16[24,1536]{1,0:T(8,128)(2,1)S(1)}, u32[]{:S(2)}, u32[]{:S(2)}) collective-permute-start(bf16[24,1536]{1,0:T(8,128)(2,1)S(1)} %slice.392), channel_id=1, source_target_pairs={{0,4},{1,5},{2,6},{3,7},{4,0},{5,1},{6,2},{7,3},{8,12},{9,13},{10,... | collective-permute-start | bytes 221192 | tf_op jit(solution)/shard_map/ppermute | solution.py:36
  248.1 4.4 %collective-permute-start.56 = (bf16[24,1536]{1,0:T(8,128)(2,1)S(1)}, bf16[24,1536]{1,0:T(8,128)(2,1)S(1)}, u32[]{:S(2)}, u32[]{:S(2)}) collective-permute-start(bf16[24,1536]{1,0:T(8,128)(2,1)S(1)} %slice.391), channel_id=1, source_target_pairs={{0,8},{1,9},{2,10},{3,11},{4,12},{5,13},{6,14},{7,15},{8,0},{9,1},... | collective-permute-start | bytes 221192 | tf_op jit(solution)/shard_map/ppermute | solution.py:36
  250.5 5.6 %collective-permute-start.45 = (bf16[144,576]{1,0:T(8,128)(2,1)S(1)}, bf16[144,576]{1,0:T(8,128)(2,1)S(1)}, u32[]{:S(2)}, u32[]{:S(2)}) collective-permute-start(bf16[144,576]{1,0:T(8,128)(2,1)S(1)} %slice.385), channel_id=1, source_target_pairs={{0,2},{1,3},{2,0},{3,1},{4,6},{5,7},{6,4},{7,5},{8,10},{9,11},{10,... | collective-permute-start | bytes 497672 | tf_op jit(solution)/shard_map/ppermute | solution.py:36
  256.2 6.4 %collective-permute-start.46 = (bf16[72,576]{1,0:T(8,128)(2,1)S(1)}, bf16[72,576]{1,0:T(8,128)(2,1)S(1)}, u32[]{:S(2)}, u32[]{:S(2)}) collective-permute-start(bf16[72,576]{1,0:T(8,128)(2,1)S(1)} %slice.390), channel_id=1, source_target_pairs={{0,24},{1,25},{2,26},{3,27},{4,28},{5,29},{6,30},{7,31},{8,16},{9,... | collective-permute-start | bytes 248840 | tf_op jit(solution)/shard_map/ppermute | solution.py:36
  (20 other events, 90.9 us)
where the time goes:
time: 269 us; the launch traced here: 264 us
  starting transfers between devices  80.8 us (30%)
  waiting for transfers between devices  63.1 us (23%)
  Pallas kernels  59.3 us (22%)
  local copies, waits for them, and re-layouts  41.3 us (15%)
  other arithmetic  18 us (7%)
    ppermute x55, starting transfers between devices, swapped(): return lax.ppermute(value, 'dev', [(i, i ^ mask) for i in range(count)])  77 us
    ppermute x55, waiting for transfers between devices, swapped(): return lax.ppermute(value, 'dev', [(i, i ^ mask) for i in range(count)])  61.6 us
    pallas_call x5, Pallas kernels, call_whole(): pl.pallas_call(kernel, out_shape=[jax.ShapeDtypeStruct(s, d) for s, d in...  59.3 us
    add x25, other arithmetic, halved(): h[:k].astype(f32) + g.astype(f32)  13.9 us
    slice x26, local copies, waits for them, and re-layouts, halved(): h[k:].astype(bf16)  8.35 us
    unnamed x70, local copies, waits for them, and re-layouts  7.99 us
  transfers between devices with their start and end apart: 57, of which 20 were waited for; matrix products, arithmetic and copies ran while one was open for 19% of the time, Pallas kernels for 6%

commit v1 on v0

--- a/solution.py
+++ b/solution.py
@@ -6,6 +6,7 @@
 from jax.experimental import pallas as pl
 from jax.experimental.pallas import tpu as pltpu
 from jax.sharding import PartitionSpec as P
+
 
 D = 576
 H = 9
@@ -489,7 +490,6 @@
     src_b,
     src_g,
     src_u,
-    src_d,
     wb0,
     wb1,
     wg0,
@@ -499,16 +499,14 @@
     wd0,
     wd1,
     mixed_out,
-    gres_out,
-    gatt_out,
-    dgain_out,
+    res_out,
+    dgate,
+    dup,
     dg_out,
     du_out,
     dd_out,
     wd,
     act,
-    dgate,
-    dup,
     wide_g,
     wide_u,
 ):
@@ -519,16 +517,14 @@
         target = pl.multiple_of(slots[p] * rows_d, rows_d)
         wd[pl.ds(target, rows_d), :] = half[at * rows_d : (at + 1) * rows_d, :]
     wb = jnp.concatenate([wb0[...], wb1[...]], axis=0)
-    spread_b = spread_wide(src_b[...])
-    spread_g = spread_wide(src_g[...])
-    spread_u = spread_wide(src_u[...])
     cot_tok = cot[...].T
-    att_wide = dot_nn(att[...].T, spread_b).astype(bf16)
+    att_wide = dot_nn(att[...].T, spread_wide(src_b[...])).astype(bf16)
     residual = tok[...].astype(f32).T + dot_nn(att_wide, wb)[:, :D]
+    res_out[...] = residual
     inverse = lax.rsqrt(jnp.mean(residual * residual, axis=-1, keepdims=True) + norm_epsilon)
     normed = (residual * inverse * gain[...]).astype(bf16)
-    wide_g[...] = dot_nn(normed, spread_g).astype(bf16)
-    wide_u[...] = dot_nn(normed, spread_u).astype(bf16)
+    wide_g[...] = dot_nn(normed, spread_wide(src_g[...])).astype(bf16)
+    wide_u[...] = dot_nn(normed, spread_wide(src_u[...])).astype(bf16)
     block = 256
 
     def ff_step(j, carry):
@@ -546,6 +542,38 @@
     lax.fori_loop(0, FF // block, ff_step, 0)
     mixed = residual + dot_nn(act[...], wd[...])
     mixed_out[...] = mixed.T.astype(bf16)
+    dg_out[...] = dot_nn(wide_g[...].T, dgate[...]).astype(bf16)
+    du_out[...] = dot_nn(wide_u[...].T, dup[...]).astype(bf16)
+    wd[...] = dot_nn(act[...].T, cot_tok).astype(bf16)
+    for p in range(count):
+        source = pl.multiple_of(slots[p] * rows_d, rows_d)
+        dd_out[p * rows_d : (p + 1) * rows_d, :] = wd[pl.ds(source, rows_d), :]
+
+
+def feed_back_kernel(
+    residual_in,
+    cot,
+    gain,
+    src_b,
+    src_g,
+    src_u,
+    dgate,
+    dup,
+    wb0,
+    wb1,
+    wg0,
+    wg1,
+    wu0,
+    wu1,
+    gres_out,
+    gatt_out,
+    dgain_out,
+):
+    residual = residual_in[...]
+    spread_b = spread_wide(src_b[...])
+    spread_g = spread_wide(src_g[...])
+    spread_u = spread_wide(src_u[...])
+    inverse = lax.rsqrt(jnp.mean(residual * residual, axis=-1, keepdims=True) + norm_epsilon)
     dn_g = dot_nt(dgate[...], jnp.concatenate([wg0[...], wg1[...]], axis=0))
     dn_u = dot_nt(dup[...], jnp.concatenate([wu0[...], wu1[...]], axis=0))
     grad_normed = sum(dot_nt(part, spread_g) for part in split_two(dn_g)) + sum(
@@ -554,22 +582,13 @@
     unit = residual * inverse
     scaled = grad_normed * gain[...]
     dgain_out[...] = jnp.sum(grad_normed * unit, axis=0, keepdims=True)
-    grad_res = cot_tok.astype(f32) + inverse * (
+    grad_res = cot[...].T.astype(f32) + inverse * (
         scaled - unit * jnp.mean(scaled * unit, axis=-1, keepdims=True)
     )
     gres_out[...] = grad_res.T
-    grad_res_b = grad_res.astype(bf16)
-    gatt_wide = dot_nt(wb[:, :D], grad_res_b).astype(bf16)
+    wb = jnp.concatenate([wb0[:, :D], wb1[:, :D]], axis=0)
+    gatt_wide = dot_nt(wb, grad_res.astype(bf16)).astype(bf16)
     gatt_out[...] = dot_nn(spread_b, gatt_wide).astype(bf16)
-    dg_out[...] = dot_nn(wide_g[...].T, dgate[...]).astype(bf16)
-    du_out[...] = dot_nn(wide_u[...].T, dup[...]).astype(bf16)
-    d_out = dot_nn(dot_nn(spread_tall(src_d[...]), att[...]).astype(bf16), grad_res_b).astype(bf16)
-    wd[...] = dot_nn(act[...].T, cot_tok).astype(bf16)
-    rows_all = rows_d + PAD
-    for p in range(count):
-        source = pl.multiple_of(slots[p] * rows_d, rows_d)
-        dd_out[p * rows_all : p * rows_all + rows_d, :] = wd[pl.ds(source, rows_d), :]
-        dd_out[p * rows_all + rows_d : (p + 1) * rows_all, :] = d_out[p * PAD : (p + 1) * PAD]
 
 
 def finish_kernel(
@@ -581,6 +600,8 @@
     cos,
     sin,
     gres,
+    att,
+    dgain_ffn,
     src_a,
     src_b,
     tall_a,
@@ -590,9 +611,8 @@
     wb0,
     wb1,
     dtok_out,
-    dgain_out,
     da_out,
-    dv_out,
+    db_out,
 ):
     x = tok[...].astype(f32)
     inverse = lax.rsqrt(jnp.mean(x * x, axis=0, keepdims=True) + norm_epsilon)
@@ -622,14 +642,22 @@
         dot_nn(spread_b, part) for part in split_two(dn_b)
     )
     scaled = grad_normed * gain[...]
-    dgain_out[...] = jnp.sum(grad_normed * unit, axis=1, keepdims=True)
     dtok_out[...] = gres[...] + inverse * (
         scaled - unit * jnp.mean(scaled * unit, axis=0, keepdims=True)
     )
+    dgain = jnp.sum(grad_normed * unit, axis=1, keepdims=True)
+    dgain = jnp.broadcast_to(dgain, (D, CHUNK)).T[:1]
+    tall_spread_b = spread_tall(tall_b[...])
     wide_a = dot_nn(spread_tall(tall_a[...]), normed).astype(bf16)
-    wide_b = dot_nn(spread_tall(tall_b[...]), normed).astype(bf16)
-    da_out[...] = dot_nt(wide_a, dqk).astype(bf16)
-    dv_out[...] = dot_nt(wide_b, dv).astype(bf16)
+    wide_b = dot_nn(tall_spread_b, normed).astype(bf16)
+    wide_att = dot_nn(tall_spread_b, att[...]).astype(bf16)
+    extra_a = tall_a[...] < 0
+    extra_b = tall_b[...] < 0
+    fill_a = jnp.concatenate([dgain, jnp.zeros((1, KVH * HD), f32)], axis=1)
+    da_out[...] = jnp.where(extra_a, fill_a, dot_nt(wide_a, dqk)).astype(bf16)
+    d_out = dot_nt(wide_att, gres[...].astype(bf16))
+    db_out[:, :D] = jnp.where(extra_b, dgain_ffn[...], d_out).astype(bf16)
+    db_out[:, D:] = dot_nt(wide_b, dv).astype(bf16)
 
 
 def call_whole(kernel, outs, operands, scratch=(), scalars=()):
@@ -645,30 +673,30 @@
     )(*scalars, *operands)
 
 
-def doubled(streams, orders):
-    held = list(streams)
-    got = None
-    for t in range(len(orders[0])):
-        got = [swapped(h, order[t]) for h, order in zip(held, orders)]
-        if t < len(orders[0]) - 1:
-            held = [jnp.concatenate([h, g], axis=0) for h, g in zip(held, got)]
-    return list(zip(held, got))
-
-
-def halved(streams, orders):
-    held = list(streams)
-    for t in range(len(orders[0])):
-        half = held[0].shape[0] // 2
-        halves = [h.shape[0] // 2 for h in held]
-        got = [
-            swapped(h[k:].astype(bf16), order[-1 - t])
-            for h, k, order in zip(held, halves, orders)
-        ]
-        held = [h[:k].astype(f32) + g.astype(f32) for h, k, g in zip(held, halves, got)]
-    return held
-
-
-def sources(order, count, per_slot):
+def step_double(held, orders, t):
+    got = []
+    for h, order in zip(held, orders):
+        got.append(swapped(h, order[t]))
+    return got
+
+
+def joined(held, got):
+    return [jnp.concatenate([h, g], axis=0) for h, g in zip(held, got)]
+
+
+def step_halve(held, orders, t, even=False):
+    halves = [h.shape[0] // 2 for h in held]
+    out = []
+    for h, k, order in zip(held, halves, orders):
+        g = swapped(h[k:].astype(bf16), order[-1 - t])
+        kept = h[:k].astype(f32)
+        if even:
+            kept = lax.reduce_precision(kept, 8, 7)
+        out.append(kept + g.astype(f32))
+    return out
+
+
+def sources(order, per_slot):
     me = lax.axis_index("dev")
     owner = me ^ jnp.asarray(slot_masks(order), jnp.int32)
     inner = jnp.arange(PAD, dtype=jnp.int32)[None, :]
@@ -692,32 +720,52 @@
     order_of = [rest[k:] + rest[:k] + [first] for k in range(len(rest))]
     ord_a, ord_b = order_of[0], order_of[2]
     ord_g, ord_u, ord_d = order_of[1], order_of[2], order_of[3]
-    src_a, src_b = sources(ord_a, count, per), sources(ord_b, count, per)
-    src_g, src_u = sources(ord_g, count, per), sources(ord_u, count, per)
-    src_d = sources(ord_d, count, per)
+    src_a, src_b = sources(ord_a, per), sources(ord_b, per)
+    src_g, src_u = sources(ord_g, per), sources(ord_u, per)
     slots = me ^ jnp.asarray(slot_masks(ord_d), jnp.int32)
     w_qs, w_kvs = w_query.reshape(per, H * HD), w_kv.reshape(per, 2 * KVH * HD)
-    w_gs = w_gate_up.reshape(per, 2 * FF)
     kv_cut = KVH * HD
     stream_a = padded_rows(jnp.concatenate([w_qs, w_kvs[:, :kv_cut]], axis=1))
     stream_b = padded_rows(jnp.concatenate([w_out.reshape(per, D), w_kvs[:, kv_cut:]], axis=1))
-    (wa0, wa1), (wb0, wb1) = doubled([stream_a, stream_b], [ord_a, ord_b])
-    stream_g, stream_u = padded_rows(w_gs[:, :FF]), padded_rows(w_gs[:, FF:])
-    stream_d = w_down.reshape(per_d, D)
-    (wg0, wg1), (wu0, wu1), (wd0, wd1) = doubled(
-        [stream_g, stream_u, stream_d], [ord_g, ord_u, ord_d]
-    )
     half_dim = HD // 2
     frequency = jnp.exp(jnp.arange(half_dim, dtype=f32) * (-2.0 * math.log(theta_base) / HD))
     angles = frequency[:, None] * positions.astype(f32)[None, :]
     cos, sin = jnp.cos(angles), jnp.sin(angles)
     tok_t, cot_t = tokens.T, cotangent.T
     gain_col = gain_attn.reshape(D, 1)
+    orders_ab, orders_gud = [ord_a, ord_b], [ord_g, ord_u, ord_d]
+    steps = len(ord_a)
+    hold = lax.optimization_barrier
+    held = [stream_a, stream_b]
+    ffn = None
+    early = (src_a[None], src_b[None], src_a[:, None], src_b[:, None])
+    early = early + (src_g[None], src_u[None], slots, cos, sin, gain_col)
+    for t in range(steps):
+        if t == 2:
+            held, w_gate_up, w_down = hold((held, w_gate_up, w_down))
+            w_gs = w_gate_up.reshape(per, 2 * FF)
+            ffn = [padded_rows(w_gs[:, :FF]), padded_rows(w_gs[:, FF:]), w_down.reshape(per_d, D)]
+        if t == 3:
+            held, early = hold((held, early))
+        got = step_double(held, orders_ab, t)
+        if t < steps - 1:
+            held = joined(held, got)
+        if t >= 2:
+            ffn = joined(ffn, step_double(ffn, orders_gud, t - 2))
+        if t == 3:
+            held, ffn = hold((held, ffn))
+    (wa0, wb0), (wa1, wb1) = held, got
+    row_a, row_b, tall_a, tall_b, row_g, row_u, slots, cos, sin, gain_col = early
     q_t, kv_t = call_whole(
         project_kernel,
         [((H * HD, row_count), bf16), ((2 * kv_cut, row_count), bf16)],
-        [tok_t, gain_col, cos, sin, src_a[None], src_b[None], wa0, wa1, wb0, wb1],
-    )
+        [tok_t, gain_col, cos, sin, row_a, row_b, wa0, wa1, wb0, wb1],
+    )
+    for t in range(steps - 2, steps):
+        got = step_double(ffn, orders_gud, t)
+        if t < steps - 1:
+            ffn = joined(ffn, got)
+    (wg0, wu0, wd0), (wg1, wu1, wd1) = ffn, got
     near = passed_along(kv_t, "dev", 1)
     chunks = row_count // CHUNK
     prob, att_t = call_whole(
@@ -729,46 +777,36 @@
         [q_t, near, kv_t, positions[None]],
     )
     wide = count * PAD
-    mixed_t, gres_t, gatt_t, dgain_ffn, dg, du, dd = call_whole(
+    mixed_t, residual, dgate, dup, dg, du, dd = call_whole(
         feed_kernel,
         [
             ((D, row_count), bf16),
-            ((D, row_count), f32),
-            ((H * HD, row_count), bf16),
-            ((1, D), f32),
+            ((row_count, D), f32),
+            ((row_count, FF), bf16),
+            ((row_count, FF), bf16),
             ((wide, FF), bf16),
             ((wide, FF), bf16),
-            ((count * (per_d + PAD), D), bf16),
+            ((FF, D), bf16),
         ],
-        [
-            att_t,
-            tok_t,
-            cot_t,
-            gain_ffn[None],
-            src_b[None],
-            src_g[None],
-            src_u[None],
-            src_d[:, None],
-            wb0,
-            wb1,
-            wg0,
-            wg1,
-            wu0,
-            wu1,
-            wd0,
-            wd1,
-        ],
+        [att_t, tok_t, cot_t, gain_ffn[None], row_b, row_g, row_u]
+        + [wb0, wb1, wg0, wg1, wu0, wu1, wd0, wd1],
         scratch=[
             pltpu.VMEM((FF, D), bf16),
-            pltpu.VMEM((row_count, FF), bf16),
-            pltpu.VMEM((row_count, FF), bf16),
             pltpu.VMEM((row_count, FF), bf16),
             pltpu.VMEM((row_count, wide), bf16),
             pltpu.VMEM((row_count, wide), bf16),
         ],
         scalars=[slots],
     )
-    share_g, share_u, share_d = halved([dg, du, dd], [ord_g, ord_u, ord_d])
+    sums = [dg, du, dd]
+    gres_t, gatt_t, dgain_ffn = call_whole(
+        feed_back_kernel,
+        [((D, row_count), f32), ((H * HD, row_count), bf16), ((1, D), f32)],
+        [residual, cot_t, gain_ffn[None], row_b, row_g, row_u, dgate, dup]
+        + [wb0, wb1, wg0, wg1, wu0, wu1],
+    )
+    for t in range(3):
+        sums = step_halve(sums, orders_gud, t)
     dq_t, dnear, down = call_whole(
         attend_back_kernel,
         [
@@ -780,47 +818,35 @@
         scratch=[pltpu.VMEM((HD, 2 * row_count), f32)] * 2,
     )
     back = passed_along(dnear, "dev", -1)
-    dtok_t, dgain_attn, da, dv = call_whole(
+    dtok_t, da, db = call_whole(
         finish_kernel,
         [
             ((D, row_count), f32),
-            ((D, 1), f32),
             ((wide, H * HD + kv_cut), bf16),
-            ((wide, kv_cut), bf16),
+            ((wide, D + kv_cut), bf16),
         ],
-        [
-            dq_t,
-            down,
-            back,
-            tok_t,
-            gain_col,
-            cos,
-            sin,
-            gres_t,
-            src_a[None],
-            src_b[None],
-            src_a[:, None],
-            src_b[:, None],
-            wa0,
-            wa1,
-            wb0,
-            wb1,
-        ],
-    )
-    share_a, share_v = halved([da, dv], [ord_a, ord_b])
-    gain_sums = sum_all(jnp.concatenate([dgain_attn.reshape(1, D), dgain_ffn], axis=0))
-    share_kv = jnp.concatenate([share_a[:per, H * HD :], share_v[:per]], axis=1)
+        [dq_t, down, back, tok_t, gain_col, cos, sin, gres_t, att_t, dgain_ffn]
+        + [row_a, row_b, tall_a, tall_b, wa0, wa1, wb0, wb1],
+    )
+    last = [da, db]
+    for t in range(steps):
+        last = step_halve(last, orders_ab, t, even=True)
+        if t + 3 < steps:
+            sums = step_halve(sums, orders_gud, t + 3)
+    share_g, share_u, share_d = sums
+    share_a, share_b = last
+    share_kv = jnp.concatenate([share_a[:per, H * HD :], share_b[:per, D:]], axis=1)
     share_gu = jnp.concatenate([share_g[:per], share_u[:per]], axis=1)
     return (
         mixed_t.T,
         dtok_t.T,
-        gain_sums[0],
+        share_a[per, :D],
         share_a[:per, : H * HD].reshape(-1),
         share_kv.reshape(-1),
-        share_d[per_d : per_d + per].reshape(-1),
-        gain_sums[1],
+        share_b[:per, :D].reshape(-1),
+        share_b[per, :D],
         share_gu.reshape(-1),
-        share_d[:per_d].reshape(-1),
+        share_d.reshape(-1),
     )
 
 
@@ -853,5 +879,15 @@
         P("dev"),
         P("dev"),
     )
+    whole_rows = fits_whole_rows(mesh.shape["dev"])
+
+    def layer(*args):
+        return shards(*args)
+
     return jax.shard_map(
-        shards if fits_whole_rows(mesh.shape["dev"]) else shards_general, mesh=mesh, in_specs=in_specs, out_specs=out_specs, check_vma=False)
+        layer if whole_rows else shards_general,
+        mesh=mesh,
+        in_specs=in_specs,
+        out_specs=out_specs,
+        check_vma=False,
+    )

time: 269 us -> 272 us (1.011)
  local copies, waits for them, and re-layouts: 41.3 us -> 36.3 us
  Pallas kernels: 59.3 us -> 64.1 us
    pallas_call x5 -> x6, Pallas kernels: 59.3 us -> 64.1 us  [call_whole(): pl.pallas_call(kernel, out_shape=[jax.ShapeDtypeStruct(s, d) for s, d in...]
    optimization_barrier x0 -> x3, local copies, waits for them, and re-layouts: none -> 2.75 us  [shards(): held, early = hold((held, early))]
    add x30 -> x25, other arithmetic: 13.9 us -> 11.3 us  [step_halve(): out.append(kept + g.astype(f32))]
    unnamed x70 -> x44, local copies, waits for them, and re-layouts: 7.99 us -> 5.52 us
    ppermute x55 -> x50, starting transfers between devices: 77 us -> 79.1 us  [swapped(): return lax.ppermute(value, 'dev', [(i, i ^ mask) for i in range(count)])]
    ppermute x55 -> x50, waiting for transfers between devices: 61.6 us -> 61.7 us  [swapped(): return lax.ppermute(value, 'dev', [(i, i ^ mask) for i in range(count)])]
  transfers between devices with their start and end apart: 57 -> 52, of which waited for: 20 -> 20; matrix products, arithmetic and copies ran while one was open for 19% -> 17% of each run, Pallas kernels for 6% -> 6%
where the time goes in v1:
time: 272 us; the launch traced here: 266 us
  starting transfers between devices  82.7 us (30%)
  waiting for transfers between devices  64.7 us (24%)
  Pallas kernels  64.1 us (24%)
  local copies, waits for them, and re-layouts  36.3 us (13%)
  other arithmetic  17 us (6%)
    ppermute x50, starting transfers between devices, swapped(): return lax.ppermute(value, 'dev', [(i, i ^ mask) for i in range(count)])  79.1 us
    pallas_call x6, Pallas kernels, call_whole(): pl.pallas_call(kernel, out_shape=[jax.ShapeDtypeStruct(s, d) for s, d in...  64.1 us
    ppermute x50, waiting for transfers between devices, swapped(): return lax.ppermute(value, 'dev', [(i, i ^ mask) for i in range(count)])  61.7 us
    add x25, other arithmetic, step_halve(): out.append(kept + g.astype(f32))  11.3 us
    slice x26, local copies, waits for them, and re-layouts, step_halve(): g = swapped(h[k:].astype(bf16), order[-1 - t])  9.64 us
    unnamed x44, local copies, waits for them, and re-layouts  5.52 us
  transfers between devices with their start and end apart: 52, of which 20 were waited for; matrix products, arithmetic and copies ran while one was open for 17% of the time, Pallas kernels for 6%

profile of v1, /device:TPU:0, one launch (start us, length us, event | category | flops | bytes accessed | tf_op | source)
XLA Modules:
  0.0 266.3 jit_solution(14698685227389716391)
XLA Ops:
  2.4 3.0 %collective-permute-start = (bf16[24,768]{1,0:T(8,128)(2,1)S(1)}, bf16[24,768]{1,0:T(8,128)(2,1)S(1)}, u32[]{:S(2)}, u32[]{:S(2)}) collective-permute-start(bf16[24,768]{1,0:T(8,128)(2,1)S(1)} %fusion.12), channel_id=1, source_target_pairs={{0,2},{1,3},{2,0},{3,1},{4,6},{5,7},{6,4},{7,5},{8,10},{9,11},{10,... | collective-permute-start | bytes 110600 | tf_op jit(solution)/shard_map/ppermute | solution.py:37
  6.3 1.6 collective-permute-start.2
  10.9 1.2 broadcast_xor_fusion.slots
  15.0 1.6 collective-permute-start.1
  16.6 2.5 collective-permute-start.3
  19.4 3.4 %collective-permute-done.3 = bf16[48,768]{1,0:T(8,128)(2,1)S(1)} collective-permute-done((bf16[48,768]{1,0:T(8,128)(2,1)S(1)}, bf16[48,768]{1,0:T(8,128)(2,1)S(1)}, u32[]{:S(2)}, u32[]{:S(2)}) %collective-permute-start.3) | collective-permute-done | bytes 73760 | tf_op jit(solution)/shard_map/ppermute | solution.py:37
  23.7 2.5 collective-permute-start.12
  27.9 1.9 collective-permute-done.12
  29.9 1.6 collective-permute-start.13
  32.2 2.5 collective-permute-start.11
  34.9 1.4 collective-permute-start.6
  36.3 1.2 collective-permute-start.7
  37.5 1.9 collective-permute-done.9
  39.4 1.9 collective-permute-done.11
  41.4 3.1 %collective-permute-done.6 = bf16[192,768]{1,0:T(8,128)(2,1)S(1)} collective-permute-done((bf16[192,768]{1,0:T(8,128)(2,1)S(1)}, bf16[192,768]{1,0:T(8,128)(2,1)S(1)}, u32[]{:S(2)}, u32[]{:S(2)}) %collective-permute-start.6) | collective-permute-done | bytes 294944 | tf_op jit(solution)/shard_map/ppermute | solution.py:37
  45.5 2.0 collective-permute-start.17
  49.6 5.1 %collective-permute-done.23 = bf16[192,576]{1,0:T(8,128)(2,1)S(1)} collective-permute-done((bf16[192,576]{1,0:T(8,128)(2,1)S(1)}, bf16[192,576]{1,0:T(8,128)(2,1)S(1)}, u32[]{:S(2)}, u32[]{:S(2)}) %collective-permute-start.23) | collective-permute-done | bytes 221216 | tf_op jit(solution)/shard_map/ppermute | solution.py:37
  54.7 12.6 %collective-permute-start.24 = (bf16[384,576]{1,0:T(8,128)(2,1)S(1)}, bf16[384,576]{1,0:T(8,128)(2,1)S(1)}, u32[]{:S(2)}, u32[]{:S(2)}) collective-permute-start(bf16[384,576]{1,0:T(8,128)(2,1)S(1)} %pad_maximum_fusion.4), channel_id=1, source_target_pairs={{0,8},{1,9},{2,10},{3,11},{4,12},{5,13},{6,14},{7,15},{8,0},{9,1},... | collective-permute-start | bytes 1327112 | tf_op jit(solution)/shard_map/ppermute | solution.py:37
  67.4 1.6 collective-permute-start.18
  69.6 9.8 %collective-permute-done.18 = bf16[192,1536]{1,0:T(8,128)(2,1)S(1)} collective-permute-done((bf16[192,1536]{1,0:T(8,128)(2,1)S(1)}, bf16[192,1536]{1,0:T(8,128)(2,1)S(1)}, u32[]{:S(2)}, u32[]{:S(2)}) %collective-permute-start.18) | collective-permute-done | bytes 589856 | tf_op jit(solution)/shard_map/ppermute | solution.py:37
  79.5 1.4 collective-permute-done.21
  84.0 2.2 copy.29
  88.3 4.8 %shard_map.214 = (bf16[576,384]{1,0:T(8,128)(2,1)}, bf16[384,384]{1,0:T(8,128)(2,1)}) custom-call(bf16[576,384]{1,0:T(8,128)(2,1)} %bitcast.4, f32[576,1]{1,0:T(8,128)} %copy.28.gain, f32[32,384]{1,0:T(8,128)} %get-tuple-element.54.cos, f32[32,384]{1,0:T(8,128)} %get-tuple-element.55.sin, s32[1,768]{1,0:T(1,128)} %select_n.74.src_a, ...), custom_call_target="tpu_custom_call" | custom-call | tf_op jit(solution)/shard_map/pallas_call | solution.py:666
  93.1 2.3 collective-permute-start.16
  97.3 12.1 %shard_map.215 = (bf16[3,3,512,384]{3,2,1,0:T(8,128)(2,1)}, bf16[576,384]{1,0:T(8,128)(2,1)}) custom-call(bf16[576,384]{1,0:T(8,128)(2,1)} %get-tuple-element.64.q, bf16[384,384]{1,0:T(8,128)(2,1)} %copy-done.13, bf16[384,384]{1,0:T(8,128)(2,1)} %get-tuple-element.65.own, s32[1,384]{1,0:T(1,128)} %broadcast_in_dim.49.pos), custom_call_target="tpu_custom_call" | custom-call | tf_op jit(solution)/shard_map/pallas_call | solution.py:666
  109.5 2.2 copy.30.wd1
  111.7 16.9 %shard_map.216 = (bf16[576,384]{1,0:T(8,128)(2,1)}, f32[384,576]{1,0:T(8,128)}, bf16[384,1536]{1,0:T(8,128)(2,1)}, bf16[384,1536]{1,0:T(8,128)(2,1)}, bf16[768,1...) custom-call(s32[32]{0:T(128)} %broadcast_xor_fusion.slots, ...), custom_call_target="tpu_custom_call" | custom-call | tf_op jit(solution)/shard_map/pallas_call | solution.py:666
  128.6 11.2 %shard_map.217 = (f32[576,384]{1,0:T(8,128)}, bf16[576,384]{1,0:T(8,128)(2,1)}, f32[1,576]{1,0:T(1,128)}) custom-call(f32[384,576]{1,0:T(8,128)} %get-tuple-element.74.residual_in, bf16[576,384]{1,0:T(8,128)(2,1)} %bitcast.8, f32[1,576]{1,0:T(1,128)} %broadcast_in_dim.50.gain, s32[1,768]{1,0:T(1,128)} %select_n.76.src_b.src_u, s32[1,768]{1,0:T(1,128)} %select_n.80.src_g, ...), custom_call_target="tpu_custom_call" | custom-call | tf_op jit(solution)/shard_map/pallas_call | solution.py:666
  139.8 8.5 %shard_map.218 = (bf16[576,384]{1,0:T(8,128)(2,1)}, bf16[384,384]{1,0:T(8,128)(2,1)}, f32[384,384]{1,0:T(8,128)}) custom-call(bf16[576,384]{1,0:T(8,128)(2,1)} %get-tuple-element.64.q, bf16[384,384]{1,0:T(8,128)(2,1)} %copy-done.13, bf16[384,384]{1,0:T(8,128)(2,1)} %get-tuple-element.65.own, bf16[3,3,512,384]{3,2,1,0:T(8,128)(2,1)} %get-tuple-element.73.prob, ...), custom_call_target="tpu_custom_call" | custom-call | tf_op jit(solution)/shard_map/pallas_call | solution.py:666
  148.3 1.3 collective-permute-start.26
  151.5 2.9 %collective-permute-done.26.back = bf16[384,384]{1,0:T(8,128)(2,1)S(1)} collective-permute-done((bf16[384,384]{1,0:T(8,128)(2,1)}, bf16[384,384]{1,0:T(8,128)(2,1)S(1)}, u32[]{:S(2)}, u32[]{:S(2)}) %collective-permute-start.26) | collective-permute-done | bytes 294944 | tf_op jit(solution)/shard_map/ppermute | solution.py:25
  155.2 10.5 %shard_map.219 = (f32[576,384]{1,0:T(8,128)}, bf16[768,768]{1,0:T(8,128)(2,1)}, bf16[768,768]{1,0:T(8,128)(2,1)}) custom-call(bf16[576,384]{1,0:T(8,128)(2,1)} %get-tuple-element.78.dq, f32[384,384]{1,0:T(8,128)} %get-tuple-element.79.own, bf16[384,384]{1,0:T(8,128)(2,1)} %copy-done.14, bf16[576,384]{1,0:T(8,128)(2,1)} %bitcast.6, f32[576,1]{1,0:T(8,128)} %copy.28.gain, ...), custom_call_target="tpu_custom_call" | custom-call | tf_op jit(solution)/shard_map/pallas_call | solution.py:666
  165.7 1.9 slice.211
  167.6 5.7 %collective-permute-start.27 = (bf16[384,768]{1,0:T(8,128)(2,1)}, bf16[384,768]{1,0:T(8,128)(2,1)}, u32[]{:S(2)}, u32[]{:S(2)}) collective-permute-start(bf16[384,768]{1,0:T(8,128)(2,1)} %slice.211), channel_id=1, source_target_pairs={{0,1},{1,0},{2,3},{3,2},{4,5},{5,4},{6,7},{7,6},{8,9},{9,8},{10,11... | collective-permute-start | bytes 1769480 | tf_op jit(solution)/shard_map/ppermute | solution.py:37
  173.4 1.5 copy.34
  180.4 1.2 convert_add_fusion.4
  182.4 2.5 collective-permute-start.28
  185.7 1.5 copy.35
  187.3 1.4 convert_add_fusion.2
  188.8 5.6 %collective-permute-done.28 = bf16[192,768]{1,0:T(8,128)(2,1)} collective-permute-done((bf16[192,768]{1,0:T(8,128)(2,1)}, bf16[192,768]{1,0:T(8,128)(2,1)}, u32[]{:S(2)}, u32[]{:S(2)}) %collective-permute-start.28) | collective-permute-done | bytes 294944 | tf_op jit(solution)/shard_map/ppermute | solution.py:37
  194.4 1.2 fusion.1
  195.6 5.6 %collective-permute-start.29 = (bf16[96,768]{1,0:T(8,128)(2,1)S(1)}, bf16[96,768]{1,0:T(8,128)(2,1)S(1)}, u32[]{:S(2)}, u32[]{:S(2)}) collective-permute-start(bf16[96,768]{1,0:T(8,128)(2,1)S(1)} %slice.398), channel_id=1, source_target_pairs={{0,8},{1,9},{2,10},{3,11},{4,12},{5,13},{6,14},{7,15},{8,0},{9,1},... | collective-permute-start | bytes 442376 | tf_op jit(solution)/shard_map/ppermute | solution.py:37
  203.0 1.7 convert_add_fusion
  204.8 2.4 collective-permute-start.43
  207.2 1.6 convert_add_fusion.1
  211.0 1.7 collective-permute-start.35
  212.9 1.7 collective-permute-start.49
  214.5 8.4 %collective-permute-done.30 = bf16[48,768]{1,0:T(8,128)(2,1)S(1)} collective-permute-done((bf16[48,768]{1,0:T(8,128)(2,1)S(1)}, bf16[48,768]{1,0:T(8,128)(2,1)S(1)}, u32[]{:S(2)}, u32[]{:S(2)}) %collective-permute-start.30) | collective-permute-done | bytes 73760 | tf_op jit(solution)/shard_map/ppermute | solution.py:37
  223.0 1.1 collective-permute-start.31
  224.2 2.9 %collective-permute-done.31 = bf16[24,768]{1,0:T(8,128)(2,1)S(1)} collective-permute-done((bf16[24,768]{1,0:T(8,128)(2,1)S(1)}, bf16[24,768]{1,0:T(8,128)(2,1)S(1)}, u32[]{:S(2)}, u32[]{:S(2)}) %collective-permute-start.31) | collective-permute-done | bytes 36896 | tf_op jit(solution)/shard_map/ppermute | solution.py:37
  230.0 3.2 %collective-permute-done.50 = bf16[96,576]{1,0:T(8,128)(2,1)S(1)} collective-permute-done((bf16[96,576]{1,0:T(8,128)(2,1)S(1)}, bf16[96,576]{1,0:T(8,128)(2,1)S(1)}, u32[]{:S(2)}, u32[]{:S(2)}) %collective-permute-start.50) | collective-permute-done | bytes 110624 | tf_op jit(solution)/shard_map/ppermute | solution.py:37
  233.3 1.8 collective-permute-start.51
  237.2 2.2 collective-permute-done.51
  240.1 1.3 slice_add_fusion
  242.5 1.2 slice_add_fusion.1
  243.7 2.4 collective-permute-start.39
  246.1 2.2 collective-permute-done.44
  248.4 1.8 collective-permute-start.45
  250.2 3.8 %collective-permute-done.39 = bf16[96,1536]{1,0:T(8,128)(2,1)S(1)} collective-permute-done((bf16[96,1536]{1,0:T(8,128)(2,1)S(1)}, bf16[96,1536]{1,0:T(8,128)(2,1)S(1)}, u32[]{:S(2)}, u32[]{:S(2)}) %collective-permute-start.39) | collective-permute-done | bytes 294944 | tf_op jit(solution)/shard_map/ppermute | solution.py:37
  254.0 3.7 %collective-permute-start.40 = (bf16[48,1536]{1,0:T(8,128)(2,1)S(1)}, bf16[48,1536]{1,0:T(8,128)(2,1)S(1)}, u32[]{:S(2)}, u32[]{:S(2)}) collective-permute-start(bf16[48,1536]{1,0:T(8,128)(2,1)S(1)} %slice.396), channel_id=1, source_target_pairs={{0,8},{1,9},{2,10},{3,11},{4,12},{5,13},{6,14},{7,15},{8,0},{9,1},... | collective-permute-start | bytes 442376 | tf_op jit(solution)/shard_map/ppermute | solution.py:37
  257.7 1.5 collective-permute-start.46
  259.2 1.6 collective-permute-done.40
  260.9 1.7 collective-permute-start.41
  262.6 2.7 %collective-permute-done.41 = bf16[24,1536]{1,0:T(8,128)(2,1)S(1)} collective-permute-done((bf16[24,1536]{1,0:T(8,128)(2,1)S(1)}, bf16[24,1536]{1,0:T(8,128)(2,1)S(1)}, u32[]{:S(2)}, u32[]{:S(2)}) %collective-permute-start.41) | collective-permute-done | bytes 73760 | tf_op jit(solution)/shard_map/ppermute | solution.py:37
  (209 shorter events, 45.5 us)
Async XLA Ops:
  0.6 22.8 %copy-start.15 = (bf16[55296]{0:T(1024)(128)(2,1)S(1)}, bf16[55296]{0:T(1024)(128)(2,1)}, u32[]{:S(2)}) copy-start(bf16[55296]{0:T(1024)(128)(2,1)} %param.22) | copy-start | bytes 331780
  0.7 22.9 %copy-start.16 = (bf16[27648]{0:T(1024)(128)(2,1)S(1)}, bf16[27648]{0:T(1024)(128)(2,1)}, u32[]{:S(2)}) copy-start(bf16[27648]{0:T(1024)(128)(2,1)} %param.23) | copy-start | bytes 165892
  2.4 12.5 %collective-permute-start = (bf16[24,768]{1,0:T(8,128)(2,1)S(1)}, bf16[24,768]{1,0:T(8,128)(2,1)S(1)}, u32[]{:S(2)}, u32[]{:S(2)}) collective-permute-start(bf16[24,768]{1,0:T(8,128)(2,1)S(1)} %fusion.12), channel_id=1, source_target_pairs={{0,2},{1,3},{2,0},{3,1},{4,6},{5,7},{6,4},{7,5},{8,10},{9,11},{10,... | collective-permute-start | bytes 110600 | tf_op jit(solution)/shard_map/ppermute | solution.py:37
  6.3 10.3 %collective-permute-start.2 = (bf16[24,768]{1,0:T(8,128)(2,1)S(1)}, bf16[24,768]{1,0:T(8,128)(2,1)S(1)}, u32[]{:S(2)}, u32[]{:S(2)}) collective-permute-start(bf16[24,768]{1,0:T(8,128)(2,1)S(1)} %fusion.13), channel_id=1, source_target_pairs={{0,8},{1,9},{2,10},{3,11},{4,12},{5,13},{6,14},{7,15},{8,0},{9,1},... | collective-permute-start | bytes 110600 | tf_op jit(solution)/shard_map/ppermute | solution.py:37
  15.0 4.4 %collective-permute-start.1 = (bf16[48,768]{1,0:T(8,128)(2,1)S(1)}, bf16[48,768]{1,0:T(8,128)(2,1)S(1)}, u32[]{:S(2)}, u32[]{:S(2)}) collective-permute-start(bf16[48,768]{1,0:T(8,128)(2,1)S(1)} %pad_maximum_fusion.16), channel_id=1, source_target_pairs={{0,4},{1,5},{2,6},{3,7},{4,0},{5,1},{6,2},{7,3},{8,12},{9,13},{10,... | collective-permute-start | bytes 221192 | tf_op jit(solution)/shard_map/ppermute | solution.py:37
  16.6 6.2 %collective-permute-start.3 = (bf16[48,768]{1,0:T(8,128)(2,1)S(1)}, bf16[48,768]{1,0:T(8,128)(2,1)S(1)}, u32[]{:S(2)}, u32[]{:S(2)}) collective-permute-start(bf16[48,768]{1,0:T(8,128)(2,1)S(1)} %pad_maximum_fusion.17), channel_id=1, source_target_pairs={{0,24},{1,25},{2,26},{3,27},{4,28},{5,29},{6,30},{7,31},{8,16},{9,... | collective-permute-start | bytes 221192 | tf_op jit(solution)/shard_map/ppermute | solution.py:37
  22.8 12.0 %collective-permute-start.4 = (bf16[96,768]{1,0:T(8,128)(2,1)S(1)}, bf16[96,768]{1,0:T(8,128)(2,1)S(1)}, u32[]{:S(2)}, u32[]{:S(2)}) collective-permute-start(bf16[96,768]{1,0:T(8,128)(2,1)S(1)} %pad_maximum_fusion.11), channel_id=1, source_target_pairs={{0,8},{1,9},{2,10},{3,11},{4,12},{5,13},{6,14},{7,15},{8,0},{9,1},... | collective-permute-start | bytes 442376 | tf_op jit(solution)/shard_map/ppermute | solution.py:37
  22.9 11.9 %collective-permute-start.5 = (bf16[96,768]{1,0:T(8,128)(2,1)S(1)}, bf16[96,768]{1,0:T(8,128)(2,1)S(1)}, u32[]{:S(2)}, u32[]{:S(2)}) collective-permute-start(bf16[96,768]{1,0:T(8,128)(2,1)S(1)} %pad_maximum_fusion.12), channel_id=1, source_target_pairs={{0,2},{1,3},{2,0},{3,1},{4,6},{5,7},{6,4},{7,5},{8,10},{9,11},{10,... | collective-permute-start | bytes 442376 | tf_op jit(solution)/shard_map/ppermute | solution.py:37
  23.7 6.2 %collective-permute-start.12 = (bf16[48,576]{1,0:T(8,128)(2,1)S(1)}, bf16[48,576]{1,0:T(8,128)(2,1)S(1)}, u32[]{:S(2)}, u32[]{:S(2)}) collective-permute-start(bf16[48,576]{1,0:T(8,128)(2,1)S(1)} %reshape.291), channel_id=1, source_target_pairs={{0,24},{1,25},{2,26},{3,27},{4,28},{5,29},{6,30},{7,31},{8,16},{9,... | collective-permute-start | bytes 165896 | tf_op jit(solution)/shard_map/ppermute | solution.py:37
  26.2 5.2 %collective-permute-start.8 = (bf16[24,1536]{1,0:T(8,128)(2,1)S(1)}, bf16[24,1536]{1,0:T(8,128)(2,1)S(1)}, u32[]{:S(2)}, u32[]{:S(2)}) collective-permute-start(bf16[24,1536]{1,0:T(8,128)(2,1)S(1)} %pad.16), channel_id=1, source_target_pairs={{0,4},{1,5},{2,6},{3,7},{4,0},{5,1},{6,2},{7,3},{8,12},{9,13},{10,... | collective-permute-start | bytes 221192 | tf_op jit(solution)/shard_map/ppermute | solution.py:37
  26.8 5.4 %collective-permute-start.10 = (bf16[24,1536]{1,0:T(8,128)(2,1)S(1)}, bf16[24,1536]{1,0:T(8,128)(2,1)S(1)}, u32[]{:S(2)}, u32[]{:S(2)}) collective-permute-start(bf16[24,1536]{1,0:T(8,128)(2,1)S(1)} %pad.17), channel_id=1, source_target_pairs={{0,8},{1,9},{2,10},{3,11},{4,12},{5,13},{6,14},{7,15},{8,0},{9,1},... | collective-permute-start | bytes 221192 | tf_op jit(solution)/shard_map/ppermute | solution.py:37
  29.9 7.6 %collective-permute-start.13 = (bf16[96,576]{1,0:T(8,128)(2,1)S(1)}, bf16[96,576]{1,0:T(8,128)(2,1)S(1)}, u32[]{:S(2)}, u32[]{:S(2)}) collective-permute-start(bf16[96,576]{1,0:T(8,128)(2,1)S(1)} %pad_maximum_fusion.15), channel_id=1, source_target_pairs={{0,2},{1,3},{2,0},{3,1},{4,6},{5,7},{6,4},{7,5},{8,10},{9,11},{10,... | collective-permute-start | bytes 331784 | tf_op jit(solution)/shard_map/ppermute | solution.py:37
  31.5 7.9 %collective-permute-start.9 = (bf16[48,1536]{1,0:T(8,128)(2,1)S(1)}, bf16[48,1536]{1,0:T(8,128)(2,1)S(1)}, u32[]{:S(2)}, u32[]{:S(2)}) collective-permute-start(bf16[48,1536]{1,0:T(8,128)(2,1)S(1)} %pad_maximum_fusion.13), channel_id=1, source_target_pairs={{0,8},{1,9},{2,10},{3,11},{4,12},{5,13},{6,14},{7,15},{8,0},{9,1},... | collective-permute-start | bytes 442376 | tf_op jit(solution)/shard_map/ppermute | solution.py:37
  32.2 9.1 %collective-permute-start.11 = (bf16[48,1536]{1,0:T(8,128)(2,1)S(1)}, bf16[48,1536]{1,0:T(8,128)(2,1)S(1)}, u32[]{:S(2)}, u32[]{:S(2)}) collective-permute-start(bf16[48,1536]{1,0:T(8,128)(2,1)S(1)} %pad_maximum_fusion.14), channel_id=1, source_target_pairs={{0,24},{1,25},{2,26},{3,27},{4,28},{5,29},{6,30},{7,31},{8,16},{9,... | collective-permute-start | bytes 442376 | tf_op jit(solution)/shard_map/ppermute | solution.py:37
  34.9 9.7 %collective-permute-start.6 = (bf16[192,768]{1,0:T(8,128)(2,1)S(1)}, bf16[192,768]{1,0:T(8,128)(2,1)S(1)}, u32[]{:S(2)}, u32[]{:S(2)}) collective-permute-start(bf16[192,768]{1,0:T(8,128)(2,1)S(1)} %pad_maximum_fusion.5), channel_id=1, source_target_pairs={{0,24},{1,25},{2,26},{3,27},{4,28},{5,29},{6,30},{7,31},{8,16},{9,... | collective-permute-start | bytes 884744 | tf_op jit(solution)/shard_map/ppermute | solution.py:37
  36.3 9.1 %collective-permute-start.7 = (bf16[192,768]{1,0:T(8,128)(2,1)S(1)}, bf16[192,768]{1,0:T(8,128)(2,1)S(1)}, u32[]{:S(2)}, u32[]{:S(2)}) collective-permute-start(bf16[192,768]{1,0:T(8,128)(2,1)S(1)} %pad_maximum_fusion.6), channel_id=1, source_target_pairs={{0,4},{1,5},{2,6},{3,7},{4,0},{5,1},{6,2},{7,3},{8,12},{9,13},{10,... | collective-permute-start | bytes 884744 | tf_op jit(solution)/shard_map/ppermute | solution.py:37
  45.4 36.9 %copy-start = (bf16[384,768]{1,0:T(8,128)(2,1)}, bf16[384,768]{1,0:T(8,128)(2,1)S(1)}, u32[]{:S(2)}) copy-start(bf16[384,768]{1,0:T(8,128)(2,1)S(1)} %pad_maximum_fusion.1.wb0) | copy-start | bytes 1769476
  45.5 21.8 %collective-permute-start.17 = (bf16[96,1536]{1,0:T(8,128)(2,1)S(1)}, bf16[96,1536]{1,0:T(8,128)(2,1)S(1)}, u32[]{:S(2)}, u32[]{:S(2)}) collective-permute-start(bf16[96,1536]{1,0:T(8,128)(2,1)S(1)} %pad_maximum_fusion.7), channel_id=1, source_target_pairs={{0,24},{1,25},{2,26},{3,27},{4,28},{5,29},{6,30},{7,31},{8,16},{9,... | collective-permute-start | bytes 884744 | tf_op jit(solution)/shard_map/ppermute | solution.py:37
  47.5 21.5 %collective-permute-start.20 = (bf16[96,1536]{1,0:T(8,128)(2,1)S(1)}, bf16[96,1536]{1,0:T(8,128)(2,1)S(1)}, u32[]{:S(2)}, u32[]{:S(2)}) collective-permute-start(bf16[96,1536]{1,0:T(8,128)(2,1)S(1)} %pad_maximum_fusion.8), channel_id=1, source_target_pairs={{0,2},{1,3},{2,0},{3,1},{4,6},{5,7},{6,4},{7,5},{8,10},{9,11},{10,... | collective-permute-start | bytes 884744 | tf_op jit(solution)/shard_map/ppermute | solution.py:37
  48.5 6.2 %collective-permute-start.23 = (bf16[192,576]{1,0:T(8,128)(2,1)S(1)}, bf16[192,576]{1,0:T(8,128)(2,1)S(1)}, u32[]{:S(2)}, u32[]{:S(2)}) collective-permute-start(bf16[192,576]{1,0:T(8,128)(2,1)S(1)} %pad_maximum_fusion.10), channel_id=1, source_target_pairs={{0,4},{1,5},{2,6},{3,7},{4,0},{5,1},{6,2},{7,3},{8,12},{9,13},{10,... | collective-permute-start | bytes 663560 | tf_op jit(solution)/shard_map/ppermute | solution.py:37
  54.7 28.5 %collective-permute-start.24 = (bf16[384,576]{1,0:T(8,128)(2,1)S(1)}, bf16[384,576]{1,0:T(8,128)(2,1)S(1)}, u32[]{:S(2)}, u32[]{:S(2)}) collective-permute-start(bf16[384,576]{1,0:T(8,128)(2,1)S(1)} %pad_maximum_fusion.4), channel_id=1, source_target_pairs={{0,8},{1,9},{2,10},{3,11},{4,12},{5,13},{6,14},{7,15},{8,0},{9,1},... | collective-permute-start | bytes 1327112 | tf_op jit(solution)/shard_map/ppermute | solution.py:37
  67.4 12.1 %collective-permute-start.18 = (bf16[192,1536]{1,0:T(8,128)(2,1)S(1)}, bf16[192,1536]{1,0:T(8,128)(2,1)S(1)}, u32[]{:S(2)}, u32[]{:S(2)}) collective-permute-start(bf16[192,1536]{1,0:T(8,128)(2,1)S(1)} %pad_maximum_fusion.2), channel_id=1, source_target_pairs={{0,2},{1,3},{2,0},{3,1},{4,6},{5,7},{6,4},{7,5},{8,10},{9,11},{10,... | collective-permute-start | bytes 1769480 | tf_op jit(solution)/shard_map/ppermute | solution.py:37
  69.0 12.0 %collective-permute-start.21 = (bf16[192,1536]{1,0:T(8,128)(2,1)S(1)}, bf16[192,1536]{1,0:T(8,128)(2,1)S(1)}, u32[]{:S(2)}, u32[]{:S(2)}) collective-permute-start(bf16[192,1536]{1,0:T(8,128)(2,1)S(1)} %pad_maximum_fusion.3), channel_id=1, source_target_pairs={{0,4},{1,5},{2,6},{3,7},{4,0},{5,1},{6,2},{7,3},{8,12},{9,13},{10,... | collective-permute-start | bytes 1769480 | tf_op jit(solution)/shard_map/ppermute | solution.py:37
  79.5 4.6 %copy-start.4 = (bf16[384,1536]{1,0:T(8,128)(2,1)}, bf16[384,1536]{1,0:T(8,128)(2,1)S(1)}, u32[]{:S(2)}) copy-start(bf16[384,1536]{1,0:T(8,128)(2,1)S(1)} %constant_dynamic-update-slice_fusion.wg0) | copy-start | bytes 3538948
  79.5 32.2 %collective-permute-start.19 = (bf16[384,1536]{1,0:T(8,128)(2,1)S(1)}, bf16[384,1536]{1,0:T(8,128)(2,1)}, u32[]{:S(2)}, u32[]{:S(2)}) collective-permute-start(bf16[384,1536]{1,0:T(8,128)(2,1)S(1)} %constant_dynamic-update-slice_fusion.wg0), channel_id=1, source_target_pairs={{0,1},{1,0},{2,3},{3,2},{4,5},{5,4},{6,7},{7,6},{8,9},{9,8},{10,11... | collective-permute-start | bytes 3538952 | tf_op jit(solution)/shard_map/ppermute | solution.py:37
  81.0 5.2 %copy-start.5 = (bf16[384,1536]{1,0:T(8,128)(2,1)}, bf16[384,1536]{1,0:T(8,128)(2,1)S(1)}, u32[]{:S(2)}) copy-start(bf16[384,1536]{1,0:T(8,128)(2,1)S(1)} %constant_dynamic-update-slice_fusion.3.wu0) | copy-start | bytes 3538948
  81.0 30.7 %collective-permute-start.22 = (bf16[384,1536]{1,0:T(8,128)(2,1)S(1)}, bf16[384,1536]{1,0:T(8,128)(2,1)}, u32[]{:S(2)}, u32[]{:S(2)}) collective-permute-start(bf16[384,1536]{1,0:T(8,128)(2,1)S(1)} %constant_dynamic-update-slice_fusion.3.wu0), channel_id=1, source_target_pairs={{0,1},{1,0},{2,3},{3,2},{4,5},{5,4},{6,7},{7,6},{8,9},{9,8},{10,11... | collective-permute-start | bytes 3538952 | tf_op jit(solution)/shard_map/ppermute | solution.py:37
  82.0 5.5 %collective-permute-start.14 = (bf16[384,768]{1,0:T(8,128)(2,1)}, bf16[384,768]{1,0:T(8,128)(2,1)}, u32[]{:S(2)}, u32[]{:S(2)}) collective-permute-start(bf16[384,768]{1,0:T(8,128)(2,1)} %pad_maximum_fusion.wa0), channel_id=1, source_target_pairs={{0,1},{1,0},{2,3},{3,2},{4,5},{5,4},{6,7},{7,6},{8,9},{9,8},{10,11... | collective-permute-start | bytes 1769480 | tf_op jit(solution)/shard_map/ppermute | solution.py:37
  82.3 5.1 %collective-permute-start.15 = (bf16[384,768]{1,0:T(8,128)(2,1)S(1)}, bf16[384,768]{1,0:T(8,128)(2,1)S(1)}, u32[]{:S(2)}, u32[]{:S(2)}) collective-permute-start(bf16[384,768]{1,0:T(8,128)(2,1)S(1)} %pad_maximum_fusion.1.wb0), channel_id=1, source_target_pairs={{0,1},{1,0},{2,3},{3,2},{4,5},{5,4},{6,7},{7,6},{8,9},{9,8},{10,11... | collective-permute-start | bytes 1769480 | tf_op jit(solution)/shard_map/ppermute | solution.py:37
  86.2 23.3 %collective-permute-start.25 = (bf16[768,576]{0,1:T(8,128)(2,1)}, bf16[768,576]{0,1:T(8,128)(2,1)}, u32[]{:S(2)}, u32[]{:S(2)}) collective-permute-start(bf16[768,576]{0,1:T(8,128)(2,1)} %copy.29), channel_id=1, source_target_pairs={{0,1},{1,0},{2,3},{3,2},{4,5},{5,4},{6,7},{7,6},{8,9},{9,8},{10,11... | collective-permute-start | bytes 2654216 | tf_op jit(solution)/shard_map/ppermute | solution.py:37
  88.3 7.1 %copy-start.17 = (s32[384]{0:T(512)S(1)}, s32[384]{0:T(512)}, u32[]{:S(2)}) copy-start(s32[384]{0:T(512)} %param.16) | copy-start | bytes 4612
  88.3 7.7 %copy-start.18 = (f32[576]{0:T(1024)S(1)}, f32[576]{0:T(1024)}, u32[]{:S(2)}) copy-start(f32[576]{0:T(1024)} %param.21) | copy-start | bytes 6916
  93.1 3.5 %collective-permute-start.16 = (bf16[384,384]{1,0:T(8,128)(2,1)}, bf16[384,384]{1,0:T(8,128)(2,1)S(1)}, u32[]{:S(2)}, u32[]{:S(2)}) collective-permute-start(bf16[384,384]{1,0:T(8,128)(2,1)} %get-tuple-element.65.own), channel_id=1, source_target_pairs={{0,1},{1,2},{2,3},{3,4},{4,5},{5,6},{6,7},{7,8},{8,9},{9,10},{10,1... | collective-permute-start | bytes 884744 | tf_op jit(solution)/shard_map/ppermute | solution.py:25
  148.3 6.1 %collective-permute-start.26 = (bf16[384,384]{1,0:T(8,128)(2,1)}, bf16[384,384]{1,0:T(8,128)(2,1)S(1)}, u32[]{:S(2)}, u32[]{:S(2)}) collective-permute-start(bf16[384,384]{1,0:T(8,128)(2,1)} %get-tuple-element.80), channel_id=1, source_target_pairs={{1,0},{2,1},{3,2},{4,3},{5,4},{6,5},{7,6},{8,7},{9,8},{10,9},{11,1... | collective-permute-start | bytes 884744 | tf_op jit(solution)/shard_map/ppermute | solution.py:25
  155.1 18.2 %copy-start.10 = (bf16[1536,576]{1,0:T(8,128)(2,1)S(1)}, bf16[1536,576]{1,0:T(8,128)(2,1)}, u32[]{:S(2)}) copy-start(bf16[1536,576]{1,0:T(8,128)(2,1)} %get-tuple-element.90) | copy-start | bytes 5308420
  167.6 12.2 %collective-permute-start.27 = (bf16[384,768]{1,0:T(8,128)(2,1)}, bf16[384,768]{1,0:T(8,128)(2,1)}, u32[]{:S(2)}, u32[]{:S(2)}) collective-permute-start(bf16[384,768]{1,0:T(8,128)(2,1)} %slice.211), channel_id=1, source_target_pairs={{0,1},{1,0},{2,3},{3,2},{4,5},{5,4},{6,7},{7,6},{8,9},{9,8},{10,11... | collective-permute-start | bytes 1769480 | tf_op jit(solution)/shard_map/ppermute | solution.py:37
  173.4 3.2 %copy-start.8 = (bf16[768,1536]{1,0:T(8,128)(2,1)S(1)}, bf16[768,1536]{1,0:T(8,128)(2,1)}, u32[]{:S(2)}) copy-start(bf16[768,1536]{1,0:T(8,128)(2,1)} %get-tuple-element.89) | copy-start | bytes 7077892
  174.9 10.8 %collective-permute-start.47 = (bf16[768,576]{0,1:T(8,128)(2,1)}, bf16[768,576]{0,1:T(8,128)(2,1)}, u32[]{:S(2)}, u32[]{:S(2)}) collective-permute-start(bf16[768,576]{0,1:T(8,128)(2,1)} %copy.34), channel_id=1, source_target_pairs={{0,1},{1,0},{2,3},{3,2},{4,5},{5,4},{6,7},{7,6},{8,9},{9,8},{10,11... | collective-permute-start | bytes 2654216 | tf_op jit(solution)/shard_map/ppermute | solution.py:37
  176.0 8.8 %collective-permute-start.32 = (bf16[384,768]{1,0:T(8,128)(2,1)S(1)}, bf16[384,768]{1,0:T(8,128)(2,1)S(1)}, u32[]{:S(2)}, u32[]{:S(2)}) collective-permute-start(bf16[384,768]{1,0:T(8,128)(2,1)S(1)} %slice.224), channel_id=1, source_target_pairs={{0,1},{1,0},{2,3},{3,2},{4,5},{5,4},{6,7},{7,6},{8,9},{9,8},{10,11... | collective-permute-start | bytes 1769480 | tf_op jit(solution)/shard_map/ppermute | solution.py:37
  177.7 25.3 %collective-permute-start.42 = (bf16[384,1536]{1,0:T(8,128)(2,1)}, bf16[384,1536]{1,0:T(8,128)(2,1)}, u32[]{:S(2)}, u32[]{:S(2)}) collective-permute-start(bf16[384,1536]{1,0:T(8,128)(2,1)} %slice.248), channel_id=1, source_target_pairs={{0,1},{1,0},{2,3},{3,2},{4,5},{5,4},{6,7},{7,6},{8,9},{9,8},{10,11... | collective-permute-start | bytes 3538952 | tf_op jit(solution)/shard_map/ppermute | solution.py:37
  179.8 5.0 %copy-start.11 = (bf16[768,768]{1,0:T(8,128)(2,1)S(1)}, bf16[768,768]{1,0:T(8,128)(2,1)}, u32[]{:S(2)}) copy-start(bf16[768,768]{1,0:T(8,128)(2,1)} %get-tuple-element.87) | copy-start | bytes 3538948
  179.8 27.4 %collective-permute-start.37 = (bf16[384,1536]{1,0:T(8,128)(2,1)}, bf16[384,1536]{1,0:T(8,128)(2,1)}, u32[]{:S(2)}, u32[]{:S(2)}) collective-permute-start(bf16[384,1536]{1,0:T(8,128)(2,1)} %slice.237), channel_id=1, source_target_pairs={{0,1},{1,0},{2,3},{3,2},{4,5},{5,4},{6,7},{7,6},{8,9},{9,8},{10,11... | collective-permute-start | bytes 3538952 | tf_op jit(solution)/shard_map/ppermute | solution.py:37
  182.4 12.0 %collective-permute-start.28 = (bf16[192,768]{1,0:T(8,128)(2,1)}, bf16[192,768]{1,0:T(8,128)(2,1)}, u32[]{:S(2)}, u32[]{:S(2)}) collective-permute-start(bf16[192,768]{1,0:T(8,128)(2,1)} %slice.393), channel_id=1, source_target_pairs={{0,24},{1,25},{2,26},{3,27},{4,28},{5,29},{6,30},{7,31},{8,16},{9,... | collective-permute-start | bytes 884744 | tf_op jit(solution)/shard_map/ppermute | solution.py:37
  185.7 15.4 %collective-permute-start.33 = (bf16[192,768]{1,0:T(8,128)(2,1)}, bf16[192,768]{1,0:T(8,128)(2,1)}, u32[]{:S(2)}, u32[]{:S(2)}) collective-permute-start(bf16[192,768]{1,0:T(8,128)(2,1)} %slice.392), channel_id=1, source_target_pairs={{0,4},{1,5},{2,6},{3,7},{4,0},{5,1},{6,2},{7,3},{8,12},{9,13},{10,... | collective-permute-start | bytes 884744 | tf_op jit(solution)/shard_map/ppermute | solution.py:37
  188.7 24.0 %collective-permute-start.48 = (bf16[384,576]{1,0:T(8,128)(2,1)S(1)}, bf16[384,576]{1,0:T(8,128)(2,1)S(1)}, u32[]{:S(2)}, u32[]{:S(2)}) collective-permute-start(bf16[384,576]{1,0:T(8,128)(2,1)S(1)} %slice.389), channel_id=1, source_target_pairs={{0,8},{1,9},{2,10},{3,11},{4,12},{5,13},{6,14},{7,15},{8,0},{9,1},... | collective-permute-start | bytes 1327112 | tf_op jit(solution)/shard_map/ppermute | solution.py:37
  194.4 8.6 %copy-start.9 = (bf16[768,1536]{1,0:T(8,128)(2,1)S(1)}, bf16[768,1536]{1,0:T(8,128)(2,1)}, u32[]{:S(2)}) copy-start(bf16[768,1536]{1,0:T(8,128)(2,1)} %get-tuple-element.89) | copy-start | bytes 7077892
  195.6 14.2 %collective-permute-start.29 = (bf16[96,768]{1,0:T(8,128)(2,1)S(1)}, bf16[96,768]{1,0:T(8,128)(2,1)S(1)}, u32[]{:S(2)}, u32[]{:S(2)}) collective-permute-start(bf16[96,768]{1,0:T(8,128)(2,1)S(1)} %slice.398), channel_id=1, source_target_pairs={{0,8},{1,9},{2,10},{3,11},{4,12},{5,13},{6,14},{7,15},{8,0},{9,1},... | collective-permute-start | bytes 442376 | tf_op jit(solution)/shard_map/ppermute | solution.py:37
  202.2 8.7 %collective-permute-start.34 = (bf16[96,768]{1,0:T(8,128)(2,1)S(1)}, bf16[96,768]{1,0:T(8,128)(2,1)S(1)}, u32[]{:S(2)}, u32[]{:S(2)}) collective-permute-start(bf16[96,768]{1,0:T(8,128)(2,1)S(1)} %slice.397), channel_id=1, source_target_pairs={{0,2},{1,3},{2,0},{3,1},{4,6},{5,7},{6,4},{7,5},{8,10},{9,11},{10,... | collective-permute-start | bytes 442376 | tf_op jit(solution)/shard_map/ppermute | solution.py:37
  203.0 4.2 %copy-start.7 = (bf16[768,1536]{1,0:T(8,128)(2,1)S(1)}, bf16[768,1536]{1,0:T(8,128)(2,1)}, u32[]{:S(2)}) copy-start(bf16[768,1536]{1,0:T(8,128)(2,1)} %get-tuple-element.88) | copy-start | bytes 7077892
  204.8 35.3 %collective-permute-start.43 = (bf16[192,1536]{1,0:T(8,128)(2,1)S(1)}, bf16[192,1536]{1,0:T(8,128)(2,1)}, u32[]{:S(2)}, u32[]{:S(2)}) collective-permute-start(bf16[192,1536]{1,0:T(8,128)(2,1)S(1)} %slice.387), channel_id=1, source_target_pairs={{0,4},{1,5},{2,6},{3,7},{4,0},{5,1},{6,2},{7,3},{8,12},{9,13},{10,... | collective-permute-start | bytes 1769480 | tf_op jit(solution)/shard_map/ppermute | solution.py:37
  209.7 32.8 %collective-permute-start.38 = (bf16[192,1536]{1,0:T(8,128)(2,1)}, bf16[192,1536]{1,0:T(8,128)(2,1)}, u32[]{:S(2)}, u32[]{:S(2)}) collective-permute-start(bf16[192,1536]{1,0:T(8,128)(2,1)} %slice.388), channel_id=1, source_target_pairs={{0,2},{1,3},{2,0},{3,1},{4,6},{5,7},{6,4},{7,5},{8,10},{9,11},{10,... | collective-permute-start | bytes 1769480 | tf_op jit(solution)/shard_map/ppermute | solution.py:37
  209.8 13.1 %collective-permute-start.30 = (bf16[48,768]{1,0:T(8,128)(2,1)S(1)}, bf16[48,768]{1,0:T(8,128)(2,1)S(1)}, u32[]{:S(2)}, u32[]{:S(2)}) collective-permute-start(bf16[48,768]{1,0:T(8,128)(2,1)S(1)} %slice.403), channel_id=1, source_target_pairs={{0,4},{1,5},{2,6},{3,7},{4,0},{5,1},{6,2},{7,3},{8,12},{9,13},{10,... | collective-permute-start | bytes 221192 | tf_op jit(solution)/shard_map/ppermute | solution.py:37
  211.0 13.1 %collective-permute-start.35 = (bf16[48,768]{1,0:T(8,128)(2,1)S(1)}, bf16[48,768]{1,0:T(8,128)(2,1)S(1)}, u32[]{:S(2)}, u32[]{:S(2)}) collective-permute-start(bf16[48,768]{1,0:T(8,128)(2,1)S(1)} %slice.402), channel_id=1, source_target_pairs={{0,24},{1,25},{2,26},{3,27},{4,28},{5,29},{6,30},{7,31},{8,16},{9,... | collective-permute-start | bytes 221192 | tf_op jit(solution)/shard_map/ppermute | solution.py:37
  212.9 15.3 %collective-permute-start.49 = (bf16[192,576]{1,0:T(8,128)(2,1)S(1)}, bf16[192,576]{1,0:T(8,128)(2,1)S(1)}, u32[]{:S(2)}, u32[]{:S(2)}) collective-permute-start(bf16[192,576]{1,0:T(8,128)(2,1)S(1)} %slice.394), channel_id=1, source_target_pairs={{0,4},{1,5},{2,6},{3,7},{4,0},{5,1},{6,2},{7,3},{8,12},{9,13},{10,... | collective-permute-start | bytes 663560 | tf_op jit(solution)/shard_map/ppermute | solution.py:37
  223.0 4.1 %collective-permute-start.31 = (bf16[24,768]{1,0:T(8,128)(2,1)S(1)}, bf16[24,768]{1,0:T(8,128)(2,1)S(1)}, u32[]{:S(2)}, u32[]{:S(2)}) collective-permute-start(bf16[24,768]{1,0:T(8,128)(2,1)S(1)} %slice.406), channel_id=1, source_target_pairs={{0,2},{1,3},{2,0},{3,1},{4,6},{5,7},{6,4},{7,5},{8,10},{9,11},{10,... | collective-permute-start | bytes 110600 | tf_op jit(solution)/shard_map/ppermute | solution.py:37
  224.2 4.0 %collective-permute-start.36 = (bf16[24,768]{1,0:T(8,128)(2,1)S(1)}, bf16[24,768]{1,0:T(8,128)(2,1)S(1)}, u32[]{:S(2)}, u32[]{:S(2)}) collective-permute-start(bf16[24,768]{1,0:T(8,128)(2,1)S(1)} %slice.405), channel_id=1, source_target_pairs={{0,8},{1,9},{2,10},{3,11},{4,12},{5,13},{6,14},{7,15},{8,0},{9,1},... | collective-permute-start | bytes 110600 | tf_op jit(solution)/shard_map/ppermute | solution.py:37
  228.3 4.9 %collective-permute-start.50 = (bf16[96,576]{1,0:T(8,128)(2,1)S(1)}, bf16[96,576]{1,0:T(8,128)(2,1)S(1)}, u32[]{:S(2)}, u32[]{:S(2)}) collective-permute-start(bf16[96,576]{1,0:T(8,128)(2,1)S(1)} %slice.399), channel_id=1, source_target_pairs={{0,2},{1,3},{2,0},{3,1},{4,6},{5,7},{6,4},{7,5},{8,10},{9,11},{10,... | collective-permute-start | bytes 331784 | tf_op jit(solution)/shard_map/ppermute | solution.py:37
  233.3 6.1 %collective-permute-start.51 = (bf16[48,576]{1,0:T(8,128)(2,1)S(1)}, bf16[48,576]{1,0:T(8,128)(2,1)S(1)}, u32[]{:S(2)}, u32[]{:S(2)}) collective-permute-start(bf16[48,576]{1,0:T(8,128)(2,1)S(1)} %slice.404), channel_id=1, source_target_pairs={{0,24},{1,25},{2,26},{3,27},{4,28},{5,29},{6,30},{7,31},{8,16},{9,... | collective-permute-start | bytes 165896 | tf_op jit(solution)/shard_map/ppermute | solution.py:37
  241.5 6.8 %collective-permute-start.44 = (bf16[96,1536]{1,0:T(8,128)(2,1)S(1)}, bf16[96,1536]{1,0:T(8,128)(2,1)S(1)}, u32[]{:S(2)}, u32[]{:S(2)}) collective-permute-start(bf16[96,1536]{1,0:T(8,128)(2,1)S(1)} %slice.390), channel_id=1, source_target_pairs={{0,2},{1,3},{2,0},{3,1},{4,6},{5,7},{6,4},{7,5},{8,10},{9,11},{10,... | collective-permute-start | bytes 884744 | tf_op jit(solution)/shard_map/ppermute | solution.py:37
  243.7 10.2 %collective-permute-start.39 = (bf16[96,1536]{1,0:T(8,128)(2,1)S(1)}, bf16[96,1536]{1,0:T(8,128)(2,1)S(1)}, u32[]{:S(2)}, u32[]{:S(2)}) collective-permute-start(bf16[96,1536]{1,0:T(8,128)(2,1)S(1)} %slice.391), channel_id=1, source_target_pairs={{0,24},{1,25},{2,26},{3,27},{4,28},{5,29},{6,30},{7,31},{8,16},{9,... | collective-permute-start | bytes 884744 | tf_op jit(solution)/shard_map/ppermute | solution.py:37
  248.4 9.3 %collective-permute-start.45 = (bf16[48,1536]{1,0:T(8,128)(2,1)S(1)}, bf16[48,1536]{1,0:T(8,128)(2,1)S(1)}, u32[]{:S(2)}, u32[]{:S(2)}) collective-permute-start(bf16[48,1536]{1,0:T(8,128)(2,1)S(1)} %slice.395), channel_id=1, source_target_pairs={{0,24},{1,25},{2,26},{3,27},{4,28},{5,29},{6,30},{7,31},{8,16},{9,... | collective-permute-start | bytes 442376 | tf_op jit(solution)/shard_map/ppermute | solution.py:37
  254.0 6.8 %collective-permute-start.40 = (bf16[48,1536]{1,0:T(8,128)(2,1)S(1)}, bf16[48,1536]{1,0:T(8,128)(2,1)S(1)}, u32[]{:S(2)}, u32[]{:S(2)}) collective-permute-start(bf16[48,1536]{1,0:T(8,128)(2,1)S(1)} %slice.396), channel_id=1, source_target_pairs={{0,8},{1,9},{2,10},{3,11},{4,12},{5,13},{6,14},{7,15},{8,0},{9,1},... | collective-permute-start | bytes 442376 | tf_op jit(solution)/shard_map/ppermute | solution.py:37
  257.7 4.9 %collective-permute-start.46 = (bf16[24,1536]{1,0:T(8,128)(2,1)S(1)}, bf16[24,1536]{1,0:T(8,128)(2,1)S(1)}, u32[]{:S(2)}, u32[]{:S(2)}) collective-permute-start(bf16[24,1536]{1,0:T(8,128)(2,1)S(1)} %slice.400), channel_id=1, source_target_pairs={{0,8},{1,9},{2,10},{3,11},{4,12},{5,13},{6,14},{7,15},{8,0},{9,1},... | collective-permute-start | bytes 221192 | tf_op jit(solution)/shard_map/ppermute | solution.py:37
  260.9 4.4 %collective-permute-start.41 = (bf16[24,1536]{1,0:T(8,128)(2,1)S(1)}, bf16[24,1536]{1,0:T(8,128)(2,1)S(1)}, u32[]{:S(2)}, u32[]{:S(2)}) collective-permute-start(bf16[24,1536]{1,0:T(8,128)(2,1)S(1)} %slice.401), channel_id=1, source_target_pairs={{0,4},{1,5},{2,6},{3,7},{4,0},{5,1},{6,2},{7,3},{8,12},{9,13},{10,... | collective-permute-start | bytes 221192 | tf_op jit(solution)/shard_map/ppermute | solution.py:37
  (7 other events, 10.7 us)

commit v2 on v1

--- a/solution.py
+++ b/solution.py
@@ -1,3 +1,4 @@
+import functools
 import math
 
 import jax
@@ -488,34 +489,29 @@
     cot,
     gain,
     src_b,
-    src_g,
-    src_u,
+    src_n,
+    tall_g,
+    tall_u,
     wb0,
     wb1,
-    wg0,
-    wg1,
-    wu0,
-    wu1,
-    wd0,
-    wd1,
+    wgu,
+    wd,
     mixed_out,
     res_out,
     dgate,
     dup,
-    dg_out,
-    du_out,
-    dd_out,
-    wd,
+    dg_low,
+    du_low,
+    dd_low,
+    dg_high,
+    du_high,
+    dd_high,
     act,
-    wide_g,
-    wide_u,
+    wide_n,
+    dd,
 ):
     count = slots.shape[0]
     rows_d = FF // count
-    for p in range(count):
-        half, at = (wd0, p) if p < count // 2 else (wd1, p - count // 2)
-        target = pl.multiple_of(slots[p] * rows_d, rows_d)
-        wd[pl.ds(target, rows_d), :] = half[at * rows_d : (at + 1) * rows_d, :]
     wb = jnp.concatenate([wb0[...], wb1[...]], axis=0)
     cot_tok = cot[...].T
     att_wide = dot_nn(att[...].T, spread_wide(src_b[...])).astype(bf16)
@@ -523,14 +519,15 @@
     res_out[...] = residual
     inverse = lax.rsqrt(jnp.mean(residual * residual, axis=-1, keepdims=True) + norm_epsilon)
     normed = (residual * inverse * gain[...]).astype(bf16)
-    wide_g[...] = dot_nn(normed, spread_wide(src_g[...])).astype(bf16)
-    wide_u[...] = dot_nn(normed, spread_wide(src_u[...])).astype(bf16)
+    wide_n[...] = dot_nn(normed, spread_wide(src_n[...])).astype(bf16)
+    normed_t = normed.T
     block = 256
 
     def ff_step(j, carry):
         cut = pl.ds(pl.multiple_of(j * block, block), block)
-        gate = dot_nn(wide_g[...], jnp.concatenate([wg0[:, cut], wg1[:, cut]], axis=0))
-        up = dot_nn(wide_u[...], jnp.concatenate([wu0[:, cut], wu1[:, cut]], axis=0))
+        cut_up = pl.ds(pl.multiple_of(j * block + FF, block), block)
+        gate = dot_nn(wide_n[...], wgu[:, cut])
+        up = dot_nn(wide_n[...], wgu[:, cut_up])
         grad_act = dot_nt(cot_tok, wd[cut, :])
         sig = jax.nn.sigmoid(gate)
         silu = gate * sig
@@ -542,12 +539,16 @@
     lax.fori_loop(0, FF // block, ff_step, 0)
     mixed = residual + dot_nn(act[...], wd[...])
     mixed_out[...] = mixed.T.astype(bf16)
-    dg_out[...] = dot_nn(wide_g[...].T, dgate[...]).astype(bf16)
-    du_out[...] = dot_nn(wide_u[...].T, dup[...]).astype(bf16)
-    wd[...] = dot_nn(act[...].T, cot_tok).astype(bf16)
+    for tall, grad, low, high in ((tall_g, dgate, dg_low, dg_high), (tall_u, dup, du_low, du_high)):
+        wide_t = dot_nn(spread_tall(tall[...]), normed_t).astype(bf16)
+        half = wide_t.shape[0] // 2
+        low[...] = dot_nn(wide_t[:half], grad[...]).astype(bf16)
+        high[...] = dot_nn(wide_t[half:], grad[...]).astype(bf16)
+    dd[...] = dot_nn(act[...].T, cot_tok).astype(bf16)
     for p in range(count):
         source = pl.multiple_of(slots[p] * rows_d, rows_d)
-        dd_out[p * rows_d : (p + 1) * rows_d, :] = wd[pl.ds(source, rows_d), :]
+        out, at = (dd_low, p) if p < count // 2 else (dd_high, p - count // 2)
+        out[at * rows_d : (at + 1) * rows_d, :] = dd[pl.ds(source, rows_d), :]
 
 
 def feed_back_kernel(
@@ -555,30 +556,22 @@
     cot,
     gain,
     src_b,
-    src_g,
-    src_u,
+    src_n,
     dgate,
     dup,
     wb0,
     wb1,
-    wg0,
-    wg1,
-    wu0,
-    wu1,
+    wgu,
     gres_out,
     gatt_out,
     dgain_out,
 ):
     residual = residual_in[...]
     spread_b = spread_wide(src_b[...])
-    spread_g = spread_wide(src_g[...])
-    spread_u = spread_wide(src_u[...])
+    spread_n = spread_wide(src_n[...])
     inverse = lax.rsqrt(jnp.mean(residual * residual, axis=-1, keepdims=True) + norm_epsilon)
-    dn_g = dot_nt(dgate[...], jnp.concatenate([wg0[...], wg1[...]], axis=0))
-    dn_u = dot_nt(dup[...], jnp.concatenate([wu0[...], wu1[...]], axis=0))
-    grad_normed = sum(dot_nt(part, spread_g) for part in split_two(dn_g)) + sum(
-        dot_nt(part, spread_u) for part in split_two(dn_u)
-    )
+    dn = dot_nt(dgate[...], wgu[:, :FF]) + dot_nt(dup[...], wgu[:, FF:])
+    grad_normed = sum(dot_nt(part, spread_n) for part in split_two(dn))
     unit = residual * inverse
     scaled = grad_normed * gain[...]
     dgain_out[...] = jnp.sum(grad_normed * unit, axis=0, keepdims=True)
@@ -611,8 +604,10 @@
     wb0,
     wb1,
     dtok_out,
-    da_out,
-    db_out,
+    da_low,
+    db_low,
+    da_high,
+    db_high,
 ):
     x = tok[...].astype(f32)
     inverse = lax.rsqrt(jnp.mean(x * x, axis=0, keepdims=True) + norm_epsilon)
@@ -651,13 +646,26 @@
     wide_a = dot_nn(spread_tall(tall_a[...]), normed).astype(bf16)
     wide_b = dot_nn(tall_spread_b, normed).astype(bf16)
     wide_att = dot_nn(tall_spread_b, att[...]).astype(bf16)
-    extra_a = tall_a[...] < 0
-    extra_b = tall_b[...] < 0
     fill_a = jnp.concatenate([dgain, jnp.zeros((1, KVH * HD), f32)], axis=1)
-    da_out[...] = jnp.where(extra_a, fill_a, dot_nt(wide_a, dqk)).astype(bf16)
-    d_out = dot_nt(wide_att, gres[...].astype(bf16))
-    db_out[:, :D] = jnp.where(extra_b, dgain_ffn[...], d_out).astype(bf16)
-    db_out[:, D:] = dot_nt(wide_b, dv).astype(bf16)
+    gres_b = gres[...].astype(bf16)
+    half = wide_a.shape[0] // 2
+    for cut, da_out, db_out in ((slice(0, half), da_low, db_low), (slice(half, None), da_high, db_high)):
+        da_out[...] = jnp.where(tall_a[cut] < 0, fill_a, dot_nt(wide_a[cut], dqk)).astype(bf16)
+        d_out = dot_nt(wide_att[cut], gres_b)
+        db_out[:, :D] = jnp.where(tall_b[cut] < 0, dgain_ffn[...], d_out).astype(bf16)
+        db_out[:, D:] = dot_nt(wide_b[cut], dv).astype(bf16)
+
+
+def merge_kernel(streams, final, *refs):
+    kept, got, outs = refs[:streams], refs[streams : 2 * streams], refs[2 * streams :]
+    for i in range(streams):
+        total = kept[i][...].astype(f32) + got[i][...].astype(f32)
+        if final:
+            outs[i][...] = total
+        else:
+            half = total.shape[0] // 2
+            outs[i][...] = total[:half].astype(bf16)
+            outs[streams + i][...] = total[half:].astype(bf16)
 
 
 def call_whole(kernel, outs, operands, scratch=(), scalars=()):
@@ -684,21 +692,26 @@
     return [jnp.concatenate([h, g], axis=0) for h, g in zip(held, got)]
 
 
-def step_halve(held, orders, t, even=False):
-    halves = [h.shape[0] // 2 for h in held]
-    out = []
-    for h, k, order in zip(held, halves, orders):
-        g = swapped(h[k:].astype(bf16), order[-1 - t])
-        kept = h[:k].astype(f32)
-        if even:
-            kept = lax.reduce_precision(kept, 8, 7)
-        out.append(kept + g.astype(f32))
-    return out
-
-
-def sources(order, per_slot):
+def step_halve(pair, orders, t):
+    kept, send = pair
+    streams = len(kept)
+    got = []
+    for value, order in zip(send, orders):
+        got.append(swapped(value, order[-1 - t]))
+    final = t == len(orders[0]) - 1
+    if final:
+        outs = [(k.shape, f32) for k in kept]
+    else:
+        outs = [((k.shape[0] // 2, k.shape[1]), bf16) for k in kept] * 2
+    merged = call_whole(functools.partial(merge_kernel, streams, final), outs, list(kept) + got)
+    return merged if final else (merged[:streams], merged[streams:])
+
+
+def sources(order, count, per_slot):
     me = lax.axis_index("dev")
-    owner = me ^ jnp.asarray(slot_masks(order), jnp.int32)
+    owner = jnp.arange(count, dtype=jnp.int32)
+    if order is not None:
+        owner = me ^ jnp.asarray(slot_masks(order), jnp.int32)
     inner = jnp.arange(PAD, dtype=jnp.int32)[None, :]
     value = jnp.where(inner < per_slot, owner[:, None] * per_slot + inner, -1)
     return value.reshape(-1)
@@ -720,11 +733,16 @@
     order_of = [rest[k:] + rest[:k] + [first] for k in range(len(rest))]
     ord_a, ord_b = order_of[0], order_of[2]
     ord_g, ord_u, ord_d = order_of[1], order_of[2], order_of[3]
-    src_a, src_b = sources(ord_a, per), sources(ord_b, per)
-    src_g, src_u = sources(ord_g, per), sources(ord_u, per)
+    src_a, src_b = sources(ord_a, count, per), sources(ord_b, count, per)
+    src_n = sources(None, count, per)
+    src_g, src_u = sources(ord_g, count, per), sources(ord_u, count, per)
     slots = me ^ jnp.asarray(slot_masks(ord_d), jnp.int32)
     w_qs, w_kvs = w_query.reshape(per, H * HD), w_kv.reshape(per, 2 * KVH * HD)
     kv_cut = KVH * HD
+    stream_gu = padded_rows(w_gate_up.reshape(per, 2 * FF))
+    stream_d = w_down.reshape(per_d, D)
+    wgu = lax.all_gather(stream_gu, "dev", axis=0, tiled=True)
+    wd = lax.all_gather(stream_d, "dev", axis=0, tiled=True)
     stream_a = padded_rows(jnp.concatenate([w_qs, w_kvs[:, :kv_cut]], axis=1))
     stream_b = padded_rows(jnp.concatenate([w_out.reshape(per, D), w_kvs[:, kv_cut:]], axis=1))
     half_dim = HD // 2
@@ -737,35 +755,21 @@
     steps = len(ord_a)
     hold = lax.optimization_barrier
     held = [stream_a, stream_b]
-    ffn = None
     early = (src_a[None], src_b[None], src_a[:, None], src_b[:, None])
-    early = early + (src_g[None], src_u[None], slots, cos, sin, gain_col)
+    early = early + (src_n[None], src_g[:, None], src_u[:, None], slots, cos, sin, gain_col)
     for t in range(steps):
         if t == 2:
-            held, w_gate_up, w_down = hold((held, w_gate_up, w_down))
-            w_gs = w_gate_up.reshape(per, 2 * FF)
-            ffn = [padded_rows(w_gs[:, :FF]), padded_rows(w_gs[:, FF:]), w_down.reshape(per_d, D)]
-        if t == 3:
             held, early = hold((held, early))
         got = step_double(held, orders_ab, t)
         if t < steps - 1:
             held = joined(held, got)
-        if t >= 2:
-            ffn = joined(ffn, step_double(ffn, orders_gud, t - 2))
-        if t == 3:
-            held, ffn = hold((held, ffn))
     (wa0, wb0), (wa1, wb1) = held, got
-    row_a, row_b, tall_a, tall_b, row_g, row_u, slots, cos, sin, gain_col = early
+    row_a, row_b, tall_a, tall_b, row_n, tall_g, tall_u, slots, cos, sin, gain_col = early
     q_t, kv_t = call_whole(
         project_kernel,
         [((H * HD, row_count), bf16), ((2 * kv_cut, row_count), bf16)],
         [tok_t, gain_col, cos, sin, row_a, row_b, wa0, wa1, wb0, wb1],
     )
-    for t in range(steps - 2, steps):
-        got = step_double(ffn, orders_gud, t)
-        if t < steps - 1:
-            ffn = joined(ffn, got)
-    (wg0, wu0, wd0), (wg1, wu1, wd1) = ffn, got
     near = passed_along(kv_t, "dev", 1)
     chunks = row_count // CHUNK
     prob, att_t = call_whole(
@@ -777,33 +781,28 @@
         [q_t, near, kv_t, positions[None]],
     )
     wide = count * PAD
-    mixed_t, residual, dgate, dup, dg, du, dd = call_whole(
+    mixed_t, residual, dgate, dup, *sums = call_whole(
         feed_kernel,
         [
             ((D, row_count), bf16),
             ((row_count, D), f32),
             ((row_count, FF), bf16),
             ((row_count, FF), bf16),
-            ((wide, FF), bf16),
-            ((wide, FF), bf16),
-            ((FF, D), bf16),
-        ],
-        [att_t, tok_t, cot_t, gain_ffn[None], row_b, row_g, row_u]
-        + [wb0, wb1, wg0, wg1, wu0, wu1, wd0, wd1],
+        ]
+        + [((wide // 2, FF), bf16), ((wide // 2, FF), bf16), ((FF // 2, D), bf16)] * 2,
+        [att_t, tok_t, cot_t, gain_ffn[None], row_b, row_n, tall_g, tall_u, wb0, wb1, wgu, wd],
         scratch=[
-            pltpu.VMEM((FF, D), bf16),
             pltpu.VMEM((row_count, FF), bf16),
             pltpu.VMEM((row_count, wide), bf16),
-            pltpu.VMEM((row_count, wide), bf16),
+            pltpu.VMEM((FF, D), bf16),
         ],
         scalars=[slots],
     )
-    sums = [dg, du, dd]
+    sums = (sums[:3], sums[3:])
     gres_t, gatt_t, dgain_ffn = call_whole(
         feed_back_kernel,
         [((D, row_count), f32), ((H * HD, row_count), bf16), ((1, D), f32)],
-        [residual, cot_t, gain_ffn[None], row_b, row_g, row_u, dgate, dup]
-        + [wb0, wb1, wg0, wg1, wu0, wu1],
+        [residual, cot_t, gain_ffn[None], row_b, row_n, dgate, dup, wb0, wb1, wgu],
     )
     for t in range(3):
         sums = step_halve(sums, orders_gud, t)
@@ -818,21 +817,21 @@
         scratch=[pltpu.VMEM((HD, 2 * row_count), f32)] * 2,
     )
     back = passed_along(dnear, "dev", -1)
-    dtok_t, da, db = call_whole(
+    dtok_t, *last = call_whole(
         finish_kernel,
         [
             ((D, row_count), f32),
-            ((wide, H * HD + kv_cut), bf16),
-            ((wide, D + kv_cut), bf16),
-        ],
+        ]
+        + [((wide // 2, H * HD + kv_cut), bf16), ((wide // 2, D + kv_cut), bf16)] * 2,
         [dq_t, down, back, tok_t, gain_col, cos, sin, gres_t, att_t, dgain_ffn]
         + [row_a, row_b, tall_a, tall_b, wa0, wa1, wb0, wb1],
     )
-    last = [da, db]
+    last = (last[:2], last[2:])
     for t in range(steps):
-        last = step_halve(last, orders_ab, t, even=True)
+        last = step_halve(last, orders_ab, t)
         if t + 3 < steps:
             sums = step_halve(sums, orders_gud, t + 3)
+            last, sums = hold((last, sums))
     share_g, share_u, share_d = sums
     share_a, share_b = last
     share_kv = jnp.concatenate([share_a[:per, H * HD :], share_b[:per, D:]], axis=1)

time: 272 us -> 317 us (1.17)
  waiting for transfers between devices: 64.7 us -> 117 us
  starting transfers between devices: 82.7 us -> 51.9 us
  Pallas kernels: 64.1 us -> 88.7 us
  other arithmetic: 17 us -> 1.88 us
  between operations: 1.52 us -> 14.8 us
    all_gather x0 -> x2, waiting for transfers between devices: none -> 69.4 us  [the longest x1 65.5 us: shards(): wgu = lax.all_gather(stream_gu, 'dev', axis=0, tiled=True)]
    ppermute x50 -> x35, starting transfers between devices: 79.1 us -> 48 us  [swapped(): return lax.ppermute(value, 'dev', [(i, i ^ mask) for i in range(count)])]
    pallas_call x6 -> x16, Pallas kernels: 64.1 us -> 88.7 us  [call_whole(): pl.pallas_call(kernel, out_shape=[jax.ShapeDtypeStruct(s, d) for s, d in...]
    ppermute x50 -> x35, waiting for transfers between devices: 61.7 us -> 46.9 us  [swapped(): return lax.ppermute(value, 'dev', [(i, i ^ mask) for i in range(count)])]
    add x25 -> x0, other arithmetic: 11.3 us -> none  [step_halve(): out.append(kept + g.astype(f32))]
    slice x29 -> x0, local copies, waits for them, and re-layouts: 9.67 us -> none  [the longest x26 9.64 us: step_halve(): g = swapped(h[k:].astype(bf16), order[-1 - t])]
    unnamed x44 -> x86, local copies, waits for them, and re-layouts: 5.52 us -> 12 us
  transfers between devices with their start and end apart: 52 -> 39, of which waited for: 20 -> 19; matrix products, arithmetic and copies ran while one was open for 17% -> 6% of each run, Pallas kernels for 6% -> 18%
where the time goes in v2:
time: 317 us; the launch traced here: 313 us
  waiting for transfers between devices  117 us (37%)
  Pallas kernels  88.7 us (28%)
  starting transfers between devices  51.9 us (16%)
  local copies, waits for them, and re-layouts  39.1 us (12%)
  between operations  14.8 us (5%)
    pallas_call x16, Pallas kernels, call_whole(): pl.pallas_call(kernel, out_shape=[jax.ShapeDtypeStruct(s, d) for s, d in...  88.7 us
    all_gather x1, waiting for transfers between devices, shards(): wgu = lax.all_gather(stream_gu, 'dev', axis=0, tiled=True)  65.5 us
    ppermute x35, starting transfers between devices, swapped(): return lax.ppermute(value, 'dev', [(i, i ^ mask) for i in range(count)])  48 us
    ppermute x35, waiting for transfers between devices, swapped(): return lax.ppermute(value, 'dev', [(i, i ^ mask) for i in range(count)])  46.9 us
    unnamed x86, local copies, waits for them, and re-layouts  12 us
  transfers between devices with their start and end apart: 39, of which 19 were waited for; matrix products, arithmetic and copies ran while one was open for 6% of the time, Pallas kernels for 18%

profile of v2, /device:TPU:0, one launch (start us, length us, event | category | flops | bytes accessed | tf_op | source)
XLA Modules:
  0.0 312.9 jit_solution(7843679182948488366)
XLA Ops:
  7.3 1.5 reshape.332
  8.9 1.0 reshape.331
  12.3 3.0 collective-permute-start
  16.2 1.6 collective-permute-start.2
  21.7 1.6 collective-permute-start.1
  23.3 2.5 collective-permute-start.3
  26.5 3.0 collective-permute-done.3
  30.6 4.4 %collective-permute-done.4 = bf16[96,768]{1,0:T(8,128)(2,1)S(1)} collective-permute-done((bf16[96,768]{1,0:T(8,128)(2,1)S(1)}, bf16[96,768]{1,0:T(8,128)(2,1)S(1)}, u32[]{:S(2)}, u32[]{:S(2)}) %collective-permute-start.4) | collective-permute-done | bytes 147488 | tf_op jit(solution)/shard_map/ppermute | solution.py:38
  35.0 2.6 collective-permute-start.5
  38.2 5.5 %collective-permute-done.5 = bf16[192,768]{1,0:T(8,128)(2,1)S(1)} collective-permute-done((bf16[192,768]{1,0:T(8,128)(2,1)S(1)}, bf16[192,768]{1,0:T(8,128)(2,1)S(1)}, u32[]{:S(2)}, u32[]{:S(2)}) %collective-permute-start.5) | collective-permute-done | bytes 294944 | tf_op jit(solution)/shard_map/ppermute | solution.py:38
  43.8 1.4 collective-permute-done.8
  46.2 1.1 collective-permute-done.9.wb1
  48.1 4.7 %shard_map.214 = (bf16[576,384]{1,0:T(8,128)(2,1)}, bf16[384,384]{1,0:T(8,128)(2,1)}) custom-call(bf16[576,384]{1,0:T(8,128)(2,1)} %bitcast.6, f32[576,1]{1,0:T(8,128)} %copy.30.gain, f32[32,384]{1,0:T(8,128)} %get-tuple-element.111.cos, f32[32,384]{1,0:T(8,128)} %get-tuple-element.112.sin, s32[1,768]{1,0:T(1,128)} %select_n.87.src_a, ...), custom_call_target="tpu_custom_call" | custom-call | tf_op jit(solution)/shard_map/pallas_call | solution.py:674
  52.8 2.3 collective-permute-start.10
  58.9 12.3 %shard_map.215 = (bf16[3,3,512,384]{3,2,1,0:T(8,128)(2,1)}, bf16[576,384]{1,0:T(8,128)(2,1)}) custom-call(bf16[576,384]{1,0:T(8,128)(2,1)} %get-tuple-element.117.q, bf16[384,384]{1,0:T(8,128)(2,1)} %copy-done.6, bf16[384,384]{1,0:T(8,128)(2,1)} %get-tuple-element.118.own, s32[1,384]{1,0:T(1,128)} %broadcast_in_dim.57.pos), custom_call_target="tpu_custom_call" | custom-call | tf_op jit(solution)/shard_map/pallas_call | solution.py:674
  71.3 3.9 %all-gather.5.cloned.1.call-done.wd = bf16[1536,576]{1,0:T(8,128)(2,1)} async-done(((bf16[48,576]{1,0:T(8,128)(2,1)}), bf16[1536,576]{1,0:T(8,128)(2,1)}) %all-gather.5.cloned.1.call-update) | async-done | bytes 1769488 | tf_op jit(solution)/shard_map/all_gather | solution.py:745
  75.1 65.5 %all-gather.3.cloned.1.call-done.wgu = bf16[768,3072]{1,0:T(8,128)(2,1)} async-done(((bf16[24,3072]{1,0:T(8,128)(2,1)}), bf16[768,3072]{1,0:T(8,128)(2,1)}) %all-gather.3.cloned.1.call-update) | async-done | bytes 4718608 | tf_op jit(solution)/shard_map/all_gather | solution.py:744
  140.7 18.3 %shard_map.216 = (bf16[576,384]{1,0:T(8,128)(2,1)}, f32[384,576]{1,0:T(8,128)}, bf16[384,1536]{1,0:T(8,128)(2,1)}, bf16[384,1536]{1,0:T(8,128)(2,1)}, bf16[384,1...) custom-call(s32[32]{0:T(128)} %broadcast_xor_fusion.slots, ...), custom_call_target="tpu_custom_call" | custom-call | tf_op jit(solution)/shard_map/pallas_call | solution.py:674
  159.5 1.5 copy.36
  161.3 3.8 %collective-permute-done.16 = bf16[768,576]{0,1:T(8,128)(2,1)} collective-permute-done((bf16[768,576]{0,1:T(8,128)(2,1)S(1)}, bf16[768,576]{0,1:T(8,128)(2,1)}, u32[]{:S(2)}, u32[]{:S(2)}) %collective-permute-start.16) | collective-permute-done | bytes 884768 | tf_op jit(solution)/shard_map/ppermute | solution.py:38
  165.1 2.4 copy.37.refs_5_
  167.6 1.0 copy-done.4
  168.9 4.8 %shard_map.221 = (bf16[192,1536]{1,0:T(8,128)(2,1)}, bf16[192,1536]{1,0:T(8,128)(2,1)}, bf16[384,576]{1,0:T(8,128)(2,1)}, bf16[192,1536]{1,0:T(8,128)(2,1)}, bf1...) custom-call(bf16[384,1536]{1,0:T(8,128)(2,1)} %get-tuple-element.145.refs_0_, ...), custom_call_target="tpu_custom_call" | custom-call | tf_op jit(solution)/shard_map/pallas_call | solution.py:674
  173.7 1.4 collective-permute-start.17
  175.7 10.9 %shard_map.217 = (f32[576,384]{1,0:T(8,128)}, bf16[576,384]{1,0:T(8,128)(2,1)}, f32[1,576]{1,0:T(1,128)}) custom-call(f32[384,576]{1,0:T(8,128)} %get-tuple-element.125.residual_in, bf16[576,384]{1,0:T(8,128)(2,1)} %bitcast.10, f32[1,576]{1,0:T(1,128)} %broadcast_in_dim.58.gain, s32[1,768]{1,0:T(1,128)} %select_n.89.src_b, s32[1,768]{1,0:T(1,128)} %select_n.93.src_n, ...), custom_call_target="tpu_custom_call" | custom-call | tf_op jit(solution)/shard_map/pallas_call | solution.py:674
  186.6 1.4 collective-permute-start.19
  188.0 8.3 %shard_map.218 = (bf16[576,384]{1,0:T(8,128)(2,1)}, bf16[384,384]{1,0:T(8,128)(2,1)}, f32[384,384]{1,0:T(8,128)}) custom-call(bf16[576,384]{1,0:T(8,128)(2,1)} %get-tuple-element.117.q, bf16[384,384]{1,0:T(8,128)(2,1)} %copy-done.6, bf16[384,384]{1,0:T(8,128)(2,1)} %get-tuple-element.118.own, bf16[3,3,512,384]{3,2,1,0:T(8,128)(2,1)} %get-tuple-element.124.prob, ...), custom_call_target="tpu_custom_call" | custom-call | tf_op jit(solution)/shard_map/pallas_call | solution.py:674
  196.4 1.5 collective-permute-start.11
  197.9 1.0 copy.34.tall_a
  200.8 10.3 %shard_map.219 = (f32[576,384]{1,0:T(8,128)}, bf16[384,768]{1,0:T(8,128)(2,1)}, bf16[384,768]{1,0:T(8,128)(2,1)}, bf16[384,768]{1,0:T(8,128)(2,1)}, bf16[384,768]{1,0:T(8,128)(2,1)}) custom-call(bf16[576,384]{1,0:T(8,128)(2,1)} %get-tuple-element.129.dq, f32[384,384]{1,0:T(8,128)} %get-tuple-element.130.own, bf16[384,384]{1,0:T(8,128)(2,1)} %copy-done.16, ...), custom_call_target="tpu_custom_call" | custom-call | tf_op jit(solution)/shard_map/pallas_call | solution.py:674
  211.1 4.4 %collective-permute-start.12 = (bf16[384,768]{1,0:T(8,128)(2,1)}, bf16[384,768]{1,0:T(8,128)(2,1)S(1)}, u32[]{:S(2)}, u32[]{:S(2)}) collective-permute-start(bf16[384,768]{1,0:T(8,128)(2,1)} %get-tuple-element.139), channel_id=1, source_target_pairs={{0,1},{1,0},{2,3},{3,2},{4,5},{5,4},{6,7},{7,6},{8,9},{9,8},{10,11... | collective-permute-start | bytes 1769480 | tf_op jit(solution)/shard_map/ppermute | solution.py:38
  216.7 3.1 %shard_map.222 = (bf16[96,1536]{1,0:T(8,128)(2,1)}, bf16[96,1536]{1,0:T(8,128)(2,1)}, bf16[192,576]{1,0:T(8,128)(2,1)}, bf16[96,1536]{1,0:T(8,128)(2,1)}, bf16[9...) custom-call(bf16[192,1536]{1,0:T(8,128)(2,1)} %get-tuple-element.151.refs_0_, bf16[192,1536]{1,0:T(8,128)(2,1)} %get-tuple-element.152.refs_1_, ...), custom_call_target="tpu_custom_call" | custom-call | tf_op jit(solution)/shard_map/pallas_call | solution.py:674
  219.9 1.7 collective-permute-start.20
  221.6 1.9 collective-permute-start.21
  223.5 7.9 %collective-permute-done.22.refs_5_ = bf16[192,576]{1,0:T(8,128)(2,1)S(1)} collective-permute-done((bf16[192,576]{1,0:T(8,128)(2,1)}, bf16[192,576]{1,0:T(8,128)(2,1)S(1)}, u32[]{:S(2)}, u32[]{:S(2)}) %collective-permute-start.22) | collective-permute-done | bytes 221216 | tf_op jit(solution)/shard_map/ppermute | solution.py:38
  232.4 2.3 shard_map.223
  234.7 4.8 %collective-permute-start.23 = (bf16[48,1536]{1,0:T(8,128)(2,1)}, bf16[48,1536]{1,0:T(8,128)(2,1)S(1)}, u32[]{:S(2)}, u32[]{:S(2)}) collective-permute-start(bf16[48,1536]{1,0:T(8,128)(2,1)} %get-tuple-element.166), channel_id=1, source_target_pairs={{0,8},{1,9},{2,10},{3,11},{4,12},{5,13},{6,14},{7,15},{8,0},{9,1},... | collective-permute-start | bytes 442376 | tf_op jit(solution)/shard_map/ppermute | solution.py:38
  239.5 1.6 collective-permute-start.24
  241.1 1.9 collective-permute-start.25
  244.1 2.7 shard_map.220
  246.8 1.0 collective-permute-done.24.refs_4_
  248.5 2.0 shard_map.224
  250.5 2.1 collective-permute-start.26
  252.6 1.1 collective-permute-start.27
  253.6 0.9 collective-permute-start.28
  254.6 1.7 collective-permute-start.30
  256.3 6.9 %collective-permute-done.30.refs_5_ = bf16[48,576]{1,0:T(8,128)(2,1)S(1)} collective-permute-done((bf16[48,576]{1,0:T(8,128)(2,1)}, bf16[48,576]{1,0:T(8,128)(2,1)S(1)}, u32[]{:S(2)}, u32[]{:S(2)}) %collective-permute-start.30) | collective-permute-done | bytes 55328 | tf_op jit(solution)/shard_map/ppermute | solution.py:38
  264.5 1.8 shard_map.226
  267.8 2.1 shard_map.225
  269.8 2.6 collective-permute-start.31
  272.4 1.2 collective-permute-start.32
  273.6 2.2 collective-permute-done.31.refs_2_
  275.8 2.0 collective-permute-done.32.refs_3_
  278.4 1.9 shard_map.227
  280.3 1.5 collective-permute-start.33
  281.8 2.1 collective-permute-start.34
  284.8 3.3 %collective-permute-done.34.refs_3_ = bf16[48,768]{1,0:T(8,128)(2,1)S(1)} collective-permute-done((bf16[48,768]{1,0:T(8,128)(2,1)}, bf16[48,768]{1,0:T(8,128)(2,1)S(1)}, u32[]{:S(2)}, u32[]{:S(2)}) %collective-permute-start.34) | collective-permute-done | bytes 73760 | tf_op jit(solution)/shard_map/ppermute | solution.py:38
  288.8 1.7 shard_map.228
  290.4 1.1 collective-permute-start.35
  293.1 1.5 collective-permute-done.35.refs_2_
  294.6 1.1 collective-permute-done.36.refs_3_
  296.3 1.5 shard_map.229
  297.8 1.3 slice_reduce_fusion.1
  302.5 1.3 slice_reduce_fusion
  (172 shorter events, 35.0 us)
Async XLA Ops:
  7.2 10.6 %copy-start.38 = (s32[32]{0:T(128)S(1)}, s32[32]{0:T(128)}, u32[]{:S(2)}) copy-start(s32[32]{0:T(128)} %constant.22.clone) | copy-start | bytes 388
  7.2 10.6 %copy-start.36 = (s32[32]{0:T(128)S(1)}, s32[32]{0:T(128)}, u32[]{:S(2)}) copy-start(s32[32]{0:T(128)} %constant.24.clone) | copy-start | bytes 388
  7.2 10.6 %copy-start.37 = (s32[32]{0:T(128)S(1)}, s32[32]{0:T(128)}, u32[]{:S(2)}) copy-start(s32[32]{0:T(128)} %constant.23.clone) | copy-start | bytes 388
  7.2 11.6 %copy-start.40 = (s32[32]{0:T(128)S(1)}, s32[32]{0:T(128)}, u32[]{:S(2)}) copy-start(s32[32]{0:T(128)} %constant.25.clone) | copy-start | bytes 388
  7.2 10.5 %copy-start.33 = (s32[384]{0:T(512)S(1)}, s32[384]{0:T(512)}, u32[]{:S(2)}) copy-start(s32[384]{0:T(512)} %param.16) | copy-start | bytes 4612
  7.2 14.4 %copy-start.34 = (f32[576]{0:T(1024)S(1)}, f32[576]{0:T(1024)}, u32[]{:S(2)}) copy-start(f32[576]{0:T(1024)} %param.17) | copy-start | bytes 6916
  7.2 67.9 %all-gather.5.cloned.1.call-start = ((), (), s32[]{:S(2)}) async-start(), calls=%async_computation.1 | async-start | bytes 2027520 | tf_op jit(solution)/shard_map/all_gather | solution.py:745
  8.9 131.8 %all-gather.3.cloned.1.call-start = ((), (), s32[]{:S(2)}) async-start(), calls=%async_computation | async-start | bytes 4866048 | tf_op jit(solution)/shard_map/all_gather | solution.py:744
  12.3 9.4 %collective-permute-start = (bf16[24,768]{1,0:T(8,128)(2,1)S(1)}, bf16[24,768]{1,0:T(8,128)(2,1)S(1)}, u32[]{:S(2)}, u32[]{:S(2)}) collective-permute-start(bf16[24,768]{1,0:T(8,128)(2,1)S(1)} %fusion.4), channel_id=1, source_target_pairs={{0,2},{1,3},{2,0},{3,1},{4,6},{5,7},{6,4},{7,5},{8,10},{9,11},{10,... | collective-permute-start | bytes 110600 | tf_op jit(solution)/shard_map/ppermute | solution.py:38
  16.2 7.1 %collective-permute-start.2 = (bf16[24,768]{1,0:T(8,128)(2,1)S(1)}, bf16[24,768]{1,0:T(8,128)(2,1)S(1)}, u32[]{:S(2)}, u32[]{:S(2)}) collective-permute-start(bf16[24,768]{1,0:T(8,128)(2,1)S(1)} %fusion.5), channel_id=1, source_target_pairs={{0,8},{1,9},{2,10},{3,11},{4,12},{5,13},{6,14},{7,15},{8,0},{9,1},... | collective-permute-start | bytes 110600 | tf_op jit(solution)/shard_map/ppermute | solution.py:38
  21.7 4.8 %collective-permute-start.1 = (bf16[48,768]{1,0:T(8,128)(2,1)S(1)}, bf16[48,768]{1,0:T(8,128)(2,1)S(1)}, u32[]{:S(2)}, u32[]{:S(2)}) collective-permute-start(bf16[48,768]{1,0:T(8,128)(2,1)S(1)} %pad_maximum_fusion.5), channel_id=1, source_target_pairs={{0,4},{1,5},{2,6},{3,7},{4,0},{5,1},{6,2},{7,3},{8,12},{9,13},{10,... | collective-permute-start | bytes 221192 | tf_op jit(solution)/shard_map/ppermute | solution.py:38
  23.3 6.3 %collective-permute-start.3 = (bf16[48,768]{1,0:T(8,128)(2,1)S(1)}, bf16[48,768]{1,0:T(8,128)(2,1)S(1)}, u32[]{:S(2)}, u32[]{:S(2)}) collective-permute-start(bf16[48,768]{1,0:T(8,128)(2,1)S(1)} %pad_maximum_fusion.6), channel_id=1, source_target_pairs={{0,24},{1,25},{2,26},{3,27},{4,28},{5,29},{6,30},{7,31},{8,16},{9,... | collective-permute-start | bytes 221192 | tf_op jit(solution)/shard_map/ppermute | solution.py:38
  29.6 5.4 %collective-permute-start.4 = (bf16[96,768]{1,0:T(8,128)(2,1)S(1)}, bf16[96,768]{1,0:T(8,128)(2,1)S(1)}, u32[]{:S(2)}, u32[]{:S(2)}) collective-permute-start(bf16[96,768]{1,0:T(8,128)(2,1)S(1)} %pad_maximum_fusion.3), channel_id=1, source_target_pairs={{0,8},{1,9},{2,10},{3,11},{4,12},{5,13},{6,14},{7,15},{8,0},{9,1},... | collective-permute-start | bytes 442376 | tf_op jit(solution)/shard_map/ppermute | solution.py:38
  29.7 8.0 %collective-permute-start.7 = (bf16[96,768]{1,0:T(8,128)(2,1)S(1)}, bf16[96,768]{1,0:T(8,128)(2,1)S(1)}, u32[]{:S(2)}, u32[]{:S(2)}) collective-permute-start(bf16[96,768]{1,0:T(8,128)(2,1)S(1)} %pad_maximum_fusion.4), channel_id=1, source_target_pairs={{0,2},{1,3},{2,0},{3,1},{4,6},{5,7},{6,4},{7,5},{8,10},{9,11},{10,... | collective-permute-start | bytes 442376 | tf_op jit(solution)/shard_map/ppermute | solution.py:38
  35.0 8.7 %collective-permute-start.5 = (bf16[192,768]{1,0:T(8,128)(2,1)S(1)}, bf16[192,768]{1,0:T(8,128)(2,1)S(1)}, u32[]{:S(2)}, u32[]{:S(2)}) collective-permute-start(bf16[192,768]{1,0:T(8,128)(2,1)S(1)} %pad_maximum_fusion), channel_id=1, source_target_pairs={{0,24},{1,25},{2,26},{3,27},{4,28},{5,29},{6,30},{7,31},{8,16},{9,... | collective-permute-start | bytes 884744 | tf_op jit(solution)/shard_map/ppermute | solution.py:38
  37.7 7.5 %collective-permute-start.8 = (bf16[192,768]{1,0:T(8,128)(2,1)S(1)}, bf16[192,768]{1,0:T(8,128)(2,1)S(1)}, u32[]{:S(2)}, u32[]{:S(2)}) collective-permute-start(bf16[192,768]{1,0:T(8,128)(2,1)S(1)} %pad_maximum_fusion.1), channel_id=1, source_target_pairs={{0,4},{1,5},{2,6},{3,7},{4,0},{5,1},{6,2},{7,3},{8,12},{9,13},{10,... | collective-permute-start | bytes 884744 | tf_op jit(solution)/shard_map/ppermute | solution.py:38
  43.7 3.6 %copy-start.2 = (bf16[384,768]{1,0:T(8,128)(2,1)}, bf16[384,768]{1,0:T(8,128)(2,1)S(1)}, u32[]{:S(2)}) copy-start(bf16[384,768]{1,0:T(8,128)(2,1)S(1)} %constant_dynamic-update-slice_fusion.wa0) | copy-start | bytes 1769476
  43.7 2.5 collective-permute-start.6
  45.2 2.1 copy-start
  45.2 2.1 collective-permute-start.9
  46.2 1.1 copy-start.3
  48.1 7.6 %copy-start.35 = (f32[576]{0:T(1024)S(1)}, f32[576]{0:T(1024)}, u32[]{:S(2)}) copy-start(f32[576]{0:T(1024)} %param.21) | copy-start | bytes 6916
  52.8 5.4 %collective-permute-start.10 = (bf16[384,384]{1,0:T(8,128)(2,1)}, bf16[384,384]{1,0:T(8,128)(2,1)S(1)}, u32[]{:S(2)}, u32[]{:S(2)}) collective-permute-start(bf16[384,384]{1,0:T(8,128)(2,1)} %get-tuple-element.118.own), channel_id=1, source_target_pairs={{0,1},{1,2},{2,3},{3,4},{4,5},{5,6},{6,7},{7,8},{8,9},{9,10},{10,1... | collective-permute-start | bytes 884744 | tf_op jit(solution)/shard_map/ppermute | solution.py:26
  159.0 8.5 %collective-permute-start.14 = (bf16[384,1536]{1,0:T(8,128)(2,1)}, bf16[384,1536]{1,0:T(8,128)(2,1)S(1)}, u32[]{:S(2)}, u32[]{:S(2)}) collective-permute-start(bf16[384,1536]{1,0:T(8,128)(2,1)} %get-tuple-element.148), channel_id=1, source_target_pairs={{0,1},{1,0},{2,3},{3,2},{4,5},{5,4},{6,7},{7,6},{8,9},{9,8},{10,11... | collective-permute-start | bytes 3538952 | tf_op jit(solution)/shard_map/ppermute | solution.py:38
  159.2 8.3 %collective-permute-start.15 = (bf16[384,1536]{1,0:T(8,128)(2,1)}, bf16[384,1536]{1,0:T(8,128)(2,1)S(1)}, u32[]{:S(2)}, u32[]{:S(2)}) collective-permute-start(bf16[384,1536]{1,0:T(8,128)(2,1)} %get-tuple-element.149), channel_id=1, source_target_pairs={{0,1},{1,0},{2,3},{3,2},{4,5},{5,4},{6,7},{7,6},{8,9},{9,8},{10,11... | collective-permute-start | bytes 3538952 | tf_op jit(solution)/shard_map/ppermute | solution.py:38
  161.0 4.1 %collective-permute-start.16 = (bf16[768,576]{0,1:T(8,128)(2,1)S(1)}, bf16[768,576]{0,1:T(8,128)(2,1)}, u32[]{:S(2)}, u32[]{:S(2)}) collective-permute-start(bf16[768,576]{0,1:T(8,128)(2,1)S(1)} %copy.36), channel_id=1, source_target_pairs={{0,1},{1,0},{2,3},{3,2},{4,5},{5,4},{6,7},{7,6},{8,9},{9,8},{10,11... | collective-permute-start | bytes 2654216 | tf_op jit(solution)/shard_map/ppermute | solution.py:38
  167.5 1.1 copy-start.4
  167.5 1.4 copy-start.5
  173.7 41.9 %collective-permute-start.17 = (bf16[192,1536]{1,0:T(8,128)(2,1)}, bf16[192,1536]{1,0:T(8,128)(2,1)S(1)}, u32[]{:S(2)}, u32[]{:S(2)}) collective-permute-start(bf16[192,1536]{1,0:T(8,128)(2,1)} %get-tuple-element.154), channel_id=1, source_target_pairs={{0,2},{1,3},{2,0},{3,1},{4,6},{5,7},{6,4},{7,5},{8,10},{9,11},{10,... | collective-permute-start | bytes 1769480 | tf_op jit(solution)/shard_map/ppermute | solution.py:38
  175.1 40.5 %collective-permute-start.18 = (bf16[192,1536]{1,0:T(8,128)(2,1)}, bf16[192,1536]{1,0:T(8,128)(2,1)S(1)}, u32[]{:S(2)}, u32[]{:S(2)}) collective-permute-start(bf16[192,1536]{1,0:T(8,128)(2,1)} %get-tuple-element.155), channel_id=1, source_target_pairs={{0,4},{1,5},{2,6},{3,7},{4,0},{5,1},{6,2},{7,3},{8,12},{9,13},{10,... | collective-permute-start | bytes 1769480 | tf_op jit(solution)/shard_map/ppermute | solution.py:38
  175.7 10.9 %copy-start.39 = (bf16[384,576]{1,0:T(8,128)(2,1)S(1)}, bf16[384,576]{1,0:T(8,128)(2,1)}, u32[]{:S(2)}) copy-start(bf16[384,576]{1,0:T(8,128)(2,1)} %get-tuple-element.156) | copy-start | bytes 1327108
  186.6 28.9 %collective-permute-start.19 = (bf16[384,576]{1,0:T(8,128)(2,1)S(1)}, bf16[384,576]{1,0:T(8,128)(2,1)S(1)}, u32[]{:S(2)}, u32[]{:S(2)}) collective-permute-start(bf16[384,576]{1,0:T(8,128)(2,1)S(1)} %copy-done.39), channel_id=1, source_target_pairs={{0,8},{1,9},{2,10},{3,11},{4,12},{5,13},{6,14},{7,15},{8,0},{9,1},... | collective-permute-start | bytes 1327112 | tf_op jit(solution)/shard_map/ppermute | solution.py:38
  196.4 3.7 %collective-permute-start.11 = (bf16[384,384]{1,0:T(8,128)(2,1)}, bf16[384,384]{1,0:T(8,128)(2,1)S(1)}, u32[]{:S(2)}, u32[]{:S(2)}) collective-permute-start(bf16[384,384]{1,0:T(8,128)(2,1)} %get-tuple-element.131), channel_id=1, source_target_pairs={{1,0},{2,1},{3,2},{4,3},{5,4},{6,5},{7,6},{8,7},{9,8},{10,9},{11,1... | collective-permute-start | bytes 884744 | tf_op jit(solution)/shard_map/ppermute | solution.py:26
  211.1 32.0 %collective-permute-start.12 = (bf16[384,768]{1,0:T(8,128)(2,1)}, bf16[384,768]{1,0:T(8,128)(2,1)S(1)}, u32[]{:S(2)}, u32[]{:S(2)}) collective-permute-start(bf16[384,768]{1,0:T(8,128)(2,1)} %get-tuple-element.139), channel_id=1, source_target_pairs={{0,1},{1,0},{2,3},{3,2},{4,5},{5,4},{6,7},{7,6},{8,9},{9,8},{10,11... | collective-permute-start | bytes 1769480 | tf_op jit(solution)/shard_map/ppermute | solution.py:38
  215.5 27.6 %collective-permute-start.13 = (bf16[384,768]{1,0:T(8,128)(2,1)}, bf16[384,768]{1,0:T(8,128)(2,1)S(1)}, u32[]{:S(2)}, u32[]{:S(2)}) collective-permute-start(bf16[384,768]{1,0:T(8,128)(2,1)} %get-tuple-element.140), channel_id=1, source_target_pairs={{0,1},{1,0},{2,3},{3,2},{4,5},{5,4},{6,7},{7,6},{8,9},{9,8},{10,11... | collective-permute-start | bytes 1769480 | tf_op jit(solution)/shard_map/ppermute | solution.py:38
  215.6 1.0 copy-start.7
  215.6 1.1 copy-start.8
  219.9 11.6 %collective-permute-start.20 = (bf16[96,1536]{1,0:T(8,128)(2,1)}, bf16[96,1536]{1,0:T(8,128)(2,1)S(1)}, u32[]{:S(2)}, u32[]{:S(2)}) collective-permute-start(bf16[96,1536]{1,0:T(8,128)(2,1)} %get-tuple-element.160), channel_id=1, source_target_pairs={{0,24},{1,25},{2,26},{3,27},{4,28},{5,29},{6,30},{7,31},{8,16},{9,... | collective-permute-start | bytes 884744 | tf_op jit(solution)/shard_map/ppermute | solution.py:38
  221.6 9.9 %collective-permute-start.21 = (bf16[96,1536]{1,0:T(8,128)(2,1)}, bf16[96,1536]{1,0:T(8,128)(2,1)S(1)}, u32[]{:S(2)}, u32[]{:S(2)}) collective-permute-start(bf16[96,1536]{1,0:T(8,128)(2,1)} %get-tuple-element.161), channel_id=1, source_target_pairs={{0,2},{1,3},{2,0},{3,1},{4,6},{5,7},{6,4},{7,5},{8,10},{9,11},{10,... | collective-permute-start | bytes 884744 | tf_op jit(solution)/shard_map/ppermute | solution.py:38
  223.5 7.9 %collective-permute-start.22 = (bf16[192,576]{1,0:T(8,128)(2,1)}, bf16[192,576]{1,0:T(8,128)(2,1)S(1)}, u32[]{:S(2)}, u32[]{:S(2)}) collective-permute-start(bf16[192,576]{1,0:T(8,128)(2,1)} %get-tuple-element.162), channel_id=1, source_target_pairs={{0,4},{1,5},{2,6},{3,7},{4,0},{5,1},{6,2},{7,3},{8,12},{9,13},{10,... | collective-permute-start | bytes 663560 | tf_op jit(solution)/shard_map/ppermute | solution.py:38
  231.5 0.9 copy-start.13
  234.7 12.1 %collective-permute-start.23 = (bf16[48,1536]{1,0:T(8,128)(2,1)}, bf16[48,1536]{1,0:T(8,128)(2,1)S(1)}, u32[]{:S(2)}, u32[]{:S(2)}) collective-permute-start(bf16[48,1536]{1,0:T(8,128)(2,1)} %get-tuple-element.166), channel_id=1, source_target_pairs={{0,8},{1,9},{2,10},{3,11},{4,12},{5,13},{6,14},{7,15},{8,0},{9,1},... | collective-permute-start | bytes 442376 | tf_op jit(solution)/shard_map/ppermute | solution.py:38
  239.5 8.3 %collective-permute-start.24 = (bf16[48,1536]{1,0:T(8,128)(2,1)}, bf16[48,1536]{1,0:T(8,128)(2,1)S(1)}, u32[]{:S(2)}, u32[]{:S(2)}) collective-permute-start(bf16[48,1536]{1,0:T(8,128)(2,1)} %get-tuple-element.167), channel_id=1, source_target_pairs={{0,24},{1,25},{2,26},{3,27},{4,28},{5,29},{6,30},{7,31},{8,16},{9,... | collective-permute-start | bytes 442376 | tf_op jit(solution)/shard_map/ppermute | solution.py:38
  241.1 5.7 %collective-permute-start.25 = (bf16[96,576]{1,0:T(8,128)(2,1)}, bf16[96,576]{1,0:T(8,128)(2,1)S(1)}, u32[]{:S(2)}, u32[]{:S(2)}) collective-permute-start(bf16[96,576]{1,0:T(8,128)(2,1)} %get-tuple-element.168), channel_id=1, source_target_pairs={{0,2},{1,3},{2,0},{3,1},{4,6},{5,7},{6,4},{7,5},{8,10},{9,11},{10,... | collective-permute-start | bytes 331784 | tf_op jit(solution)/shard_map/ppermute | solution.py:38
  243.1 1.0 copy-start.10
  246.8 1.0 copy-start.24
  246.8 1.0 copy-start.18
  250.5 15.9 %collective-permute-start.26 = (bf16[192,768]{1,0:T(8,128)(2,1)}, bf16[192,768]{1,0:T(8,128)(2,1)S(1)}, u32[]{:S(2)}, u32[]{:S(2)}) collective-permute-start(bf16[192,768]{1,0:T(8,128)(2,1)} %get-tuple-element.177), channel_id=1, source_target_pairs={{0,24},{1,25},{2,26},{3,27},{4,28},{5,29},{6,30},{7,31},{8,16},{9,... | collective-permute-start | bytes 884744 | tf_op jit(solution)/shard_map/ppermute | solution.py:38
  252.6 13.8 %collective-permute-start.27 = (bf16[192,768]{1,0:T(8,128)(2,1)}, bf16[192,768]{1,0:T(8,128)(2,1)S(1)}, u32[]{:S(2)}, u32[]{:S(2)}) collective-permute-start(bf16[192,768]{1,0:T(8,128)(2,1)} %get-tuple-element.178), channel_id=1, source_target_pairs={{0,4},{1,5},{2,6},{3,7},{4,0},{5,1},{6,2},{7,3},{8,12},{9,13},{10,... | collective-permute-start | bytes 884744 | tf_op jit(solution)/shard_map/ppermute | solution.py:38
  253.6 9.6 %collective-permute-start.28 = (bf16[24,1536]{1,0:T(8,128)(2,1)}, bf16[24,1536]{1,0:T(8,128)(2,1)S(1)}, u32[]{:S(2)}, u32[]{:S(2)}) collective-permute-start(bf16[24,1536]{1,0:T(8,128)(2,1)} %get-tuple-element.186), channel_id=1, source_target_pairs={{0,4},{1,5},{2,6},{3,7},{4,0},{5,1},{6,2},{7,3},{8,12},{9,13},{10,... | collective-permute-start | bytes 221192 | tf_op jit(solution)/shard_map/ppermute | solution.py:38
  254.6 8.7 %collective-permute-start.29 = (bf16[24,1536]{1,0:T(8,128)(2,1)}, bf16[24,1536]{1,0:T(8,128)(2,1)S(1)}, u32[]{:S(2)}, u32[]{:S(2)}) collective-permute-start(bf16[24,1536]{1,0:T(8,128)(2,1)} %get-tuple-element.187), channel_id=1, source_target_pairs={{0,8},{1,9},{2,10},{3,11},{4,12},{5,13},{6,14},{7,15},{8,0},{9,1},... | collective-permute-start | bytes 221192 | tf_op jit(solution)/shard_map/ppermute | solution.py:38
  254.6 8.7 %collective-permute-start.30 = (bf16[48,576]{1,0:T(8,128)(2,1)}, bf16[48,576]{1,0:T(8,128)(2,1)S(1)}, u32[]{:S(2)}, u32[]{:S(2)}) collective-permute-start(bf16[48,576]{1,0:T(8,128)(2,1)} %get-tuple-element.188), channel_id=1, source_target_pairs={{0,24},{1,25},{2,26},{3,27},{4,28},{5,29},{6,30},{7,31},{8,16},{9,... | collective-permute-start | bytes 165896 | tf_op jit(solution)/shard_map/ppermute | solution.py:38
  266.3 25.2 %copy-start.20 = (f32[24,1536]{1,0:T(8,128)S(1)}, f32[24,1536]{1,0:T(8,128)}, u32[]{:S(2)}) copy-start(f32[24,1536]{1,0:T(8,128)} %get-tuple-element.206) | copy-start | bytes 442372
  266.3 25.2 %copy-start.21 = (f32[24,1536]{1,0:T(8,128)S(1)}, f32[24,1536]{1,0:T(8,128)}, u32[]{:S(2)}) copy-start(f32[24,1536]{1,0:T(8,128)} %get-tuple-element.207) | copy-start | bytes 442372
  269.8 22.5 %copy-start.25 = (f32[48,576]{1,0:T(8,128)S(1)}, f32[48,576]{1,0:T(8,128)}, u32[]{:S(2)}) copy-start(f32[48,576]{1,0:T(8,128)} %get-tuple-element.208) | copy-start | bytes 331780
  269.8 5.9 %collective-permute-start.31 = (bf16[96,768]{1,0:T(8,128)(2,1)}, bf16[96,768]{1,0:T(8,128)(2,1)S(1)}, u32[]{:S(2)}, u32[]{:S(2)}) collective-permute-start(bf16[96,768]{1,0:T(8,128)(2,1)} %get-tuple-element.194), channel_id=1, source_target_pairs={{0,8},{1,9},{2,10},{3,11},{4,12},{5,13},{6,14},{7,15},{8,0},{9,1},... | collective-permute-start | bytes 442376 | tf_op jit(solution)/shard_map/ppermute | solution.py:38
  272.4 5.4 %collective-permute-start.32 = (bf16[96,768]{1,0:T(8,128)(2,1)}, bf16[96,768]{1,0:T(8,128)(2,1)S(1)}, u32[]{:S(2)}, u32[]{:S(2)}) collective-permute-start(bf16[96,768]{1,0:T(8,128)(2,1)} %get-tuple-element.195), channel_id=1, source_target_pairs={{0,2},{1,3},{2,0},{3,1},{4,6},{5,7},{6,4},{7,5},{8,10},{9,11},{10,... | collective-permute-start | bytes 442376 | tf_op jit(solution)/shard_map/ppermute | solution.py:38
  275.8 2.0 copy-start.22
  280.3 4.6 %collective-permute-start.33 = (bf16[48,768]{1,0:T(8,128)(2,1)}, bf16[48,768]{1,0:T(8,128)(2,1)S(1)}, u32[]{:S(2)}, u32[]{:S(2)}) collective-permute-start(bf16[48,768]{1,0:T(8,128)(2,1)} %get-tuple-element.198), channel_id=1, source_target_pairs={{0,4},{1,5},{2,6},{3,7},{4,0},{5,1},{6,2},{7,3},{8,12},{9,13},{10,... | collective-permute-start | bytes 221192 | tf_op jit(solution)/shard_map/ppermute | solution.py:38
  281.8 6.4 %collective-permute-start.34 = (bf16[48,768]{1,0:T(8,128)(2,1)}, bf16[48,768]{1,0:T(8,128)(2,1)S(1)}, u32[]{:S(2)}, u32[]{:S(2)}) collective-permute-start(bf16[48,768]{1,0:T(8,128)(2,1)} %get-tuple-element.199), channel_id=1, source_target_pairs={{0,24},{1,25},{2,26},{3,27},{4,28},{5,29},{6,30},{7,31},{8,16},{9,... | collective-permute-start | bytes 221192 | tf_op jit(solution)/shard_map/ppermute | solution.py:38
  284.8 3.3 %copy-start.28 = (bf16[48,768]{1,0:T(8,128)(2,1)}, bf16[48,768]{1,0:T(8,128)(2,1)S(1)}, u32[]{:S(2)}) copy-start(bf16[48,768]{1,0:T(8,128)(2,1)S(1)} %collective-permute-done.33.refs_2_) | copy-start | bytes 221188
  290.4 4.2 %collective-permute-start.35 = (bf16[24,768]{1,0:T(8,128)(2,1)}, bf16[24,768]{1,0:T(8,128)(2,1)S(1)}, u32[]{:S(2)}, u32[]{:S(2)}) collective-permute-start(bf16[24,768]{1,0:T(8,128)(2,1)} %get-tuple-element.202), channel_id=1, source_target_pairs={{0,2},{1,3},{2,0},{3,1},{4,6},{5,7},{6,4},{7,5},{8,10},{9,11},{10,... | collective-permute-start | bytes 110600 | tf_op jit(solution)/shard_map/ppermute | solution.py:38
  291.6 4.2 %collective-permute-start.36 = (bf16[24,768]{1,0:T(8,128)(2,1)}, bf16[24,768]{1,0:T(8,128)(2,1)S(1)}, u32[]{:S(2)}, u32[]{:S(2)}) collective-permute-start(bf16[24,768]{1,0:T(8,128)(2,1)} %get-tuple-element.203), channel_id=1, source_target_pairs={{0,8},{1,9},{2,10},{3,11},{4,12},{5,13},{6,14},{7,15},{8,0},{9,1},... | collective-permute-start | bytes 110600 | tf_op jit(solution)/shard_map/ppermute | solution.py:38
  294.6 1.1 copy-start.31
  (16 other events, 11.2 us)
Sparse Core Ops, SparseCore 0:
  11.5 63.5 all-gather.4
  78.6 62.0 all-gather.2

commit v3 on v2

--- a/solution.py
+++ b/solution.py
@@ -1,4 +1,3 @@
-import functools
 import math
 
 import jax
@@ -355,6 +354,7 @@
 
 
 PAD = 24
+FOLD_LANES = 640
 CHUNK = 128
 bf16 = jnp.bfloat16
 f32 = jnp.float32
@@ -366,11 +366,6 @@
 
 def dot_nt(a, b):
     return lax.dot_general(a, b, (((1,), (1,)), ((), ())), preferred_element_type=f32)
-
-
-def split_two(value):
-    high = value.astype(bf16)
-    return high, (value - high.astype(f32)).astype(bf16)
 
 
 def spread_wide(source_row):
@@ -482,22 +477,55 @@
         down_out[low : low + HD, :] = dv[:, tokens:]
 
 
+def prepare_kernel(
+    att,
+    tok,
+    gain_in,
+    gain,
+    row_b,
+    row_n,
+    tall_g,
+    tall_u,
+    tall_a,
+    tall_b,
+    wb0,
+    wb1,
+    res_out,
+    wide_n,
+    tall_wide_g,
+    tall_wide_u,
+    tall_wide_a,
+    tall_wide_b,
+    tall_wide_att,
+):
+    wb = jnp.concatenate([wb0[...], wb1[...]], axis=0)
+    x = tok[...].astype(f32)
+    att_wide = dot_nn(att[...].T, spread_wide(row_b[...])).astype(bf16)
+    residual = x.T + dot_nn(att_wide, wb)[:, :D]
+    res_out[...] = residual
+    inverse = lax.rsqrt(jnp.mean(residual * residual, axis=-1, keepdims=True) + norm_epsilon)
+    normed = (residual * inverse * gain[...]).astype(bf16)
+    wide_n[...] = dot_nn(normed, spread_wide(row_n[...])).astype(bf16)
+    normed_t = normed.T
+    tall_wide_g[...] = dot_nn(spread_tall(tall_g[...]), normed_t).astype(bf16)
+    tall_wide_u[...] = dot_nn(spread_tall(tall_u[...]), normed_t).astype(bf16)
+    inverse_in = lax.rsqrt(jnp.mean(x * x, axis=0, keepdims=True) + norm_epsilon)
+    normed_in = (x * inverse_in * gain_in[...]).astype(bf16)
+    spread_b = spread_tall(tall_b[...])
+    tall_wide_a[...] = dot_nn(spread_tall(tall_a[...]), normed_in).astype(bf16)
+    tall_wide_b[...] = dot_nn(spread_b, normed_in).astype(bf16)
+    tall_wide_att[...] = dot_nn(spread_b, att[...]).astype(bf16)
+
+
 def feed_kernel(
     slots,
-    att,
-    tok,
+    residual,
     cot,
-    gain,
-    src_b,
-    src_n,
-    tall_g,
-    tall_u,
-    wb0,
-    wb1,
-    wgu,
-    wd,
+    wide_n,
+    tall_wide_g,
+    tall_wide_u,
+    wall,
     mixed_out,
-    res_out,
     dgate,
     dup,
     dg_low,
@@ -507,27 +535,25 @@
     du_high,
     dd_high,
     act,
-    wide_n,
-    dd,
+    wd,
 ):
     count = slots.shape[0]
     rows_d = FF // count
-    wb = jnp.concatenate([wb0[...], wb1[...]], axis=0)
+    fold = rows_d // 2
+    for j in range(count):
+        for k in range(2):
+            at = 2 * FF + k * FOLD_LANES
+            wd[j * rows_d + k * fold : j * rows_d + (k + 1) * fold, :] = wall[
+                j * PAD : j * PAD + fold, at : at + D
+            ]
     cot_tok = cot[...].T
-    att_wide = dot_nn(att[...].T, spread_wide(src_b[...])).astype(bf16)
-    residual = tok[...].astype(f32).T + dot_nn(att_wide, wb)[:, :D]
-    res_out[...] = residual
-    inverse = lax.rsqrt(jnp.mean(residual * residual, axis=-1, keepdims=True) + norm_epsilon)
-    normed = (residual * inverse * gain[...]).astype(bf16)
-    wide_n[...] = dot_nn(normed, spread_wide(src_n[...])).astype(bf16)
-    normed_t = normed.T
     block = 256
 
     def ff_step(j, carry):
         cut = pl.ds(pl.multiple_of(j * block, block), block)
         cut_up = pl.ds(pl.multiple_of(j * block + FF, block), block)
-        gate = dot_nn(wide_n[...], wgu[:, cut])
-        up = dot_nn(wide_n[...], wgu[:, cut_up])
+        gate = dot_nn(wide_n[...], wall[:, cut])
+        up = dot_nn(wide_n[...], wall[:, cut_up])
         grad_act = dot_nt(cot_tok, wd[cut, :])
         sig = jax.nn.sigmoid(gate)
         silu = gate * sig
@@ -537,18 +563,18 @@
         return carry
 
     lax.fori_loop(0, FF // block, ff_step, 0)
-    mixed = residual + dot_nn(act[...], wd[...])
+    mixed = residual[...] + dot_nn(act[...], wd[...])
     mixed_out[...] = mixed.T.astype(bf16)
-    for tall, grad, low, high in ((tall_g, dgate, dg_low, dg_high), (tall_u, dup, du_low, du_high)):
-        wide_t = dot_nn(spread_tall(tall[...]), normed_t).astype(bf16)
-        half = wide_t.shape[0] // 2
-        low[...] = dot_nn(wide_t[:half], grad[...]).astype(bf16)
-        high[...] = dot_nn(wide_t[half:], grad[...]).astype(bf16)
-    dd[...] = dot_nn(act[...].T, cot_tok).astype(bf16)
+    half = tall_wide_g.shape[0] // 2
+    dg_low[...] = dot_nn(tall_wide_g[:half, :], dgate[...]).astype(bf16)
+    dg_high[...] = dot_nn(tall_wide_g[half:, :], dgate[...]).astype(bf16)
+    du_low[...] = dot_nn(tall_wide_u[:half, :], dup[...]).astype(bf16)
+    du_high[...] = dot_nn(tall_wide_u[half:, :], dup[...]).astype(bf16)
+    wd[...] = dot_nn(act[...].T, cot_tok).astype(bf16)
     for p in range(count):
         source = pl.multiple_of(slots[p] * rows_d, rows_d)
         out, at = (dd_low, p) if p < count // 2 else (dd_high, p - count // 2)
-        out[at * rows_d : (at + 1) * rows_d, :] = dd[pl.ds(source, rows_d), :]
+        out[at * rows_d : (at + 1) * rows_d, :] = wd[pl.ds(source, rows_d), :]
 
 
 def feed_back_kernel(
@@ -561,7 +587,7 @@
     dup,
     wb0,
     wb1,
-    wgu,
+    wall,
     gres_out,
     gatt_out,
     dgain_out,
@@ -570,8 +596,8 @@
     spread_b = spread_wide(src_b[...])
     spread_n = spread_wide(src_n[...])
     inverse = lax.rsqrt(jnp.mean(residual * residual, axis=-1, keepdims=True) + norm_epsilon)
-    dn = dot_nt(dgate[...], wgu[:, :FF]) + dot_nt(dup[...], wgu[:, FF:])
-    grad_normed = sum(dot_nt(part, spread_n) for part in split_two(dn))
+    dn = dot_nt(dgate[...], wall[:, :FF]) + dot_nt(dup[...], wall[:, FF : 2 * FF])
+    grad_normed = dot_nt(dn.astype(bf16), spread_n)
     unit = residual * inverse
     scaled = grad_normed * gain[...]
     dgain_out[...] = jnp.sum(grad_normed * unit, axis=0, keepdims=True)
@@ -593,7 +619,9 @@
     cos,
     sin,
     gres,
-    att,
+    wide_a,
+    wide_b,
+    wide_att,
     dgain_ffn,
     src_a,
     src_b,
@@ -612,7 +640,6 @@
     x = tok[...].astype(f32)
     inverse = lax.rsqrt(jnp.mean(x * x, axis=0, keepdims=True) + norm_epsilon)
     unit = x * inverse
-    normed = (unit * gain[...]).astype(bf16)
     total = own[...] + back[...].astype(f32)
     half = HD // 2
     parts = [dq[...]]
@@ -633,39 +660,21 @@
     dn_b = dot_nn(wb, dvx)
     spread_a = spread_wide(src_a[...])
     spread_b = spread_wide(src_b[...])
-    grad_normed = sum(dot_nn(spread_a, part) for part in split_two(dn_a)) + sum(
-        dot_nn(spread_b, part) for part in split_two(dn_b)
-    )
+    grad_normed = dot_nn(spread_a, dn_a.astype(bf16)) + dot_nn(spread_b, dn_b.astype(bf16))
     scaled = grad_normed * gain[...]
     dtok_out[...] = gres[...] + inverse * (
         scaled - unit * jnp.mean(scaled * unit, axis=0, keepdims=True)
     )
     dgain = jnp.sum(grad_normed * unit, axis=1, keepdims=True)
     dgain = jnp.broadcast_to(dgain, (D, CHUNK)).T[:1]
-    tall_spread_b = spread_tall(tall_b[...])
-    wide_a = dot_nn(spread_tall(tall_a[...]), normed).astype(bf16)
-    wide_b = dot_nn(tall_spread_b, normed).astype(bf16)
-    wide_att = dot_nn(tall_spread_b, att[...]).astype(bf16)
     fill_a = jnp.concatenate([dgain, jnp.zeros((1, KVH * HD), f32)], axis=1)
     gres_b = gres[...].astype(bf16)
     half = wide_a.shape[0] // 2
     for cut, da_out, db_out in ((slice(0, half), da_low, db_low), (slice(half, None), da_high, db_high)):
-        da_out[...] = jnp.where(tall_a[cut] < 0, fill_a, dot_nt(wide_a[cut], dqk)).astype(bf16)
-        d_out = dot_nt(wide_att[cut], gres_b)
-        db_out[:, :D] = jnp.where(tall_b[cut] < 0, dgain_ffn[...], d_out).astype(bf16)
-        db_out[:, D:] = dot_nt(wide_b[cut], dv).astype(bf16)
-
-
-def merge_kernel(streams, final, *refs):
-    kept, got, outs = refs[:streams], refs[streams : 2 * streams], refs[2 * streams :]
-    for i in range(streams):
-        total = kept[i][...].astype(f32) + got[i][...].astype(f32)
-        if final:
-            outs[i][...] = total
-        else:
-            half = total.shape[0] // 2
-            outs[i][...] = total[:half].astype(bf16)
-            outs[streams + i][...] = total[half:].astype(bf16)
+        da_out[...] = jnp.where(tall_a[cut, :] < 0, fill_a, dot_nt(wide_a[cut, :], dqk)).astype(bf16)
+        d_out = dot_nt(wide_att[cut, :], gres_b)
+        db_out[:, :D] = jnp.where(tall_b[cut, :] < 0, dgain_ffn[...], d_out).astype(bf16)
+        db_out[:, D:] = dot_nt(wide_b[cut, :], dv).astype(bf16)
 
 
 def call_whole(kernel, outs, operands, scratch=(), scalars=()):
@@ -692,19 +701,18 @@
     return [jnp.concatenate([h, g], axis=0) for h, g in zip(held, got)]
 
 
-def step_halve(pair, orders, t):
+def step_halve(pair, orders, t, even=False):
     kept, send = pair
-    streams = len(kept)
-    got = []
-    for value, order in zip(send, orders):
-        got.append(swapped(value, order[-1 - t]))
     final = t == len(orders[0]) - 1
-    if final:
-        outs = [(k.shape, f32) for k in kept]
-    else:
-        outs = [((k.shape[0] // 2, k.shape[1]), bf16) for k in kept] * 2
-    merged = call_whole(functools.partial(merge_kernel, streams, final), outs, list(kept) + got)
-    return merged if final else (merged[:streams], merged[streams:])
+    low, high = [], []
+    for k, value, order in zip(kept, send, orders):
+        g = swapped(value, order[-1 - t])
+        if even:
+            k = lax.reduce_precision(k.astype(f32), 8, 7)
+        half = k.shape[0] if final else k.shape[0] // 2
+        low.append(k[:half].astype(f32) + g[:half].astype(f32))
+        high.append((k[half:].astype(f32) + g[half:].astype(f32)).astype(bf16))
+    return low if final else (low, high)
 
 
 def sources(order, count, per_slot):
@@ -740,9 +748,10 @@
     w_qs, w_kvs = w_query.reshape(per, H * HD), w_kv.reshape(per, 2 * KVH * HD)
     kv_cut = KVH * HD
     stream_gu = padded_rows(w_gate_up.reshape(per, 2 * FF))
-    stream_d = w_down.reshape(per_d, D)
-    wgu = lax.all_gather(stream_gu, "dev", axis=0, tiled=True)
-    wd = lax.all_gather(stream_d, "dev", axis=0, tiled=True)
+    folded = w_down.reshape(2, per_d // 2, D)
+    folded = jnp.pad(folded, ((0, 0), (0, PAD - per_d // 2), (0, FOLD_LANES - D)))
+    stream_ffn = jnp.concatenate([stream_gu, folded[0], folded[1]], axis=1)
+    wall = lax.all_gather(stream_ffn, "dev", axis=0, tiled=True)
     stream_a = padded_rows(jnp.concatenate([w_qs, w_kvs[:, :kv_cut]], axis=1))
     stream_b = padded_rows(jnp.concatenate([w_out.reshape(per, D), w_kvs[:, kv_cut:]], axis=1))
     half_dim = HD // 2
@@ -781,28 +790,30 @@
         [q_t, near, kv_t, positions[None]],
     )
     wide = count * PAD
-    mixed_t, residual, dgate, dup, *sums = call_whole(
+    tall_shape = ((wide, row_count), bf16)
+    residual, wide_n, tall_wide_g, tall_wide_u, wide_a, wide_b, wide_att = call_whole(
+        prepare_kernel,
+        [((row_count, D), f32), ((row_count, wide), bf16)] + [tall_shape] * 5,
+        [att_t, tok_t, gain_col, gain_ffn[None], row_b, row_n, tall_g, tall_u, tall_a, tall_b]
+        + [wb0, wb1],
+    )
+    mixed_t, dgate, dup, *sums = call_whole(
         feed_kernel,
         [
             ((D, row_count), bf16),
-            ((row_count, D), f32),
             ((row_count, FF), bf16),
             ((row_count, FF), bf16),
         ]
         + [((wide // 2, FF), bf16), ((wide // 2, FF), bf16), ((FF // 2, D), bf16)] * 2,
-        [att_t, tok_t, cot_t, gain_ffn[None], row_b, row_n, tall_g, tall_u, wb0, wb1, wgu, wd],
-        scratch=[
-            pltpu.VMEM((row_count, FF), bf16),
-            pltpu.VMEM((row_count, wide), bf16),
-            pltpu.VMEM((FF, D), bf16),
-        ],
+        [residual, cot_t, wide_n, tall_wide_g, tall_wide_u, wall],
+        scratch=[pltpu.VMEM((row_count, FF), bf16), pltpu.VMEM((FF, D), bf16)],
         scalars=[slots],
     )
     sums = (sums[:3], sums[3:])
     gres_t, gatt_t, dgain_ffn = call_whole(
         feed_back_kernel,
         [((D, row_count), f32), ((H * HD, row_count), bf16), ((1, D), f32)],
-        [residual, cot_t, gain_ffn[None], row_b, row_n, dgate, dup, wb0, wb1, wgu],
+        [residual, cot_t, gain_ffn[None], row_b, row_n, dgate, dup, wb0, wb1, wall],
     )
     for t in range(3):
         sums = step_halve(sums, orders_gud, t)
@@ -823,15 +834,14 @@
             ((D, row_count), f32),
         ]
         + [((wide // 2, H * HD + kv_cut), bf16), ((wide // 2, D + kv_cut), bf16)] * 2,
-        [dq_t, down, back, tok_t, gain_col, cos, sin, gres_t, att_t, dgain_ffn]
+        [dq_t, down, back, tok_t, gain_col, cos, sin, gres_t, wide_a, wide_b, wide_att, dgain_ffn]
         + [row_a, row_b, tall_a, tall_b, wa0, wa1, wb0, wb1],
     )
     last = (last[:2], last[2:])
     for t in range(steps):
-        last = step_halve(last, orders_ab, t)
+        last = step_halve(last, orders_ab, t, even=True)
         if t + 3 < steps:
             sums = step_halve(sums, orders_gud, t + 3)
-            last, sums = hold((last, sums))
     share_g, share_u, share_d = sums
     share_a, share_b = last
     share_kv = jnp.concatenate([share_a[:per, H * HD :], share_b[:per, D:]], axis=1)
@@ -851,7 +861,7 @@
 
 def fits_whole_rows(count):
     per = D // count
-    return D % count == 0 and FF % count == 0 and (FF // count) % 16 == 0 and 16 <= per <= PAD
+    return D % count == 0 and FF % count == 0 and (FF // count) % 16 == 0 and 16 <= per < PAD and FF // count <= 2 * PAD
 
 
 def solution(mesh):

time: 317 us -> 248 us (0.78)
  waiting for transfers between devices: 117 us -> 75.6 us
  Pallas kernels: 88.7 us -> 66.5 us
  local copies, waits for them, and re-layouts: 39.1 us -> 20.8 us
  other arithmetic: 1.88 us -> 12.6 us
    all_gather x2 -> x1, waiting for transfers between devices: 69.4 us -> 11.8 us  [shards(): wall = lax.all_gather(stream_ffn, 'dev', axis=0, tiled=True)]
    pallas_call x16 -> x7, Pallas kernels: 88.7 us -> 66.5 us  [call_whole(): pl.pallas_call(kernel, out_shape=[jax.ShapeDtypeStruct(s, d) for s, d in...]
    ppermute x35, waiting for transfers between devices: 46.9 us -> 63.4 us  [swapped(): return lax.ppermute(value, 'dev', [(i, i ^ mask) for i in range(count)])]
    unnamed x86 -> x46, local copies, waits for them, and re-layouts: 12 us -> 2.9 us
    convert_element_type x0 -> x20, other arithmetic: none -> 8.67 us  [step_halve(): high.append((k[half:].astype(f32) + g[half:].astype(f32)).astype(bf16))]
  transfers between devices with their start and end apart: 39 -> 38, of which waited for: 19 -> 18; matrix products, arithmetic and copies ran while one was open for 6% -> 11% of each run, Pallas kernels for 18% -> 13%
where the time goes in v3:
time: 248 us; the launch traced here: 244 us
  waiting for transfers between devices  75.6 us (30%)
  Pallas kernels  66.5 us (27%)
  starting transfers between devices  54.1 us (22%)
  local copies, waits for them, and re-layouts  20.8 us (8%)
  between operations  14.8 us (6%)
  other arithmetic  12.6 us (5%)
    pallas_call x7, Pallas kernels, call_whole(): pl.pallas_call(kernel, out_shape=[jax.ShapeDtypeStruct(s, d) for s, d in...  66.5 us
    ppermute x35, waiting for transfers between devices, swapped(): return lax.ppermute(value, 'dev', [(i, i ^ mask) for i in range(count)])  63.4 us
    ppermute x35, starting transfers between devices, swapped(): return lax.ppermute(value, 'dev', [(i, i ^ mask) for i in range(count)])  50.2 us
    all_gather x1, waiting for transfers between devices, shards(): wall = lax.all_gather(stream_ffn, 'dev', axis=0, tiled=True)  11.8 us
    convert_element_type x20, other arithmetic, step_halve(): high.append((k[half:].astype(f32) + g[half:].astype(f32)).astype(bf16))  8.67 us
  transfers between devices with their start and end apart: 38, of which 18 were waited for; matrix products, arithmetic and copies ran while one was open for 11% of the time, Pallas kernels for 13%

profile of v3, /device:TPU:0, one launch (start us, length us, event | category | flops | bytes accessed | tf_op | source)
XLA Modules:
  0.0 244.3 jit_solution(152903693138415575)
XLA Ops:
  7.3 0.9 reshape.332
  8.3 1.0 reshape.331
  10.0 0.7 reshape.328
  11.0 3.1 %collective-permute-start.2 = (bf16[24,768]{1,0:T(8,128)(2,1)S(1)}, bf16[24,768]{1,0:T(8,128)(2,1)S(1)}, u32[]{:S(2)}, u32[]{:S(2)}) collective-permute-start(bf16[24,768]{1,0:T(8,128)(2,1)S(1)} %fusion.38), channel_id=1, source_target_pairs={{0,8},{1,9},{2,10},{3,11},{4,12},{5,13},{6,14},{7,15},{8,0},{9,1},... | collective-permute-start | bytes 110600 | tf_op jit(solution)/shard_map/ppermute | solution.py:37
  14.2 1.5 collective-permute-start
  15.9 0.9 multiply_sine_fusion
  19.6 2.5 %collective-permute-start.3 = (bf16[48,768]{1,0:T(8,128)(2,1)S(1)}, bf16[48,768]{1,0:T(8,128)(2,1)S(1)}, u32[]{:S(2)}, u32[]{:S(2)}) collective-permute-start(bf16[48,768]{1,0:T(8,128)(2,1)S(1)} %pad_maximum_fusion.6), channel_id=1, source_target_pairs={{0,24},{1,25},{2,26},{3,27},{4,28},{5,29},{6,30},{7,31},{8,16},{9,... | collective-permute-start | bytes 221192 | tf_op jit(solution)/shard_map/ppermute | solution.py:37
  22.2 1.6 collective-permute-start.1
  23.7 2.1 collective-permute-done.3
  25.8 2.0 collective-permute-done.1
  28.1 5.1 %collective-permute-done.7 = bf16[96,768]{1,0:T(8,128)(2,1)S(1)} collective-permute-done((bf16[96,768]{1,0:T(8,128)(2,1)S(1)}, bf16[96,768]{1,0:T(8,128)(2,1)S(1)}, u32[]{:S(2)}, u32[]{:S(2)}) %collective-permute-start.7) | collective-permute-done | bytes 147488 | tf_op jit(solution)/shard_map/ppermute | solution.py:37
  33.2 2.1 collective-permute-start.8
  35.9 4.1 %collective-permute-done.8 = bf16[192,768]{1,0:T(8,128)(2,1)S(1)} collective-permute-done((bf16[192,768]{1,0:T(8,128)(2,1)S(1)}, bf16[192,768]{1,0:T(8,128)(2,1)S(1)}, u32[]{:S(2)}, u32[]{:S(2)}) %collective-permute-start.8) | collective-permute-done | bytes 294944 | tf_op jit(solution)/shard_map/ppermute | solution.py:37
  40.1 3.9 %collective-permute-done.5 = bf16[192,768]{1,0:T(8,128)(2,1)S(1)} collective-permute-done((bf16[192,768]{1,0:T(8,128)(2,1)S(1)}, bf16[192,768]{1,0:T(8,128)(2,1)S(1)}, u32[]{:S(2)}, u32[]{:S(2)}) %collective-permute-start.5) | collective-permute-done | bytes 294944 | tf_op jit(solution)/shard_map/ppermute | solution.py:37
  44.1 0.9 copy.33.gain.gain_in
  45.0 1.1 collective-permute-done.6.wa1
  46.1 0.8 copy-done.3
  46.9 4.8 %shard_map.214 = (bf16[576,384]{1,0:T(8,128)(2,1)}, bf16[384,384]{1,0:T(8,128)(2,1)}) custom-call(bf16[576,384]{1,0:T(8,128)(2,1)} %bitcast.8, f32[576,1]{1,0:T(8,128)} %copy.33.gain.gain_in, f32[32,384]{1,0:T(8,128)} %get-tuple-element.55.cos, f32[32,384]{1,0:T(8,128)} %get-tuple-element.56.sin, s32[1,768]{1,0:T(1,128)} %select_n.87.src_a, ...), custom_call_target="tpu_custom_call" | custom-call | tf_op jit(solution)/shard_map/pallas_call | solution.py:683
  51.7 2.5 %collective-permute-start.10 = (bf16[384,384]{1,0:T(8,128)(2,1)}, bf16[384,384]{1,0:T(8,128)(2,1)S(1)}, u32[]{:S(2)}, u32[]{:S(2)}) collective-permute-start(bf16[384,384]{1,0:T(8,128)(2,1)} %get-tuple-element.62.own), channel_id=1, source_target_pairs={{0,1},{1,2},{2,3},{3,4},{4,5},{5,6},{6,7},{7,8},{8,9},{9,10},{10,1... | collective-permute-start | bytes 884744 | tf_op jit(solution)/shard_map/ppermute | solution.py:25
  55.3 0.9 copy.37.tall_a
  56.3 0.9 copy.38.tall_b
  57.2 0.9 copy.35.tall_g
  58.1 0.9 copy.36.tall_u
  59.8 12.3 %shard_map.215 = (bf16[3,3,512,384]{3,2,1,0:T(8,128)(2,1)}, bf16[576,384]{1,0:T(8,128)(2,1)}) custom-call(bf16[576,384]{1,0:T(8,128)(2,1)} %get-tuple-element.61.q, bf16[384,384]{1,0:T(8,128)(2,1)} %copy-done.6, bf16[384,384]{1,0:T(8,128)(2,1)} %get-tuple-element.62.own, s32[1,384]{1,0:T(1,128)} %broadcast_in_dim.57.pos), custom_call_target="tpu_custom_call" | custom-call | tf_op jit(solution)/shard_map/pallas_call | solution.py:683
  72.1 7.8 %shard_map.216 = (f32[384,576]{1,0:T(8,128)}, bf16[384,768]{1,0:T(8,128)(2,1)}, bf16[768,384]{1,0:T(8,128)(2,1)}, bf16[768,384]{1,0:T(8,128)(2,1)}, bf16[768,384...) custom-call(bf16[576,384]{1,0:T(8,128)(2,1)} %get-tuple-element.63.att, ...), custom_call_target="tpu_custom_call" | custom-call | tf_op jit(solution)/shard_map/pallas_call | solution.py:683
  79.9 11.8 %all-gather.2.cloned.1.call-done.wall = bf16[768,4352]{1,0:T(8,128)(2,1)} async-done(((bf16[24,4352]{1,0:T(8,128)(2,1)}), bf16[768,4352]{1,0:T(8,128)(2,1)}) %all-gather.2.cloned.1.call-update) | async-done | bytes 6684688 | tf_op jit(solution)/shard_map/all_gather | solution.py:754
  91.7 14.9 %shard_map.217 = (bf16[576,384]{1,0:T(8,128)(2,1)}, bf16[384,1536]{1,0:T(8,128)(2,1)}, bf16[384,1536]{1,0:T(8,128)(2,1)}, bf16[384,1536]{1,0:T(8,128)(2,1)}, bf1...) custom-call(s32[32]{0:T(128)} %broadcast_xor_fusion.slots, ...), custom_call_target="tpu_custom_call" | custom-call | tf_op jit(solution)/shard_map/pallas_call | solution.py:683
  106.6 10.3 %shard_map.218 = (f32[576,384]{1,0:T(8,128)}, bf16[576,384]{1,0:T(8,128)(2,1)}, f32[1,576]{1,0:T(1,128)}) custom-call(f32[384,576]{1,0:T(8,128)} %get-tuple-element.69.residual.residual_in, bf16[576,384]{1,0:T(8,128)(2,1)} %bitcast.12, f32[1,576]{1,0:T(1,128)} %broadcast_in_dim.58.gain, s32[1,768]{1,0:T(1,128)} %select_n.89.src_b.row_b, ...), custom_call_target="tpu_custom_call" | custom-call | tf_op jit(solution)/shard_map/pallas_call | solution.py:683
  116.9 8.4 %shard_map.219 = (bf16[576,384]{1,0:T(8,128)(2,1)}, bf16[384,384]{1,0:T(8,128)(2,1)}, f32[384,384]{1,0:T(8,128)}) custom-call(bf16[576,384]{1,0:T(8,128)(2,1)} %get-tuple-element.61.q, bf16[384,384]{1,0:T(8,128)(2,1)} %copy-done.6, bf16[384,384]{1,0:T(8,128)(2,1)} %get-tuple-element.62.own, bf16[3,3,512,384]{3,2,1,0:T(8,128)(2,1)} %get-tuple-element.74.prob, ...), custom_call_target="tpu_custom_call" | custom-call | tf_op jit(solution)/shard_map/pallas_call | solution.py:683
  125.3 1.3 collective-permute-start.11
  126.6 0.8 copy.42
  127.4 1.2 collective-permute-start.32
  129.7 8.0 %shard_map.220 = (f32[576,384]{1,0:T(8,128)}, bf16[384,768]{1,0:T(8,128)(2,1)}, bf16[384,768]{1,0:T(8,128)(2,1)}, bf16[384,768]{1,0:T(8,128)(2,1)}, bf16[384,768]{1,0:T(8,128)(2,1)}) custom-call(bf16[576,384]{1,0:T(8,128)(2,1)} %get-tuple-element.78.dq, f32[384,384]{1,0:T(8,128)} %get-tuple-element.79.own, bf16[384,384]{1,0:T(8,128)(2,1)} %copy-done.10, ...), custom_call_target="tpu_custom_call" | custom-call | tf_op jit(solution)/shard_map/pallas_call | solution.py:683
  137.7 4.9 %collective-permute-start.12 = (bf16[384,768]{1,0:T(8,128)(2,1)}, bf16[384,768]{1,0:T(8,128)(2,1)S(1)}, u32[]{:S(2)}, u32[]{:S(2)}) collective-permute-start(bf16[384,768]{1,0:T(8,128)(2,1)} %get-tuple-element.88), channel_id=1, source_target_pairs={{0,1},{1,0},{2,3},{3,2},{4,5},{5,4},{6,7},{7,6},{8,9},{9,8},{10,11... | collective-permute-start | bytes 1769480 | tf_op jit(solution)/shard_map/ppermute | solution.py:37
  143.2 1.1 convert_reduce-precision_fusion.1
  144.6 1.2 fusion.41
  146.4 2.5 %collective-permute-start.13 = (bf16[192,768]{1,0:T(8,128)(2,1)S(1)}, bf16[192,768]{1,0:T(8,128)(2,1)S(1)}, u32[]{:S(2)}, u32[]{:S(2)}) collective-permute-start(bf16[192,768]{1,0:T(8,128)(2,1)S(1)} %get-tuple-element.107), channel_id=1, source_target_pairs={{0,24},{1,25},{2,26},{3,27},{4,28},{5,29},{6,30},{7,31},{8,16},{9,... | collective-permute-start | bytes 884744 | tf_op jit(solution)/shard_map/ppermute | solution.py:37
  148.9 1.2 fusion.2
  150.0 1.5 collective-permute-start.18
  151.7 1.6 collective-permute-start.33
  153.3 4.9 %collective-permute-done.13 = bf16[192,768]{1,0:T(8,128)(2,1)S(1)} collective-permute-done((bf16[192,768]{1,0:T(8,128)(2,1)S(1)}, bf16[192,768]{1,0:T(8,128)(2,1)S(1)}, u32[]{:S(2)}, u32[]{:S(2)}) %collective-permute-start.13) | collective-permute-done | bytes 294944 | tf_op jit(solution)/shard_map/ppermute | solution.py:37
  158.3 5.5 %collective-permute-start.14 = (bf16[96,768]{1,0:T(8,128)(2,1)S(1)}, bf16[96,768]{1,0:T(8,128)(2,1)S(1)}, u32[]{:S(2)}, u32[]{:S(2)}) collective-permute-start(bf16[96,768]{1,0:T(8,128)(2,1)S(1)} %get-tuple-element.121), channel_id=1, source_target_pairs={{0,8},{1,9},{2,10},{3,11},{4,12},{5,13},{6,14},{7,15},{8,0},{9,1},... | collective-permute-start | bytes 442376 | tf_op jit(solution)/shard_map/ppermute | solution.py:37
  163.8 2.4 collective-permute-start.19
  166.2 2.4 add_convert_fusion.1
  168.7 2.3 add_convert_fusion
  171.0 1.5 collective-permute-start.28
  173.2 1.6 collective-permute-start.15
  174.8 1.5 collective-permute-start.20
  176.3 16.0 %collective-permute-done.15 = bf16[48,768]{1,0:T(8,128)(2,1)S(1)} collective-permute-done((bf16[48,768]{1,0:T(8,128)(2,1)S(1)}, bf16[48,768]{1,0:T(8,128)(2,1)S(1)}, u32[]{:S(2)}, u32[]{:S(2)}) %collective-permute-start.15) | collective-permute-done | bytes 73760 | tf_op jit(solution)/shard_map/ppermute | solution.py:37
  192.3 1.8 collective-permute-start.16
  194.5 1.9 collective-permute-done.16
  197.0 1.2 collective-permute-done.21
  199.6 3.6 %collective-permute-done.35 = bf16[96,576]{1,0:T(8,128)(2,1)S(1)} collective-permute-done((bf16[96,576]{1,0:T(8,128)(2,1)S(1)}, bf16[96,576]{1,0:T(8,128)(2,1)S(1)}, u32[]{:S(2)}, u32[]{:S(2)}) %collective-permute-start.35) | collective-permute-done | bytes 110624 | tf_op jit(solution)/shard_map/ppermute | solution.py:37
  203.8 1.8 collective-permute-start.36
  207.7 2.4 collective-permute-done.36
  210.2 0.7 reshape.337
  210.9 1.2 fusion.1
  212.1 1.9 collective-permute-start.24
  214.7 7.6 %collective-permute-done.24 = bf16[96,1536]{1,0:T(8,128)(2,1)S(1)} collective-permute-done((bf16[96,1536]{1,0:T(8,128)(2,1)S(1)}, bf16[96,1536]{1,0:T(8,128)(2,1)S(1)}, u32[]{:S(2)}, u32[]{:S(2)}) %collective-permute-start.24) | collective-permute-done | bytes 294944 | tf_op jit(solution)/shard_map/ppermute | solution.py:37
  222.5 1.7 collective-permute-start.30
  224.2 3.3 %collective-permute-done.25 = bf16[48,1536]{1,0:T(8,128)(2,1)S(1)} collective-permute-done((bf16[48,1536]{1,0:T(8,128)(2,1)S(1)}, bf16[48,1536]{1,0:T(8,128)(2,1)S(1)}, u32[]{:S(2)}, u32[]{:S(2)}) %collective-permute-start.25) | collective-permute-done | bytes 147488 | tf_op jit(solution)/shard_map/ppermute | solution.py:37
  227.5 4.5 %collective-permute-start.26 = (bf16[24,1536]{1,0:T(8,128)(2,1)S(1)}, bf16[24,1536]{1,0:T(8,128)(2,1)S(1)}, u32[]{:S(2)}, u32[]{:S(2)}) collective-permute-start(bf16[24,1536]{1,0:T(8,128)(2,1)S(1)} %get-tuple-element.129), channel_id=1, source_target_pairs={{0,4},{1,5},{2,6},{3,7},{4,0},{5,1},{6,2},{7,3},{8,12},{9,13},{10,... | collective-permute-start | bytes 221192 | tf_op jit(solution)/shard_map/ppermute | solution.py:37
  232.1 2.2 collective-permute-done.26
  234.4 2.1 collective-permute-done.31
  (150 shorter events, 17.8 us)
Async XLA Ops:
  7.2 8.6 %copy-start.18 = (s32[32]{0:T(128)S(1)}, s32[32]{0:T(128)}, u32[]{:S(2)}) copy-start(s32[32]{0:T(128)} %constant.22.clone) | copy-start | bytes 388
  7.2 8.6 %copy-start.16 = (s32[32]{0:T(128)S(1)}, s32[32]{0:T(128)}, u32[]{:S(2)}) copy-start(s32[32]{0:T(128)} %constant.24.clone) | copy-start | bytes 388
  7.2 8.6 %copy-start.17 = (s32[32]{0:T(128)S(1)}, s32[32]{0:T(128)}, u32[]{:S(2)}) copy-start(s32[32]{0:T(128)} %constant.23.clone) | copy-start | bytes 388
  7.2 9.5 %copy-start.19 = (s32[32]{0:T(128)S(1)}, s32[32]{0:T(128)}, u32[]{:S(2)}) copy-start(s32[32]{0:T(128)} %constant.25.clone) | copy-start | bytes 388
  7.2 3.5 %copy-start.11 = (bf16[10368]{0:T(1024)(128)(2,1)S(1)}, bf16[10368]{0:T(1024)(128)(2,1)}, u32[]{:S(2)}) copy-start(bf16[10368]{0:T(1024)(128)(2,1)} %param.20) | copy-start | bytes 62212
  7.2 6.8 %copy-start.12 = (bf16[10368]{0:T(1024)(128)(2,1)S(1)}, bf16[10368]{0:T(1024)(128)(2,1)}, u32[]{:S(2)}) copy-start(bf16[10368]{0:T(1024)(128)(2,1)} %param.18) | copy-start | bytes 62212
  7.2 8.5 %copy-start.13 = (s32[384]{0:T(512)S(1)}, s32[384]{0:T(512)}, u32[]{:S(2)}) copy-start(s32[384]{0:T(512)} %param.16) | copy-start | bytes 4612
  7.3 11.6 %copy-start.14 = (f32[576]{0:T(1024)S(1)}, f32[576]{0:T(1024)}, u32[]{:S(2)}) copy-start(f32[576]{0:T(1024)} %param.17) | copy-start | bytes 6916
  7.3 84.4 %all-gather.2.cloned.1.call-start = ((), (), s32[]{:S(2)}) async-start(), calls=%async_computation | async-start | bytes 6893568 | tf_op jit(solution)/shard_map/all_gather | solution.py:754
  11.0 8.6 %collective-permute-start.2 = (bf16[24,768]{1,0:T(8,128)(2,1)S(1)}, bf16[24,768]{1,0:T(8,128)(2,1)S(1)}, u32[]{:S(2)}, u32[]{:S(2)}) collective-permute-start(bf16[24,768]{1,0:T(8,128)(2,1)S(1)} %fusion.38), channel_id=1, source_target_pairs={{0,8},{1,9},{2,10},{3,11},{4,12},{5,13},{6,14},{7,15},{8,0},{9,1},... | collective-permute-start | bytes 110600 | tf_op jit(solution)/shard_map/ppermute | solution.py:37
  14.2 7.9 %collective-permute-start = (bf16[24,768]{1,0:T(8,128)(2,1)S(1)}, bf16[24,768]{1,0:T(8,128)(2,1)S(1)}, u32[]{:S(2)}, u32[]{:S(2)}) collective-permute-start(bf16[24,768]{1,0:T(8,128)(2,1)S(1)} %fusion.37), channel_id=1, source_target_pairs={{0,2},{1,3},{2,0},{3,1},{4,6},{5,7},{6,4},{7,5},{8,10},{9,11},{10,... | collective-permute-start | bytes 110600 | tf_op jit(solution)/shard_map/ppermute | solution.py:37
  19.6 6.2 %collective-permute-start.3 = (bf16[48,768]{1,0:T(8,128)(2,1)S(1)}, bf16[48,768]{1,0:T(8,128)(2,1)S(1)}, u32[]{:S(2)}, u32[]{:S(2)}) collective-permute-start(bf16[48,768]{1,0:T(8,128)(2,1)S(1)} %pad_maximum_fusion.6), channel_id=1, source_target_pairs={{0,24},{1,25},{2,26},{3,27},{4,28},{5,29},{6,30},{7,31},{8,16},{9,... | collective-permute-start | bytes 221192 | tf_op jit(solution)/shard_map/ppermute | solution.py:37
  22.2 5.7 %collective-permute-start.1 = (bf16[48,768]{1,0:T(8,128)(2,1)S(1)}, bf16[48,768]{1,0:T(8,128)(2,1)S(1)}, u32[]{:S(2)}, u32[]{:S(2)}) collective-permute-start(bf16[48,768]{1,0:T(8,128)(2,1)S(1)} %pad_maximum_fusion.5), channel_id=1, source_target_pairs={{0,4},{1,5},{2,6},{3,7},{4,0},{5,1},{6,2},{7,3},{8,12},{9,13},{10,... | collective-permute-start | bytes 221192 | tf_op jit(solution)/shard_map/ppermute | solution.py:37
  27.9 7.4 %collective-permute-start.4 = (bf16[96,768]{1,0:T(8,128)(2,1)S(1)}, bf16[96,768]{1,0:T(8,128)(2,1)S(1)}, u32[]{:S(2)}, u32[]{:S(2)}) collective-permute-start(bf16[96,768]{1,0:T(8,128)(2,1)S(1)} %pad_maximum_fusion.3), channel_id=1, source_target_pairs={{0,8},{1,9},{2,10},{3,11},{4,12},{5,13},{6,14},{7,15},{8,0},{9,1},... | collective-permute-start | bytes 442376 | tf_op jit(solution)/shard_map/ppermute | solution.py:37
  28.0 5.2 %collective-permute-start.7 = (bf16[96,768]{1,0:T(8,128)(2,1)S(1)}, bf16[96,768]{1,0:T(8,128)(2,1)S(1)}, u32[]{:S(2)}, u32[]{:S(2)}) collective-permute-start(bf16[96,768]{1,0:T(8,128)(2,1)S(1)} %pad_maximum_fusion.4), channel_id=1, source_target_pairs={{0,2},{1,3},{2,0},{3,1},{4,6},{5,7},{6,4},{7,5},{8,10},{9,11},{10,... | collective-permute-start | bytes 442376 | tf_op jit(solution)/shard_map/ppermute | solution.py:37
  33.2 6.8 %collective-permute-start.8 = (bf16[192,768]{1,0:T(8,128)(2,1)S(1)}, bf16[192,768]{1,0:T(8,128)(2,1)S(1)}, u32[]{:S(2)}, u32[]{:S(2)}) collective-permute-start(bf16[192,768]{1,0:T(8,128)(2,1)S(1)} %pad_maximum_fusion.1), channel_id=1, source_target_pairs={{0,4},{1,5},{2,6},{3,7},{4,0},{5,1},{6,2},{7,3},{8,12},{9,13},{10,... | collective-permute-start | bytes 884744 | tf_op jit(solution)/shard_map/ppermute | solution.py:37
  35.3 8.7 %collective-permute-start.5 = (bf16[192,768]{1,0:T(8,128)(2,1)S(1)}, bf16[192,768]{1,0:T(8,128)(2,1)S(1)}, u32[]{:S(2)}, u32[]{:S(2)}) collective-permute-start(bf16[192,768]{1,0:T(8,128)(2,1)S(1)} %pad_maximum_fusion), channel_id=1, source_target_pairs={{0,24},{1,25},{2,26},{3,27},{4,28},{5,29},{6,30},{7,31},{8,16},{9,... | collective-permute-start | bytes 884744 | tf_op jit(solution)/shard_map/ppermute | solution.py:37
  40.0 6.1 %copy-start = (bf16[384,768]{1,0:T(8,128)(2,1)}, bf16[384,768]{1,0:T(8,128)(2,1)S(1)}, u32[]{:S(2)}) copy-start(bf16[384,768]{1,0:T(8,128)(2,1)S(1)} %constant_dynamic-update-slice_fusion.3.wb0) | copy-start | bytes 1769476
  40.0 4.9 %collective-permute-start.9 = (bf16[384,768]{1,0:T(8,128)(2,1)S(1)}, bf16[384,768]{1,0:T(8,128)(2,1)S(1)}, u32[]{:S(2)}, u32[]{:S(2)}) collective-permute-start(bf16[384,768]{1,0:T(8,128)(2,1)S(1)} %constant_dynamic-update-slice_fusion.3.wb0), channel_id=1, source_target_pairs={{0,1},{1,0},{2,3},{3,2},{4,5},{5,4},{6,7},{7,6},{8,9},{9,8},{10,11... | collective-permute-start | bytes 1769480 | tf_op jit(solution)/shard_map/ppermute | solution.py:37
  44.0 2.1 copy-start.2
  44.0 2.1 collective-permute-start.6
  45.0 1.1 copy-start.1
  46.1 0.8 copy-start.3
  46.9 7.8 %copy-start.15 = (f32[576]{0:T(1024)S(1)}, f32[576]{0:T(1024)}, u32[]{:S(2)}) copy-start(f32[576]{0:T(1024)} %param.21) | copy-start | bytes 6916
  51.7 7.4 %collective-permute-start.10 = (bf16[384,384]{1,0:T(8,128)(2,1)}, bf16[384,384]{1,0:T(8,128)(2,1)S(1)}, u32[]{:S(2)}, u32[]{:S(2)}) collective-permute-start(bf16[384,384]{1,0:T(8,128)(2,1)} %get-tuple-element.62.own), channel_id=1, source_target_pairs={{0,1},{1,2},{2,3},{3,4},{4,5},{5,6},{6,7},{7,8},{8,9},{9,10},{10,1... | collective-permute-start | bytes 884744 | tf_op jit(solution)/shard_map/ppermute | solution.py:25
  59.1 0.7 copy-start.6
  116.9 9.7 %copy-start.7 = (bf16[768,576]{1,0:T(8,128)(2,1)S(1)}, bf16[768,576]{1,0:T(8,128)(2,1)}, u32[]{:S(2)}) copy-start(bf16[768,576]{1,0:T(8,128)(2,1)} %get-tuple-element.96) | copy-start | bytes 2654212
  125.3 3.7 %collective-permute-start.11 = (bf16[384,384]{1,0:T(8,128)(2,1)}, bf16[384,384]{1,0:T(8,128)(2,1)S(1)}, u32[]{:S(2)}, u32[]{:S(2)}) collective-permute-start(bf16[384,384]{1,0:T(8,128)(2,1)} %get-tuple-element.80), channel_id=1, source_target_pairs={{1,0},{2,1},{3,2},{4,3},{5,4},{6,5},{7,6},{8,7},{9,8},{10,9},{11,1... | collective-permute-start | bytes 884744 | tf_op jit(solution)/shard_map/ppermute | solution.py:25
  127.4 17.2 %collective-permute-start.32 = (bf16[768,576]{0,1:T(8,128)(2,1)S(1)}, bf16[768,576]{0,1:T(8,128)(2,1)}, u32[]{:S(2)}, u32[]{:S(2)}) collective-permute-start(bf16[768,576]{0,1:T(8,128)(2,1)S(1)} %copy.42), channel_id=1, source_target_pairs={{0,1},{1,0},{2,3},{3,2},{4,5},{5,4},{6,7},{7,6},{8,9},{9,8},{10,11... | collective-permute-start | bytes 2654216 | tf_op jit(solution)/shard_map/ppermute | solution.py:37
  129.0 0.7 copy-start.10
  137.7 6.6 %copy-start.9 = (bf16[384,768]{1,0:T(8,128)(2,1)S(1)}, bf16[384,768]{1,0:T(8,128)(2,1)}, u32[]{:S(2)}) copy-start(bf16[384,768]{1,0:T(8,128)(2,1)} %get-tuple-element.89) | copy-start | bytes 1769476
  137.7 6.7 %collective-permute-start.12 = (bf16[384,768]{1,0:T(8,128)(2,1)}, bf16[384,768]{1,0:T(8,128)(2,1)S(1)}, u32[]{:S(2)}, u32[]{:S(2)}) collective-permute-start(bf16[384,768]{1,0:T(8,128)(2,1)} %get-tuple-element.88), channel_id=1, source_target_pairs={{0,1},{1,0},{2,3},{3,2},{4,5},{5,4},{6,7},{7,6},{8,9},{9,8},{10,11... | collective-permute-start | bytes 1769480 | tf_op jit(solution)/shard_map/ppermute | solution.py:37
  142.6 23.6 %collective-permute-start.22 = (bf16[384,1536]{1,0:T(8,128)(2,1)}, bf16[384,1536]{1,0:T(8,128)(2,1)}, u32[]{:S(2)}, u32[]{:S(2)}) collective-permute-start(bf16[384,1536]{1,0:T(8,128)(2,1)} %get-tuple-element.92), channel_id=1, source_target_pairs={{0,1},{1,0},{2,3},{3,2},{4,5},{5,4},{6,7},{7,6},{8,9},{9,8},{10,11... | collective-permute-start | bytes 3538952 | tf_op jit(solution)/shard_map/ppermute | solution.py:37
  142.7 26.0 %collective-permute-start.27 = (bf16[384,1536]{1,0:T(8,128)(2,1)}, bf16[384,1536]{1,0:T(8,128)(2,1)}, u32[]{:S(2)}, u32[]{:S(2)}) collective-permute-start(bf16[384,1536]{1,0:T(8,128)(2,1)} %get-tuple-element.94), channel_id=1, source_target_pairs={{0,1},{1,0},{2,3},{3,2},{4,5},{5,4},{6,7},{7,6},{8,9},{9,8},{10,11... | collective-permute-start | bytes 3538952 | tf_op jit(solution)/shard_map/ppermute | solution.py:37
  143.1 5.7 %collective-permute-start.17 = (bf16[384,768]{1,0:T(8,128)(2,1)}, bf16[384,768]{1,0:T(8,128)(2,1)}, u32[]{:S(2)}, u32[]{:S(2)}) collective-permute-start(bf16[384,768]{1,0:T(8,128)(2,1)} %get-tuple-element.90), channel_id=1, source_target_pairs={{0,1},{1,0},{2,3},{3,2},{4,5},{5,4},{6,7},{7,6},{8,9},{9,8},{10,11... | collective-permute-start | bytes 1769480 | tf_op jit(solution)/shard_map/ppermute | solution.py:37
  146.4 5.1 %copy-start.8 = (bf16[768,576]{1,0:T(8,128)(2,1)S(1)}, bf16[768,576]{1,0:T(8,128)(2,1)}, u32[]{:S(2)}) copy-start(bf16[768,576]{1,0:T(8,128)(2,1)} %get-tuple-element.95) | copy-start | bytes 2654212
  146.4 11.8 %collective-permute-start.13 = (bf16[192,768]{1,0:T(8,128)(2,1)S(1)}, bf16[192,768]{1,0:T(8,128)(2,1)S(1)}, u32[]{:S(2)}, u32[]{:S(2)}) collective-permute-start(bf16[192,768]{1,0:T(8,128)(2,1)S(1)} %get-tuple-element.107), channel_id=1, source_target_pairs={{0,24},{1,25},{2,26},{3,27},{4,28},{5,29},{6,30},{7,31},{8,16},{9,... | collective-permute-start | bytes 884744 | tf_op jit(solution)/shard_map/ppermute | solution.py:37
  150.0 13.7 %collective-permute-start.18 = (bf16[192,768]{1,0:T(8,128)(2,1)S(1)}, bf16[192,768]{1,0:T(8,128)(2,1)S(1)}, u32[]{:S(2)}, u32[]{:S(2)}) collective-permute-start(bf16[192,768]{1,0:T(8,128)(2,1)S(1)} %get-tuple-element.105), channel_id=1, source_target_pairs={{0,4},{1,5},{2,6},{3,7},{4,0},{5,1},{6,2},{7,3},{8,12},{9,13},{10,... | collective-permute-start | bytes 884744 | tf_op jit(solution)/shard_map/ppermute | solution.py:37
  151.7 20.7 %collective-permute-start.33 = (bf16[384,576]{1,0:T(8,128)(2,1)S(1)}, bf16[384,576]{1,0:T(8,128)(2,1)S(1)}, u32[]{:S(2)}, u32[]{:S(2)}) collective-permute-start(bf16[384,576]{1,0:T(8,128)(2,1)S(1)} %get-tuple-element.111), channel_id=1, source_target_pairs={{0,8},{1,9},{2,10},{3,11},{4,12},{5,13},{6,14},{7,15},{8,0},{9,1},... | collective-permute-start | bytes 1327112 | tf_op jit(solution)/shard_map/ppermute | solution.py:37
  158.2 8.0 %copy-start.5 = (bf16[384,1536]{1,0:T(8,128)(2,1)S(1)}, bf16[384,1536]{1,0:T(8,128)(2,1)}, u32[]{:S(2)}) copy-start(bf16[384,1536]{1,0:T(8,128)(2,1)} %get-tuple-element.91) | copy-start | bytes 3538948
  158.3 14.9 %collective-permute-start.14 = (bf16[96,768]{1,0:T(8,128)(2,1)S(1)}, bf16[96,768]{1,0:T(8,128)(2,1)S(1)}, u32[]{:S(2)}, u32[]{:S(2)}) collective-permute-start(bf16[96,768]{1,0:T(8,128)(2,1)S(1)} %get-tuple-element.121), channel_id=1, source_target_pairs={{0,8},{1,9},{2,10},{3,11},{4,12},{5,13},{6,14},{7,15},{8,0},{9,1},... | collective-permute-start | bytes 442376 | tf_op jit(solution)/shard_map/ppermute | solution.py:37
  163.8 10.9 %collective-permute-start.19 = (bf16[96,768]{1,0:T(8,128)(2,1)S(1)}, bf16[96,768]{1,0:T(8,128)(2,1)S(1)}, u32[]{:S(2)}, u32[]{:S(2)}) collective-permute-start(bf16[96,768]{1,0:T(8,128)(2,1)S(1)} %get-tuple-element.119), channel_id=1, source_target_pairs={{0,2},{1,3},{2,0},{3,1},{4,6},{5,7},{6,4},{7,5},{8,10},{9,11},{10,... | collective-permute-start | bytes 442376 | tf_op jit(solution)/shard_map/ppermute | solution.py:37
  166.2 2.5 %copy-start.4 = (bf16[384,1536]{1,0:T(8,128)(2,1)S(1)}, bf16[384,1536]{1,0:T(8,128)(2,1)}, u32[]{:S(2)}) copy-start(bf16[384,1536]{1,0:T(8,128)(2,1)} %get-tuple-element.93) | copy-start | bytes 3538948
  168.6 42.3 %collective-permute-start.23 = (bf16[192,1536]{1,0:T(8,128)(2,1)}, bf16[192,1536]{1,0:T(8,128)(2,1)}, u32[]{:S(2)}, u32[]{:S(2)}) collective-permute-start(bf16[192,1536]{1,0:T(8,128)(2,1)} %get-tuple-element.97), channel_id=1, source_target_pairs={{0,2},{1,3},{2,0},{3,1},{4,6},{5,7},{6,4},{7,5},{8,10},{9,11},{10,... | collective-permute-start | bytes 1769480 | tf_op jit(solution)/shard_map/ppermute | solution.py:37
  171.0 42.9 %collective-permute-start.28 = (bf16[192,1536]{1,0:T(8,128)(2,1)}, bf16[192,1536]{1,0:T(8,128)(2,1)S(1)}, u32[]{:S(2)}, u32[]{:S(2)}) collective-permute-start(bf16[192,1536]{1,0:T(8,128)(2,1)} %get-tuple-element.99), channel_id=1, source_target_pairs={{0,4},{1,5},{2,6},{3,7},{4,0},{5,1},{6,2},{7,3},{8,12},{9,13},{10,... | collective-permute-start | bytes 1769480 | tf_op jit(solution)/shard_map/ppermute | solution.py:37
  172.6 25.6 %collective-permute-start.34 = (bf16[192,576]{1,0:T(8,128)(2,1)S(1)}, bf16[192,576]{1,0:T(8,128)(2,1)S(1)}, u32[]{:S(2)}, u32[]{:S(2)}) collective-permute-start(bf16[192,576]{1,0:T(8,128)(2,1)S(1)} %get-tuple-element.109), channel_id=1, source_target_pairs={{0,4},{1,5},{2,6},{3,7},{4,0},{5,1},{6,2},{7,3},{8,12},{9,13},{10,... | collective-permute-start | bytes 663560 | tf_op jit(solution)/shard_map/ppermute | solution.py:37
  173.2 19.1 %collective-permute-start.15 = (bf16[48,768]{1,0:T(8,128)(2,1)S(1)}, bf16[48,768]{1,0:T(8,128)(2,1)S(1)}, u32[]{:S(2)}, u32[]{:S(2)}) collective-permute-start(bf16[48,768]{1,0:T(8,128)(2,1)S(1)} %get-tuple-element.127), channel_id=1, source_target_pairs={{0,4},{1,5},{2,6},{3,7},{4,0},{5,1},{6,2},{7,3},{8,12},{9,13},{10,... | collective-permute-start | bytes 221192 | tf_op jit(solution)/shard_map/ppermute | solution.py:37
  174.8 19.3 %collective-permute-start.20 = (bf16[48,768]{1,0:T(8,128)(2,1)S(1)}, bf16[48,768]{1,0:T(8,128)(2,1)S(1)}, u32[]{:S(2)}, u32[]{:S(2)}) collective-permute-start(bf16[48,768]{1,0:T(8,128)(2,1)S(1)} %get-tuple-element.125), channel_id=1, source_target_pairs={{0,24},{1,25},{2,26},{3,27},{4,28},{5,29},{6,30},{7,31},{8,16},{9,... | collective-permute-start | bytes 221192 | tf_op jit(solution)/shard_map/ppermute | solution.py:37
  192.3 4.0 %collective-permute-start.16 = (bf16[24,768]{1,0:T(8,128)(2,1)S(1)}, bf16[24,768]{1,0:T(8,128)(2,1)S(1)}, u32[]{:S(2)}, u32[]{:S(2)}) collective-permute-start(bf16[24,768]{1,0:T(8,128)(2,1)S(1)} %fusion.30), channel_id=1, source_target_pairs={{0,2},{1,3},{2,0},{3,1},{4,6},{5,7},{6,4},{7,5},{8,10},{9,11},{10,... | collective-permute-start | bytes 110600 | tf_op jit(solution)/shard_map/ppermute | solution.py:37
  194.1 4.0 %collective-permute-start.21 = (bf16[24,768]{1,0:T(8,128)(2,1)S(1)}, bf16[24,768]{1,0:T(8,128)(2,1)S(1)}, u32[]{:S(2)}, u32[]{:S(2)}) collective-permute-start(bf16[24,768]{1,0:T(8,128)(2,1)S(1)} %fusion.27), channel_id=1, source_target_pairs={{0,8},{1,9},{2,10},{3,11},{4,12},{5,13},{6,14},{7,15},{8,0},{9,1},... | collective-permute-start | bytes 110600 | tf_op jit(solution)/shard_map/ppermute | solution.py:37
  198.2 4.9 %collective-permute-start.35 = (bf16[96,576]{1,0:T(8,128)(2,1)S(1)}, bf16[96,576]{1,0:T(8,128)(2,1)S(1)}, u32[]{:S(2)}, u32[]{:S(2)}) collective-permute-start(bf16[96,576]{1,0:T(8,128)(2,1)S(1)} %get-tuple-element.123), channel_id=1, source_target_pairs={{0,2},{1,3},{2,0},{3,1},{4,6},{5,7},{6,4},{7,5},{8,10},{9,11},{10,... | collective-permute-start | bytes 331784 | tf_op jit(solution)/shard_map/ppermute | solution.py:37
  203.8 6.3 %collective-permute-start.36 = (bf16[48,576]{1,0:T(8,128)(2,1)}, bf16[48,576]{1,0:T(8,128)(2,1)S(1)}, u32[]{:S(2)}, u32[]{:S(2)}) collective-permute-start(bf16[48,576]{1,0:T(8,128)(2,1)} %fusion.25), channel_id=1, source_target_pairs={{0,24},{1,25},{2,26},{3,27},{4,28},{5,29},{6,30},{7,31},{8,16},{9,... | collective-permute-start | bytes 165896 | tf_op jit(solution)/shard_map/ppermute | solution.py:37
  212.1 10.2 %collective-permute-start.24 = (bf16[96,1536]{1,0:T(8,128)(2,1)S(1)}, bf16[96,1536]{1,0:T(8,128)(2,1)S(1)}, u32[]{:S(2)}, u32[]{:S(2)}) collective-permute-start(bf16[96,1536]{1,0:T(8,128)(2,1)S(1)} %get-tuple-element.101), channel_id=1, source_target_pairs={{0,24},{1,25},{2,26},{3,27},{4,28},{5,29},{6,30},{7,31},{8,16},{9,... | collective-permute-start | bytes 884744 | tf_op jit(solution)/shard_map/ppermute | solution.py:37
  214.0 8.3 %collective-permute-start.29 = (bf16[96,1536]{1,0:T(8,128)(2,1)S(1)}, bf16[96,1536]{1,0:T(8,128)(2,1)S(1)}, u32[]{:S(2)}, u32[]{:S(2)}) collective-permute-start(bf16[96,1536]{1,0:T(8,128)(2,1)S(1)} %get-tuple-element.103), channel_id=1, source_target_pairs={{0,2},{1,3},{2,0},{3,1},{4,6},{5,7},{6,4},{7,5},{8,10},{9,11},{10,... | collective-permute-start | bytes 884744 | tf_op jit(solution)/shard_map/ppermute | solution.py:37
  222.3 5.2 %collective-permute-start.25 = (bf16[48,1536]{1,0:T(8,128)(2,1)S(1)}, bf16[48,1536]{1,0:T(8,128)(2,1)S(1)}, u32[]{:S(2)}, u32[]{:S(2)}) collective-permute-start(bf16[48,1536]{1,0:T(8,128)(2,1)S(1)} %get-tuple-element.115), channel_id=1, source_target_pairs={{0,8},{1,9},{2,10},{3,11},{4,12},{5,13},{6,14},{7,15},{8,0},{9,1},... | collective-permute-start | bytes 442376 | tf_op jit(solution)/shard_map/ppermute | solution.py:37
  222.5 9.5 %collective-permute-start.30 = (bf16[48,1536]{1,0:T(8,128)(2,1)S(1)}, bf16[48,1536]{1,0:T(8,128)(2,1)S(1)}, u32[]{:S(2)}, u32[]{:S(2)}) collective-permute-start(bf16[48,1536]{1,0:T(8,128)(2,1)S(1)} %get-tuple-element.117), channel_id=1, source_target_pairs={{0,24},{1,25},{2,26},{3,27},{4,28},{5,29},{6,30},{7,31},{8,16},{9,... | collective-permute-start | bytes 442376 | tf_op jit(solution)/shard_map/ppermute | solution.py:37
  227.5 6.8 %collective-permute-start.26 = (bf16[24,1536]{1,0:T(8,128)(2,1)S(1)}, bf16[24,1536]{1,0:T(8,128)(2,1)S(1)}, u32[]{:S(2)}, u32[]{:S(2)}) collective-permute-start(bf16[24,1536]{1,0:T(8,128)(2,1)S(1)} %get-tuple-element.129), channel_id=1, source_target_pairs={{0,4},{1,5},{2,6},{3,7},{4,0},{5,1},{6,2},{7,3},{8,12},{9,13},{10,... | collective-permute-start | bytes 221192 | tf_op jit(solution)/shard_map/ppermute | solution.py:37
  232.0 4.4 %collective-permute-start.31 = (bf16[24,1536]{1,0:T(8,128)(2,1)S(1)}, bf16[24,1536]{1,0:T(8,128)(2,1)S(1)}, u32[]{:S(2)}, u32[]{:S(2)}) collective-permute-start(bf16[24,1536]{1,0:T(8,128)(2,1)S(1)} %get-tuple-element.131), channel_id=1, source_target_pairs={{0,8},{1,9},{2,10},{3,11},{4,12},{5,13},{6,14},{7,15},{8,0},{9,1},... | collective-permute-start | bytes 221192 | tf_op jit(solution)/shard_map/ppermute | solution.py:37
Sparse Core Ops, SparseCore 0:
  11.5 80.0 all-gather.1

commit v4 on v3

--- a/solution.py
+++ b/solution.py
@@ -525,6 +525,7 @@
     tall_wide_g,
     tall_wide_u,
     wall,
+    wd,
     mixed_out,
     dgate,
     dup,
@@ -535,17 +536,10 @@
     du_high,
     dd_high,
     act,
-    wd,
+    dd,
 ):
     count = slots.shape[0]
     rows_d = FF // count
-    fold = rows_d // 2
-    for j in range(count):
-        for k in range(2):
-            at = 2 * FF + k * FOLD_LANES
-            wd[j * rows_d + k * fold : j * rows_d + (k + 1) * fold, :] = wall[
-                j * PAD : j * PAD + fold, at : at + D
-            ]
     cot_tok = cot[...].T
     block = 256
 
@@ -570,11 +564,11 @@
     dg_high[...] = dot_nn(tall_wide_g[half:, :], dgate[...]).astype(bf16)
     du_low[...] = dot_nn(tall_wide_u[:half, :], dup[...]).astype(bf16)
     du_high[...] = dot_nn(tall_wide_u[half:, :], dup[...]).astype(bf16)
-    wd[...] = dot_nn(act[...].T, cot_tok).astype(bf16)
+    dd[...] = dot_nn(act[...].T, cot_tok).astype(bf16)
     for p in range(count):
         source = pl.multiple_of(slots[p] * rows_d, rows_d)
         out, at = (dd_low, p) if p < count // 2 else (dd_high, p - count // 2)
-        out[at * rows_d : (at + 1) * rows_d, :] = wd[pl.ds(source, rows_d), :]
+        out[at * rows_d : (at + 1) * rows_d, :] = dd[pl.ds(source, rows_d), :]
 
 
 def feed_back_kernel(
@@ -790,6 +784,11 @@
         [q_t, near, kv_t, positions[None]],
     )
     wide = count * PAD
+    folds = []
+    for k in range(2):
+        at = 2 * FF + k * FOLD_LANES
+        folds.append(wall[:, at : at + D].reshape(count, PAD, D)[:, : per_d // 2])
+    wd = jnp.concatenate(folds, axis=1).reshape(FF, D)
     tall_shape = ((wide, row_count), bf16)
     residual, wide_n, tall_wide_g, tall_wide_u, wide_a, wide_b, wide_att = call_whole(
         prepare_kernel,
@@ -805,7 +804,7 @@
             ((row_count, FF), bf16),
         ]
         + [((wide // 2, FF), bf16), ((wide // 2, FF), bf16), ((FF // 2, D), bf16)] * 2,
-        [residual, cot_t, wide_n, tall_wide_g, tall_wide_u, wall],
+        [residual, cot_t, wide_n, tall_wide_g, tall_wide_u, wall, wd],
         scratch=[pltpu.VMEM((row_count, FF), bf16), pltpu.VMEM((FF, D), bf16)],
         scalars=[slots],
     )

time: 248 us -> 252 us (1.016)
  no operation moved by 1% of the time
where the time goes in v4:
time: 252 us; the launch traced here: 248 us
  waiting for transfers between devices  75.6 us (30%)
  Pallas kernels  66.9 us (27%)
  starting transfers between devices  54.1 us (21%)
  local copies, waits for them, and re-layouts  22.5 us (9%)
  between operations  14.8 us (6%)
  other arithmetic  14.2 us (6%)
    pallas_call x7, Pallas kernels, call_whole(): pl.pallas_call(kernel, out_shape=[jax.ShapeDtypeStruct(s, d) for s, d in...  66.9 us
    ppermute x35, waiting for transfers between devices, swapped(): return lax.ppermute(value, 'dev', [(i, i ^ mask) for i in range(count)])  63.4 us
    ppermute x35, starting transfers between devices, swapped(): return lax.ppermute(value, 'dev', [(i, i ^ mask) for i in range(count)])  50.3 us
    all_gather x1, waiting for transfers between devices, shards(): wall = lax.all_gather(stream_ffn, 'dev', axis=0, tiled=True)  11.9 us
    convert_element_type x20, other arithmetic, step_halve(): high.append((k[half:].astype(f32) + g[half:].astype(f32)).astype(bf16))  8.67 us
  transfers between devices with their start and end apart: 38, of which 18 were waited for; matrix products, arithmetic and copies ran while one was open for 11% of the time, Pallas kernels for 13%

profile of v4, /device:TPU:0, one launch (start us, length us, event | category | flops | bytes accessed | tf_op | source)
XLA Modules:
  0.0 248.1 jit_solution(6528091465498865445)
XLA Ops:
  7.3 0.9 reshape.341
  8.3 1.0 reshape.340
  11.0 3.1 %collective-permute-start.2 = (bf16[24,768]{1,0:T(8,128)(2,1)S(1)}, bf16[24,768]{1,0:T(8,128)(2,1)S(1)}, u32[]{:S(2)}, u32[]{:S(2)}) collective-permute-start(bf16[24,768]{1,0:T(8,128)(2,1)S(1)} %fusion.38), channel_id=1, source_target_pairs={{0,8},{1,9},{2,10},{3,11},{4,12},{5,13},{6,14},{7,15},{8,0},{9,1},... | collective-permute-start | bytes 110600 | tf_op jit(solution)/shard_map/ppermute | solution.py:37
  14.2 1.5 collective-permute-start
  15.9 0.9 multiply_sine_fusion
  19.6 2.5 %collective-permute-start.3 = (bf16[48,768]{1,0:T(8,128)(2,1)S(1)}, bf16[48,768]{1,0:T(8,128)(2,1)S(1)}, u32[]{:S(2)}, u32[]{:S(2)}) collective-permute-start(bf16[48,768]{1,0:T(8,128)(2,1)S(1)} %pad_maximum_fusion.7), channel_id=1, source_target_pairs={{0,24},{1,25},{2,26},{3,27},{4,28},{5,29},{6,30},{7,31},{8,16},{9,... | collective-permute-start | bytes 221192 | tf_op jit(solution)/shard_map/ppermute | solution.py:37
  22.2 1.6 collective-permute-start.1
  23.8 2.1 collective-permute-done.3
  25.9 2.0 collective-permute-done.1
  28.1 5.1 %collective-permute-done.7 = bf16[96,768]{1,0:T(8,128)(2,1)S(1)} collective-permute-done((bf16[96,768]{1,0:T(8,128)(2,1)S(1)}, bf16[96,768]{1,0:T(8,128)(2,1)S(1)}, u32[]{:S(2)}, u32[]{:S(2)}) %collective-permute-start.7) | collective-permute-done | bytes 147488 | tf_op jit(solution)/shard_map/ppermute | solution.py:37
  33.2 2.0 collective-permute-start.8
  35.9 4.1 %collective-permute-done.8 = bf16[192,768]{1,0:T(8,128)(2,1)S(1)} collective-permute-done((bf16[192,768]{1,0:T(8,128)(2,1)S(1)}, bf16[192,768]{1,0:T(8,128)(2,1)S(1)}, u32[]{:S(2)}, u32[]{:S(2)}) %collective-permute-start.8) | collective-permute-done | bytes 294944 | tf_op jit(solution)/shard_map/ppermute | solution.py:37
  40.1 3.8 %collective-permute-done.5 = bf16[192,768]{1,0:T(8,128)(2,1)S(1)} collective-permute-done((bf16[192,768]{1,0:T(8,128)(2,1)S(1)}, bf16[192,768]{1,0:T(8,128)(2,1)S(1)}, u32[]{:S(2)}, u32[]{:S(2)}) %collective-permute-start.5) | collective-permute-done | bytes 294944 | tf_op jit(solution)/shard_map/ppermute | solution.py:37
  44.1 0.9 copy.33.gain.gain_in
  45.0 1.1 collective-permute-done.6.wa1
  46.1 0.8 copy-done.3
  46.9 4.7 %shard_map.214 = (bf16[576,384]{1,0:T(8,128)(2,1)}, bf16[384,384]{1,0:T(8,128)(2,1)}) custom-call(bf16[576,384]{1,0:T(8,128)(2,1)} %bitcast.12, f32[576,1]{1,0:T(8,128)} %copy.33.gain.gain_in, f32[32,384]{1,0:T(8,128)} %get-tuple-element.55.cos, f32[32,384]{1,0:T(8,128)} %get-tuple-element.56.sin, s32[1,768]{1,0:T(1,128)} %select_n.87.src_a, ...), custom_call_target="tpu_custom_call" | custom-call | tf_op jit(solution)/shard_map/pallas_call | solution.py:677
  51.6 2.5 %collective-permute-start.10 = (bf16[384,384]{1,0:T(8,128)(2,1)}, bf16[384,384]{1,0:T(8,128)(2,1)S(1)}, u32[]{:S(2)}, u32[]{:S(2)}) collective-permute-start(bf16[384,384]{1,0:T(8,128)(2,1)} %get-tuple-element.62.own), channel_id=1, source_target_pairs={{0,1},{1,2},{2,3},{3,4},{4,5},{5,6},{6,7},{7,8},{8,9},{9,10},{10,1... | collective-permute-start | bytes 884744 | tf_op jit(solution)/shard_map/ppermute | solution.py:25
  55.3 1.0 copy.37.tall_a
  56.3 1.0 copy.38.tall_b
  57.2 0.9 copy.35.tall_g
  58.2 0.9 copy.36.tall_u
  59.8 12.2 %shard_map.215 = (bf16[3,3,512,384]{3,2,1,0:T(8,128)(2,1)}, bf16[576,384]{1,0:T(8,128)(2,1)}) custom-call(bf16[576,384]{1,0:T(8,128)(2,1)} %get-tuple-element.61.q, bf16[384,384]{1,0:T(8,128)(2,1)} %copy-done.6, bf16[384,384]{1,0:T(8,128)(2,1)} %get-tuple-element.62.own, s32[1,384]{1,0:T(1,128)} %broadcast_in_dim.57.pos), custom_call_target="tpu_custom_call" | custom-call | tf_op jit(solution)/shard_map/pallas_call | solution.py:677
  72.1 7.8 %shard_map.216 = (f32[384,576]{1,0:T(8,128)}, bf16[384,768]{1,0:T(8,128)(2,1)}, bf16[768,384]{1,0:T(8,128)(2,1)}, bf16[768,384]{1,0:T(8,128)(2,1)}, bf16[768,384...) custom-call(bf16[576,384]{1,0:T(8,128)(2,1)} %get-tuple-element.63.att, ...), custom_call_target="tpu_custom_call" | custom-call | tf_op jit(solution)/shard_map/pallas_call | solution.py:677
  79.9 11.9 %all-gather.2.cloned.1.call-done.wall = bf16[768,4352]{1,0:T(8,128)(2,1)} async-done(((bf16[24,4352]{1,0:T(8,128)(2,1)}), bf16[768,4352]{1,0:T(8,128)(2,1)}) %all-gather.2.cloned.1.call-update) | async-done | bytes 6684688 | tf_op jit(solution)/shard_map/all_gather | solution.py:748
  91.7 1.7 fusion.41
  93.4 1.6 pad_maximum_fusion
  95.0 15.3 %shard_map.217 = (bf16[576,384]{1,0:T(8,128)(2,1)}, bf16[384,1536]{1,0:T(8,128)(2,1)}, bf16[384,1536]{1,0:T(8,128)(2,1)}, bf16[384,1536]{1,0:T(8,128)(2,1)}, bf1...) custom-call(s32[32]{0:T(128)} %broadcast_xor_fusion.slots, ...), custom_call_target="tpu_custom_call" | custom-call | tf_op jit(solution)/shard_map/pallas_call | solution.py:677
  110.3 10.3 %shard_map.218 = (f32[576,384]{1,0:T(8,128)}, bf16[576,384]{1,0:T(8,128)(2,1)}, f32[1,576]{1,0:T(1,128)}) custom-call(f32[384,576]{1,0:T(8,128)} %get-tuple-element.69.residual.residual_in, bf16[576,384]{1,0:T(8,128)(2,1)} %bitcast.18, f32[1,576]{1,0:T(1,128)} %broadcast_in_dim.58.gain, s32[1,768]{1,0:T(1,128)} %select_n.89.src_b.row_b, ...), custom_call_target="tpu_custom_call" | custom-call | tf_op jit(solution)/shard_map/pallas_call | solution.py:677
  120.6 8.4 %shard_map.219 = (bf16[576,384]{1,0:T(8,128)(2,1)}, bf16[384,384]{1,0:T(8,128)(2,1)}, f32[384,384]{1,0:T(8,128)}) custom-call(bf16[576,384]{1,0:T(8,128)(2,1)} %get-tuple-element.61.q, bf16[384,384]{1,0:T(8,128)(2,1)} %copy-done.6, bf16[384,384]{1,0:T(8,128)(2,1)} %get-tuple-element.62.own, bf16[3,3,512,384]{3,2,1,0:T(8,128)(2,1)} %get-tuple-element.74.prob, ...), custom_call_target="tpu_custom_call" | custom-call | tf_op jit(solution)/shard_map/pallas_call | solution.py:677
  129.0 1.3 collective-permute-start.11
  130.3 0.8 copy.42
  131.2 1.2 collective-permute-start.32
  133.4 8.0 %shard_map.220 = (f32[576,384]{1,0:T(8,128)}, bf16[384,768]{1,0:T(8,128)(2,1)}, bf16[384,768]{1,0:T(8,128)(2,1)}, bf16[384,768]{1,0:T(8,128)(2,1)}, bf16[384,768]{1,0:T(8,128)(2,1)}) custom-call(bf16[576,384]{1,0:T(8,128)(2,1)} %get-tuple-element.78.dq, f32[384,384]{1,0:T(8,128)} %get-tuple-element.79.own, bf16[384,384]{1,0:T(8,128)(2,1)} %copy-done.10, ...), custom_call_target="tpu_custom_call" | custom-call | tf_op jit(solution)/shard_map/pallas_call | solution.py:677
  141.5 4.9 %collective-permute-start.12 = (bf16[384,768]{1,0:T(8,128)(2,1)}, bf16[384,768]{1,0:T(8,128)(2,1)S(1)}, u32[]{:S(2)}, u32[]{:S(2)}) collective-permute-start(bf16[384,768]{1,0:T(8,128)(2,1)} %get-tuple-element.88), channel_id=1, source_target_pairs={{0,1},{1,0},{2,3},{3,2},{4,5},{5,4},{6,7},{7,6},{8,9},{9,8},{10,11... | collective-permute-start | bytes 1769480 | tf_op jit(solution)/shard_map/ppermute | solution.py:37
  146.9 1.1 convert_reduce-precision_fusion.1
  148.3 1.2 fusion.42
  150.1 2.5 %collective-permute-start.13 = (bf16[192,768]{1,0:T(8,128)(2,1)S(1)}, bf16[192,768]{1,0:T(8,128)(2,1)S(1)}, u32[]{:S(2)}, u32[]{:S(2)}) collective-permute-start(bf16[192,768]{1,0:T(8,128)(2,1)S(1)} %get-tuple-element.109), channel_id=1, source_target_pairs={{0,24},{1,25},{2,26},{3,27},{4,28},{5,29},{6,30},{7,31},{8,16},{9,... | collective-permute-start | bytes 884744 | tf_op jit(solution)/shard_map/ppermute | solution.py:37
  152.6 1.2 fusion.2
  153.8 1.5 collective-permute-start.18
  155.5 1.6 collective-permute-start.33
  157.1 4.9 %collective-permute-done.13 = bf16[192,768]{1,0:T(8,128)(2,1)S(1)} collective-permute-done((bf16[192,768]{1,0:T(8,128)(2,1)S(1)}, bf16[192,768]{1,0:T(8,128)(2,1)S(1)}, u32[]{:S(2)}, u32[]{:S(2)}) %collective-permute-start.13) | collective-permute-done | bytes 294944 | tf_op jit(solution)/shard_map/ppermute | solution.py:37
  162.0 5.5 %collective-permute-start.14 = (bf16[96,768]{1,0:T(8,128)(2,1)S(1)}, bf16[96,768]{1,0:T(8,128)(2,1)S(1)}, u32[]{:S(2)}, u32[]{:S(2)}) collective-permute-start(bf16[96,768]{1,0:T(8,128)(2,1)S(1)} %get-tuple-element.123), channel_id=1, source_target_pairs={{0,8},{1,9},{2,10},{3,11},{4,12},{5,13},{6,14},{7,15},{8,0},{9,1},... | collective-permute-start | bytes 442376 | tf_op jit(solution)/shard_map/ppermute | solution.py:37
  167.6 2.4 collective-permute-start.19
  170.0 2.4 add_convert_fusion.1
  172.4 2.3 add_convert_fusion
  174.7 1.5 collective-permute-start.28
  176.9 1.6 collective-permute-start.15
  178.6 1.5 collective-permute-start.20
  180.0 16.0 %collective-permute-done.15 = bf16[48,768]{1,0:T(8,128)(2,1)S(1)} collective-permute-done((bf16[48,768]{1,0:T(8,128)(2,1)S(1)}, bf16[48,768]{1,0:T(8,128)(2,1)S(1)}, u32[]{:S(2)}, u32[]{:S(2)}) %collective-permute-start.15) | collective-permute-done | bytes 73760 | tf_op jit(solution)/shard_map/ppermute | solution.py:37
  196.0 1.8 collective-permute-start.16
  198.2 1.9 collective-permute-done.16
  200.7 1.2 collective-permute-done.21
  203.3 3.6 %collective-permute-done.35 = bf16[96,576]{1,0:T(8,128)(2,1)S(1)} collective-permute-done((bf16[96,576]{1,0:T(8,128)(2,1)S(1)}, bf16[96,576]{1,0:T(8,128)(2,1)S(1)}, u32[]{:S(2)}, u32[]{:S(2)}) %collective-permute-start.35) | collective-permute-done | bytes 110624 | tf_op jit(solution)/shard_map/ppermute | solution.py:37
  207.5 1.8 collective-permute-start.36
  211.4 2.4 collective-permute-done.36
  214.6 1.2 fusion.1
  215.8 1.9 collective-permute-start.24
  218.4 7.6 %collective-permute-done.24 = bf16[96,1536]{1,0:T(8,128)(2,1)S(1)} collective-permute-done((bf16[96,1536]{1,0:T(8,128)(2,1)S(1)}, bf16[96,1536]{1,0:T(8,128)(2,1)S(1)}, u32[]{:S(2)}, u32[]{:S(2)}) %collective-permute-start.24) | collective-permute-done | bytes 294944 | tf_op jit(solution)/shard_map/ppermute | solution.py:37
  226.2 1.7 collective-permute-start.30
  227.9 3.3 %collective-permute-done.25 = bf16[48,1536]{1,0:T(8,128)(2,1)S(1)} collective-permute-done((bf16[48,1536]{1,0:T(8,128)(2,1)S(1)}, bf16[48,1536]{1,0:T(8,128)(2,1)S(1)}, u32[]{:S(2)}, u32[]{:S(2)}) %collective-permute-start.25) | collective-permute-done | bytes 147488 | tf_op jit(solution)/shard_map/ppermute | solution.py:37
  231.3 4.5 %collective-permute-start.26 = (bf16[24,1536]{1,0:T(8,128)(2,1)S(1)}, bf16[24,1536]{1,0:T(8,128)(2,1)S(1)}, u32[]{:S(2)}, u32[]{:S(2)}) collective-permute-start(bf16[24,1536]{1,0:T(8,128)(2,1)S(1)} %get-tuple-element.131), channel_id=1, source_target_pairs={{0,4},{1,5},{2,6},{3,7},{4,0},{5,1},{6,2},{7,3},{8,12},{9,13},{10,... | collective-permute-start | bytes 221192 | tf_op jit(solution)/shard_map/ppermute | solution.py:37
  235.9 2.2 collective-permute-done.26
  238.2 2.1 collective-permute-done.31
  (152 shorter events, 19.3 us)
Async XLA Ops:
  7.2 8.6 %copy-start.18 = (s32[32]{0:T(128)S(1)}, s32[32]{0:T(128)}, u32[]{:S(2)}) copy-start(s32[32]{0:T(128)} %constant.22.clone) | copy-start | bytes 388
  7.2 8.6 %copy-start.16 = (s32[32]{0:T(128)S(1)}, s32[32]{0:T(128)}, u32[]{:S(2)}) copy-start(s32[32]{0:T(128)} %constant.24.clone) | copy-start | bytes 388
  7.2 8.6 %copy-start.17 = (s32[32]{0:T(128)S(1)}, s32[32]{0:T(128)}, u32[]{:S(2)}) copy-start(s32[32]{0:T(128)} %constant.23.clone) | copy-start | bytes 388
  7.2 9.5 %copy-start.19 = (s32[32]{0:T(128)S(1)}, s32[32]{0:T(128)}, u32[]{:S(2)}) copy-start(s32[32]{0:T(128)} %constant.25.clone) | copy-start | bytes 388
  7.2 3.5 %copy-start.11 = (bf16[10368]{0:T(1024)(128)(2,1)S(1)}, bf16[10368]{0:T(1024)(128)(2,1)}, u32[]{:S(2)}) copy-start(bf16[10368]{0:T(1024)(128)(2,1)} %param.20) | copy-start | bytes 62212
  7.2 6.8 %copy-start.12 = (bf16[10368]{0:T(1024)(128)(2,1)S(1)}, bf16[10368]{0:T(1024)(128)(2,1)}, u32[]{:S(2)}) copy-start(bf16[10368]{0:T(1024)(128)(2,1)} %param.18) | copy-start | bytes 62212
  7.2 8.5 %copy-start.13 = (s32[384]{0:T(512)S(1)}, s32[384]{0:T(512)}, u32[]{:S(2)}) copy-start(s32[384]{0:T(512)} %param.16) | copy-start | bytes 4612
  7.3 11.6 %copy-start.14 = (f32[576]{0:T(1024)S(1)}, f32[576]{0:T(1024)}, u32[]{:S(2)}) copy-start(f32[576]{0:T(1024)} %param.17) | copy-start | bytes 6916
  7.3 84.5 %all-gather.2.cloned.1.call-start = ((), (), s32[]{:S(2)}) async-start(), calls=%async_computation | async-start | bytes 6893568 | tf_op jit(solution)/shard_map/all_gather | solution.py:748
  11.0 8.7 %collective-permute-start.2 = (bf16[24,768]{1,0:T(8,128)(2,1)S(1)}, bf16[24,768]{1,0:T(8,128)(2,1)S(1)}, u32[]{:S(2)}, u32[]{:S(2)}) collective-permute-start(bf16[24,768]{1,0:T(8,128)(2,1)S(1)} %fusion.38), channel_id=1, source_target_pairs={{0,8},{1,9},{2,10},{3,11},{4,12},{5,13},{6,14},{7,15},{8,0},{9,1},... | collective-permute-start | bytes 110600 | tf_op jit(solution)/shard_map/ppermute | solution.py:37
  14.2 8.0 %collective-permute-start = (bf16[24,768]{1,0:T(8,128)(2,1)S(1)}, bf16[24,768]{1,0:T(8,128)(2,1)S(1)}, u32[]{:S(2)}, u32[]{:S(2)}) collective-permute-start(bf16[24,768]{1,0:T(8,128)(2,1)S(1)} %fusion.37), channel_id=1, source_target_pairs={{0,2},{1,3},{2,0},{3,1},{4,6},{5,7},{6,4},{7,5},{8,10},{9,11},{10,... | collective-permute-start | bytes 110600 | tf_op jit(solution)/shard_map/ppermute | solution.py:37
  19.6 6.2 %collective-permute-start.3 = (bf16[48,768]{1,0:T(8,128)(2,1)S(1)}, bf16[48,768]{1,0:T(8,128)(2,1)S(1)}, u32[]{:S(2)}, u32[]{:S(2)}) collective-permute-start(bf16[48,768]{1,0:T(8,128)(2,1)S(1)} %pad_maximum_fusion.7), channel_id=1, source_target_pairs={{0,24},{1,25},{2,26},{3,27},{4,28},{5,29},{6,30},{7,31},{8,16},{9,... | collective-permute-start | bytes 221192 | tf_op jit(solution)/shard_map/ppermute | solution.py:37
  22.2 5.7 %collective-permute-start.1 = (bf16[48,768]{1,0:T(8,128)(2,1)S(1)}, bf16[48,768]{1,0:T(8,128)(2,1)S(1)}, u32[]{:S(2)}, u32[]{:S(2)}) collective-permute-start(bf16[48,768]{1,0:T(8,128)(2,1)S(1)} %pad_maximum_fusion.6), channel_id=1, source_target_pairs={{0,4},{1,5},{2,6},{3,7},{4,0},{5,1},{6,2},{7,3},{8,12},{9,13},{10,... | collective-permute-start | bytes 221192 | tf_op jit(solution)/shard_map/ppermute | solution.py:37
  27.9 7.3 %collective-permute-start.4 = (bf16[96,768]{1,0:T(8,128)(2,1)S(1)}, bf16[96,768]{1,0:T(8,128)(2,1)S(1)}, u32[]{:S(2)}, u32[]{:S(2)}) collective-permute-start(bf16[96,768]{1,0:T(8,128)(2,1)S(1)} %pad_maximum_fusion.4), channel_id=1, source_target_pairs={{0,8},{1,9},{2,10},{3,11},{4,12},{5,13},{6,14},{7,15},{8,0},{9,1},... | collective-permute-start | bytes 442376 | tf_op jit(solution)/shard_map/ppermute | solution.py:37
  28.0 5.2 %collective-permute-start.7 = (bf16[96,768]{1,0:T(8,128)(2,1)S(1)}, bf16[96,768]{1,0:T(8,128)(2,1)S(1)}, u32[]{:S(2)}, u32[]{:S(2)}) collective-permute-start(bf16[96,768]{1,0:T(8,128)(2,1)S(1)} %pad_maximum_fusion.5), channel_id=1, source_target_pairs={{0,2},{1,3},{2,0},{3,1},{4,6},{5,7},{6,4},{7,5},{8,10},{9,11},{10,... | collective-permute-start | bytes 442376 | tf_op jit(solution)/shard_map/ppermute | solution.py:37
  33.2 6.8 %collective-permute-start.8 = (bf16[192,768]{1,0:T(8,128)(2,1)S(1)}, bf16[192,768]{1,0:T(8,128)(2,1)S(1)}, u32[]{:S(2)}, u32[]{:S(2)}) collective-permute-start(bf16[192,768]{1,0:T(8,128)(2,1)S(1)} %pad_maximum_fusion.2), channel_id=1, source_target_pairs={{0,4},{1,5},{2,6},{3,7},{4,0},{5,1},{6,2},{7,3},{8,12},{9,13},{10,... | collective-permute-start | bytes 884744 | tf_op jit(solution)/shard_map/ppermute | solution.py:37
  35.3 8.7 %collective-permute-start.5 = (bf16[192,768]{1,0:T(8,128)(2,1)S(1)}, bf16[192,768]{1,0:T(8,128)(2,1)S(1)}, u32[]{:S(2)}, u32[]{:S(2)}) collective-permute-start(bf16[192,768]{1,0:T(8,128)(2,1)S(1)} %pad_maximum_fusion.1), channel_id=1, source_target_pairs={{0,24},{1,25},{2,26},{3,27},{4,28},{5,29},{6,30},{7,31},{8,16},{9,... | collective-permute-start | bytes 884744 | tf_op jit(solution)/shard_map/ppermute | solution.py:37
  40.0 6.0 %copy-start = (bf16[384,768]{1,0:T(8,128)(2,1)}, bf16[384,768]{1,0:T(8,128)(2,1)S(1)}, u32[]{:S(2)}) copy-start(bf16[384,768]{1,0:T(8,128)(2,1)S(1)} %constant_dynamic-update-slice_fusion.3.wb0) | copy-start | bytes 1769476
  40.0 4.9 %collective-permute-start.9 = (bf16[384,768]{1,0:T(8,128)(2,1)S(1)}, bf16[384,768]{1,0:T(8,128)(2,1)S(1)}, u32[]{:S(2)}, u32[]{:S(2)}) collective-permute-start(bf16[384,768]{1,0:T(8,128)(2,1)S(1)} %constant_dynamic-update-slice_fusion.3.wb0), channel_id=1, source_target_pairs={{0,1},{1,0},{2,3},{3,2},{4,5},{5,4},{6,7},{7,6},{8,9},{9,8},{10,11... | collective-permute-start | bytes 1769480 | tf_op jit(solution)/shard_map/ppermute | solution.py:37
  44.0 2.1 copy-start.2
  44.0 2.1 collective-permute-start.6
  45.0 1.1 copy-start.1
  46.1 0.8 copy-start.3
  46.9 7.8 %copy-start.15 = (f32[576]{0:T(1024)S(1)}, f32[576]{0:T(1024)}, u32[]{:S(2)}) copy-start(f32[576]{0:T(1024)} %param.21) | copy-start | bytes 6916
  51.6 7.5 %collective-permute-start.10 = (bf16[384,384]{1,0:T(8,128)(2,1)}, bf16[384,384]{1,0:T(8,128)(2,1)S(1)}, u32[]{:S(2)}, u32[]{:S(2)}) collective-permute-start(bf16[384,384]{1,0:T(8,128)(2,1)} %get-tuple-element.62.own), channel_id=1, source_target_pairs={{0,1},{1,2},{2,3},{3,4},{4,5},{5,6},{6,7},{7,8},{8,9},{9,10},{10,1... | collective-permute-start | bytes 884744 | tf_op jit(solution)/shard_map/ppermute | solution.py:25
  59.1 0.7 copy-start.6
  120.6 9.7 %copy-start.7 = (bf16[768,576]{1,0:T(8,128)(2,1)S(1)}, bf16[768,576]{1,0:T(8,128)(2,1)}, u32[]{:S(2)}) copy-start(bf16[768,576]{1,0:T(8,128)(2,1)} %get-tuple-element.96) | copy-start | bytes 2654212
  129.0 3.7 %collective-permute-start.11 = (bf16[384,384]{1,0:T(8,128)(2,1)}, bf16[384,384]{1,0:T(8,128)(2,1)S(1)}, u32[]{:S(2)}, u32[]{:S(2)}) collective-permute-start(bf16[384,384]{1,0:T(8,128)(2,1)} %get-tuple-element.80), channel_id=1, source_target_pairs={{1,0},{2,1},{3,2},{4,3},{5,4},{6,5},{7,6},{8,7},{9,8},{10,9},{11,1... | collective-permute-start | bytes 884744 | tf_op jit(solution)/shard_map/ppermute | solution.py:25
  131.2 17.2 %collective-permute-start.32 = (bf16[768,576]{0,1:T(8,128)(2,1)S(1)}, bf16[768,576]{0,1:T(8,128)(2,1)}, u32[]{:S(2)}, u32[]{:S(2)}) collective-permute-start(bf16[768,576]{0,1:T(8,128)(2,1)S(1)} %copy.42), channel_id=1, source_target_pairs={{0,1},{1,0},{2,3},{3,2},{4,5},{5,4},{6,7},{7,6},{8,9},{9,8},{10,11... | collective-permute-start | bytes 2654216 | tf_op jit(solution)/shard_map/ppermute | solution.py:37
  132.7 0.7 copy-start.10
  141.5 6.6 %copy-start.9 = (bf16[384,768]{1,0:T(8,128)(2,1)S(1)}, bf16[384,768]{1,0:T(8,128)(2,1)}, u32[]{:S(2)}) copy-start(bf16[384,768]{1,0:T(8,128)(2,1)} %get-tuple-element.89) | copy-start | bytes 1769476
  141.5 6.7 %collective-permute-start.12 = (bf16[384,768]{1,0:T(8,128)(2,1)}, bf16[384,768]{1,0:T(8,128)(2,1)S(1)}, u32[]{:S(2)}, u32[]{:S(2)}) collective-permute-start(bf16[384,768]{1,0:T(8,128)(2,1)} %get-tuple-element.88), channel_id=1, source_target_pairs={{0,1},{1,0},{2,3},{3,2},{4,5},{5,4},{6,7},{7,6},{8,9},{9,8},{10,11... | collective-permute-start | bytes 1769480 | tf_op jit(solution)/shard_map/ppermute | solution.py:37
  146.4 23.6 %collective-permute-start.22 = (bf16[384,1536]{1,0:T(8,128)(2,1)}, bf16[384,1536]{1,0:T(8,128)(2,1)}, u32[]{:S(2)}, u32[]{:S(2)}) collective-permute-start(bf16[384,1536]{1,0:T(8,128)(2,1)} %get-tuple-element.92), channel_id=1, source_target_pairs={{0,1},{1,0},{2,3},{3,2},{4,5},{5,4},{6,7},{7,6},{8,9},{9,8},{10,11... | collective-permute-start | bytes 3538952 | tf_op jit(solution)/shard_map/ppermute | solution.py:37
  146.4 26.0 %collective-permute-start.27 = (bf16[384,1536]{1,0:T(8,128)(2,1)}, bf16[384,1536]{1,0:T(8,128)(2,1)}, u32[]{:S(2)}, u32[]{:S(2)}) collective-permute-start(bf16[384,1536]{1,0:T(8,128)(2,1)} %get-tuple-element.94), channel_id=1, source_target_pairs={{0,1},{1,0},{2,3},{3,2},{4,5},{5,4},{6,7},{7,6},{8,9},{9,8},{10,11... | collective-permute-start | bytes 3538952 | tf_op jit(solution)/shard_map/ppermute | solution.py:37
  146.9 5.7 %collective-permute-start.17 = (bf16[384,768]{1,0:T(8,128)(2,1)}, bf16[384,768]{1,0:T(8,128)(2,1)}, u32[]{:S(2)}, u32[]{:S(2)}) collective-permute-start(bf16[384,768]{1,0:T(8,128)(2,1)} %get-tuple-element.90), channel_id=1, source_target_pairs={{0,1},{1,0},{2,3},{3,2},{4,5},{5,4},{6,7},{7,6},{8,9},{9,8},{10,11... | collective-permute-start | bytes 1769480 | tf_op jit(solution)/shard_map/ppermute | solution.py:37
  150.1 5.2 %copy-start.8 = (bf16[768,576]{1,0:T(8,128)(2,1)S(1)}, bf16[768,576]{1,0:T(8,128)(2,1)}, u32[]{:S(2)}) copy-start(bf16[768,576]{1,0:T(8,128)(2,1)} %get-tuple-element.95) | copy-start | bytes 2654212
  150.1 11.8 %collective-permute-start.13 = (bf16[192,768]{1,0:T(8,128)(2,1)S(1)}, bf16[192,768]{1,0:T(8,128)(2,1)S(1)}, u32[]{:S(2)}, u32[]{:S(2)}) collective-permute-start(bf16[192,768]{1,0:T(8,128)(2,1)S(1)} %get-tuple-element.109), channel_id=1, source_target_pairs={{0,24},{1,25},{2,26},{3,27},{4,28},{5,29},{6,30},{7,31},{8,16},{9,... | collective-permute-start | bytes 884744 | tf_op jit(solution)/shard_map/ppermute | solution.py:37
  153.8 13.7 %collective-permute-start.18 = (bf16[192,768]{1,0:T(8,128)(2,1)S(1)}, bf16[192,768]{1,0:T(8,128)(2,1)S(1)}, u32[]{:S(2)}, u32[]{:S(2)}) collective-permute-start(bf16[192,768]{1,0:T(8,128)(2,1)S(1)} %get-tuple-element.107), channel_id=1, source_target_pairs={{0,4},{1,5},{2,6},{3,7},{4,0},{5,1},{6,2},{7,3},{8,12},{9,13},{10,... | collective-permute-start | bytes 884744 | tf_op jit(solution)/shard_map/ppermute | solution.py:37
  155.5 20.7 %collective-permute-start.33 = (bf16[384,576]{1,0:T(8,128)(2,1)S(1)}, bf16[384,576]{1,0:T(8,128)(2,1)S(1)}, u32[]{:S(2)}, u32[]{:S(2)}) collective-permute-start(bf16[384,576]{1,0:T(8,128)(2,1)S(1)} %get-tuple-element.113), channel_id=1, source_target_pairs={{0,8},{1,9},{2,10},{3,11},{4,12},{5,13},{6,14},{7,15},{8,0},{9,1},... | collective-permute-start | bytes 1327112 | tf_op jit(solution)/shard_map/ppermute | solution.py:37
  161.9 8.0 %copy-start.5 = (bf16[384,1536]{1,0:T(8,128)(2,1)S(1)}, bf16[384,1536]{1,0:T(8,128)(2,1)}, u32[]{:S(2)}) copy-start(bf16[384,1536]{1,0:T(8,128)(2,1)} %get-tuple-element.91) | copy-start | bytes 3538948
  162.0 14.9 %collective-permute-start.14 = (bf16[96,768]{1,0:T(8,128)(2,1)S(1)}, bf16[96,768]{1,0:T(8,128)(2,1)S(1)}, u32[]{:S(2)}, u32[]{:S(2)}) collective-permute-start(bf16[96,768]{1,0:T(8,128)(2,1)S(1)} %get-tuple-element.123), channel_id=1, source_target_pairs={{0,8},{1,9},{2,10},{3,11},{4,12},{5,13},{6,14},{7,15},{8,0},{9,1},... | collective-permute-start | bytes 442376 | tf_op jit(solution)/shard_map/ppermute | solution.py:37
  167.6 11.0 %collective-permute-start.19 = (bf16[96,768]{1,0:T(8,128)(2,1)S(1)}, bf16[96,768]{1,0:T(8,128)(2,1)S(1)}, u32[]{:S(2)}, u32[]{:S(2)}) collective-permute-start(bf16[96,768]{1,0:T(8,128)(2,1)S(1)} %get-tuple-element.121), channel_id=1, source_target_pairs={{0,2},{1,3},{2,0},{3,1},{4,6},{5,7},{6,4},{7,5},{8,10},{9,11},{10,... | collective-permute-start | bytes 442376 | tf_op jit(solution)/shard_map/ppermute | solution.py:37
  170.0 2.5 copy-start.4
  172.4 42.3 %collective-permute-start.23 = (bf16[192,1536]{1,0:T(8,128)(2,1)}, bf16[192,1536]{1,0:T(8,128)(2,1)}, u32[]{:S(2)}, u32[]{:S(2)}) collective-permute-start(bf16[192,1536]{1,0:T(8,128)(2,1)} %get-tuple-element.99), channel_id=1, source_target_pairs={{0,2},{1,3},{2,0},{3,1},{4,6},{5,7},{6,4},{7,5},{8,10},{9,11},{10,... | collective-permute-start | bytes 1769480 | tf_op jit(solution)/shard_map/ppermute | solution.py:37
  174.7 42.9 %collective-permute-start.28 = (bf16[192,1536]{1,0:T(8,128)(2,1)}, bf16[192,1536]{1,0:T(8,128)(2,1)S(1)}, u32[]{:S(2)}, u32[]{:S(2)}) collective-permute-start(bf16[192,1536]{1,0:T(8,128)(2,1)} %get-tuple-element.101), channel_id=1, source_target_pairs={{0,4},{1,5},{2,6},{3,7},{4,0},{5,1},{6,2},{7,3},{8,12},{9,13},{10,... | collective-permute-start | bytes 1769480 | tf_op jit(solution)/shard_map/ppermute | solution.py:37
  176.3 25.5 %collective-permute-start.34 = (bf16[192,576]{1,0:T(8,128)(2,1)S(1)}, bf16[192,576]{1,0:T(8,128)(2,1)S(1)}, u32[]{:S(2)}, u32[]{:S(2)}) collective-permute-start(bf16[192,576]{1,0:T(8,128)(2,1)S(1)} %get-tuple-element.111), channel_id=1, source_target_pairs={{0,4},{1,5},{2,6},{3,7},{4,0},{5,1},{6,2},{7,3},{8,12},{9,13},{10,... | collective-permute-start | bytes 663560 | tf_op jit(solution)/shard_map/ppermute | solution.py:37
  176.9 19.1 %collective-permute-start.15 = (bf16[48,768]{1,0:T(8,128)(2,1)S(1)}, bf16[48,768]{1,0:T(8,128)(2,1)S(1)}, u32[]{:S(2)}, u32[]{:S(2)}) collective-permute-start(bf16[48,768]{1,0:T(8,128)(2,1)S(1)} %get-tuple-element.129), channel_id=1, source_target_pairs={{0,4},{1,5},{2,6},{3,7},{4,0},{5,1},{6,2},{7,3},{8,12},{9,13},{10,... | collective-permute-start | bytes 221192 | tf_op jit(solution)/shard_map/ppermute | solution.py:37
  178.6 19.2 %collective-permute-start.20 = (bf16[48,768]{1,0:T(8,128)(2,1)S(1)}, bf16[48,768]{1,0:T(8,128)(2,1)S(1)}, u32[]{:S(2)}, u32[]{:S(2)}) collective-permute-start(bf16[48,768]{1,0:T(8,128)(2,1)S(1)} %get-tuple-element.127), channel_id=1, source_target_pairs={{0,24},{1,25},{2,26},{3,27},{4,28},{5,29},{6,30},{7,31},{8,16},{9,... | collective-permute-start | bytes 221192 | tf_op jit(solution)/shard_map/ppermute | solution.py:37
  196.0 4.0 %collective-permute-start.16 = (bf16[24,768]{1,0:T(8,128)(2,1)S(1)}, bf16[24,768]{1,0:T(8,128)(2,1)S(1)}, u32[]{:S(2)}, u32[]{:S(2)}) collective-permute-start(bf16[24,768]{1,0:T(8,128)(2,1)S(1)} %fusion.30), channel_id=1, source_target_pairs={{0,2},{1,3},{2,0},{3,1},{4,6},{5,7},{6,4},{7,5},{8,10},{9,11},{10,... | collective-permute-start | bytes 110600 | tf_op jit(solution)/shard_map/ppermute | solution.py:37
  197.8 4.0 %collective-permute-start.21 = (bf16[24,768]{1,0:T(8,128)(2,1)S(1)}, bf16[24,768]{1,0:T(8,128)(2,1)S(1)}, u32[]{:S(2)}, u32[]{:S(2)}) collective-permute-start(bf16[24,768]{1,0:T(8,128)(2,1)S(1)} %fusion.27), channel_id=1, source_target_pairs={{0,8},{1,9},{2,10},{3,11},{4,12},{5,13},{6,14},{7,15},{8,0},{9,1},... | collective-permute-start | bytes 110600 | tf_op jit(solution)/shard_map/ppermute | solution.py:37
  201.9 4.9 %collective-permute-start.35 = (bf16[96,576]{1,0:T(8,128)(2,1)S(1)}, bf16[96,576]{1,0:T(8,128)(2,1)S(1)}, u32[]{:S(2)}, u32[]{:S(2)}) collective-permute-start(bf16[96,576]{1,0:T(8,128)(2,1)S(1)} %get-tuple-element.125), channel_id=1, source_target_pairs={{0,2},{1,3},{2,0},{3,1},{4,6},{5,7},{6,4},{7,5},{8,10},{9,11},{10,... | collective-permute-start | bytes 331784 | tf_op jit(solution)/shard_map/ppermute | solution.py:37
  207.5 6.3 %collective-permute-start.36 = (bf16[48,576]{1,0:T(8,128)(2,1)}, bf16[48,576]{1,0:T(8,128)(2,1)S(1)}, u32[]{:S(2)}, u32[]{:S(2)}) collective-permute-start(bf16[48,576]{1,0:T(8,128)(2,1)} %fusion.25), channel_id=1, source_target_pairs={{0,24},{1,25},{2,26},{3,27},{4,28},{5,29},{6,30},{7,31},{8,16},{9,... | collective-permute-start | bytes 165896 | tf_op jit(solution)/shard_map/ppermute | solution.py:37
  215.8 10.2 %collective-permute-start.24 = (bf16[96,1536]{1,0:T(8,128)(2,1)S(1)}, bf16[96,1536]{1,0:T(8,128)(2,1)S(1)}, u32[]{:S(2)}, u32[]{:S(2)}) collective-permute-start(bf16[96,1536]{1,0:T(8,128)(2,1)S(1)} %get-tuple-element.103), channel_id=1, source_target_pairs={{0,24},{1,25},{2,26},{3,27},{4,28},{5,29},{6,30},{7,31},{8,16},{9,... | collective-permute-start | bytes 884744 | tf_op jit(solution)/shard_map/ppermute | solution.py:37
  217.8 8.3 %collective-permute-start.29 = (bf16[96,1536]{1,0:T(8,128)(2,1)S(1)}, bf16[96,1536]{1,0:T(8,128)(2,1)S(1)}, u32[]{:S(2)}, u32[]{:S(2)}) collective-permute-start(bf16[96,1536]{1,0:T(8,128)(2,1)S(1)} %get-tuple-element.105), channel_id=1, source_target_pairs={{0,2},{1,3},{2,0},{3,1},{4,6},{5,7},{6,4},{7,5},{8,10},{9,11},{10,... | collective-permute-start | bytes 884744 | tf_op jit(solution)/shard_map/ppermute | solution.py:37
  226.0 5.2 %collective-permute-start.25 = (bf16[48,1536]{1,0:T(8,128)(2,1)S(1)}, bf16[48,1536]{1,0:T(8,128)(2,1)S(1)}, u32[]{:S(2)}, u32[]{:S(2)}) collective-permute-start(bf16[48,1536]{1,0:T(8,128)(2,1)S(1)} %get-tuple-element.117), channel_id=1, source_target_pairs={{0,8},{1,9},{2,10},{3,11},{4,12},{5,13},{6,14},{7,15},{8,0},{9,1},... | collective-permute-start | bytes 442376 | tf_op jit(solution)/shard_map/ppermute | solution.py:37
  226.2 9.6 %collective-permute-start.30 = (bf16[48,1536]{1,0:T(8,128)(2,1)S(1)}, bf16[48,1536]{1,0:T(8,128)(2,1)S(1)}, u32[]{:S(2)}, u32[]{:S(2)}) collective-permute-start(bf16[48,1536]{1,0:T(8,128)(2,1)S(1)} %get-tuple-element.119), channel_id=1, source_target_pairs={{0,24},{1,25},{2,26},{3,27},{4,28},{5,29},{6,30},{7,31},{8,16},{9,... | collective-permute-start | bytes 442376 | tf_op jit(solution)/shard_map/ppermute | solution.py:37
  231.3 6.9 %collective-permute-start.26 = (bf16[24,1536]{1,0:T(8,128)(2,1)S(1)}, bf16[24,1536]{1,0:T(8,128)(2,1)S(1)}, u32[]{:S(2)}, u32[]{:S(2)}) collective-permute-start(bf16[24,1536]{1,0:T(8,128)(2,1)S(1)} %get-tuple-element.131), channel_id=1, source_target_pairs={{0,4},{1,5},{2,6},{3,7},{4,0},{5,1},{6,2},{7,3},{8,12},{9,13},{10,... | collective-permute-start | bytes 221192 | tf_op jit(solution)/shard_map/ppermute | solution.py:37
  235.8 4.4 %collective-permute-start.31 = (bf16[24,1536]{1,0:T(8,128)(2,1)S(1)}, bf16[24,1536]{1,0:T(8,128)(2,1)S(1)}, u32[]{:S(2)}, u32[]{:S(2)}) collective-permute-start(bf16[24,1536]{1,0:T(8,128)(2,1)S(1)} %get-tuple-element.133), channel_id=1, source_target_pairs={{0,8},{1,9},{2,10},{3,11},{4,12},{5,13},{6,14},{7,15},{8,0},{9,1},... | collective-permute-start | bytes 221192 | tf_op jit(solution)/shard_map/ppermute | solution.py:37
Sparse Core Ops, SparseCore 0:
  11.5 80.1 all-gather.1

commit v5 on v3

--- a/solution.py
+++ b/solution.py
@@ -477,55 +477,31 @@
         down_out[low : low + HD, :] = dv[:, tokens:]
 
 
-def prepare_kernel(
+def prepare_kernel(att, tok, gain_in, tall_a, tall_b, wide_a, wide_b, wide_att):
+    x = tok[...].astype(f32)
+    inverse = lax.rsqrt(jnp.mean(x * x, axis=0, keepdims=True) + norm_epsilon)
+    normed = (x * inverse * gain_in[...]).astype(bf16)
+    spread_b = spread_tall(tall_b[...])
+    wide_a[...] = dot_nn(spread_tall(tall_a[...]), normed).astype(bf16)
+    wide_b[...] = dot_nn(spread_b, normed).astype(bf16)
+    wide_att[...] = dot_nn(spread_b, att[...]).astype(bf16)
+
+
+def feed_kernel(
+    slots,
     att,
     tok,
-    gain_in,
+    cot,
     gain,
     row_b,
     row_n,
     tall_g,
     tall_u,
-    tall_a,
-    tall_b,
     wb0,
     wb1,
-    res_out,
-    wide_n,
-    tall_wide_g,
-    tall_wide_u,
-    tall_wide_a,
-    tall_wide_b,
-    tall_wide_att,
-):
-    wb = jnp.concatenate([wb0[...], wb1[...]], axis=0)
-    x = tok[...].astype(f32)
-    att_wide = dot_nn(att[...].T, spread_wide(row_b[...])).astype(bf16)
-    residual = x.T + dot_nn(att_wide, wb)[:, :D]
-    res_out[...] = residual
-    inverse = lax.rsqrt(jnp.mean(residual * residual, axis=-1, keepdims=True) + norm_epsilon)
-    normed = (residual * inverse * gain[...]).astype(bf16)
-    wide_n[...] = dot_nn(normed, spread_wide(row_n[...])).astype(bf16)
-    normed_t = normed.T
-    tall_wide_g[...] = dot_nn(spread_tall(tall_g[...]), normed_t).astype(bf16)
-    tall_wide_u[...] = dot_nn(spread_tall(tall_u[...]), normed_t).astype(bf16)
-    inverse_in = lax.rsqrt(jnp.mean(x * x, axis=0, keepdims=True) + norm_epsilon)
-    normed_in = (x * inverse_in * gain_in[...]).astype(bf16)
-    spread_b = spread_tall(tall_b[...])
-    tall_wide_a[...] = dot_nn(spread_tall(tall_a[...]), normed_in).astype(bf16)
-    tall_wide_b[...] = dot_nn(spread_b, normed_in).astype(bf16)
-    tall_wide_att[...] = dot_nn(spread_b, att[...]).astype(bf16)
-
-
-def feed_kernel(
-    slots,
-    residual,
-    cot,
-    wide_n,
-    tall_wide_g,
-    tall_wide_u,
     wall,
     mixed_out,
+    res_out,
     dgate,
     dup,
     dg_low,
@@ -535,6 +511,7 @@
     du_high,
     dd_high,
     act,
+    wide_n,
     wd,
 ):
     count = slots.shape[0]
@@ -546,7 +523,15 @@
             wd[j * rows_d + k * fold : j * rows_d + (k + 1) * fold, :] = wall[
                 j * PAD : j * PAD + fold, at : at + D
             ]
+    wb = jnp.concatenate([wb0[...], wb1[...]], axis=0)
     cot_tok = cot[...].T
+    att_wide = dot_nn(att[...].T, spread_wide(row_b[...])).astype(bf16)
+    residual = tok[...].astype(f32).T + dot_nn(att_wide, wb)[:, :D]
+    res_out[...] = residual
+    inverse = lax.rsqrt(jnp.mean(residual * residual, axis=-1, keepdims=True) + norm_epsilon)
+    normed = (residual * inverse * gain[...]).astype(bf16)
+    wide_n[...] = dot_nn(normed, spread_wide(row_n[...])).astype(bf16)
+    normed_t = normed.T
     block = 256
 
     def ff_step(j, carry):
@@ -563,13 +548,13 @@
         return carry
 
     lax.fori_loop(0, FF // block, ff_step, 0)
-    mixed = residual[...] + dot_nn(act[...], wd[...])
+    mixed = residual + dot_nn(act[...], wd[...])
     mixed_out[...] = mixed.T.astype(bf16)
-    half = tall_wide_g.shape[0] // 2
-    dg_low[...] = dot_nn(tall_wide_g[:half, :], dgate[...]).astype(bf16)
-    dg_high[...] = dot_nn(tall_wide_g[half:, :], dgate[...]).astype(bf16)
-    du_low[...] = dot_nn(tall_wide_u[:half, :], dup[...]).astype(bf16)
-    du_high[...] = dot_nn(tall_wide_u[half:, :], dup[...]).astype(bf16)
+    for tall, grad, low, high in ((tall_g, dgate, dg_low, dg_high), (tall_u, dup, du_low, du_high)):
+        wide_t = dot_nn(spread_tall(tall[...]), normed_t).astype(bf16)
+        half = wide_t.shape[0] // 2
+        low[...] = dot_nn(wide_t[:half], grad[...]).astype(bf16)
+        high[...] = dot_nn(wide_t[half:], grad[...]).astype(bf16)
     wd[...] = dot_nn(act[...].T, cot_tok).astype(bf16)
     for p in range(count):
         source = pl.multiple_of(slots[p] * rows_d, rows_d)
@@ -791,22 +776,25 @@
     )
     wide = count * PAD
     tall_shape = ((wide, row_count), bf16)
-    residual, wide_n, tall_wide_g, tall_wide_u, wide_a, wide_b, wide_att = call_whole(
-        prepare_kernel,
-        [((row_count, D), f32), ((row_count, wide), bf16)] + [tall_shape] * 5,
-        [att_t, tok_t, gain_col, gain_ffn[None], row_b, row_n, tall_g, tall_u, tall_a, tall_b]
-        + [wb0, wb1],
-    )
-    mixed_t, dgate, dup, *sums = call_whole(
+    wide_a, wide_b, wide_att = call_whole(
+        prepare_kernel, [tall_shape] * 3, [att_t, tok_t, gain_col, tall_a, tall_b]
+    )
+    att_t, wide_a, wide_b, wide_att = hold((att_t, wide_a, wide_b, wide_att))
+    mixed_t, residual, dgate, dup, *sums = call_whole(
         feed_kernel,
         [
             ((D, row_count), bf16),
+            ((row_count, D), f32),
             ((row_count, FF), bf16),
             ((row_count, FF), bf16),
         ]
         + [((wide // 2, FF), bf16), ((wide // 2, FF), bf16), ((FF // 2, D), bf16)] * 2,
-        [residual, cot_t, wide_n, tall_wide_g, tall_wide_u, wall],
-        scratch=[pltpu.VMEM((row_count, FF), bf16), pltpu.VMEM((FF, D), bf16)],
+        [att_t, tok_t, cot_t, gain_ffn[None], row_b, row_n, tall_g, tall_u, wb0, wb1, wall],
+        scratch=[
+            pltpu.VMEM((row_count, FF), bf16),
+            pltpu.VMEM((row_count, wide), bf16),
+            pltpu.VMEM((FF, D), bf16),
+        ],
         scalars=[slots],
     )
     sums = (sums[:3], sums[3:])

time: 248 us -> 251 us (1.012)
  waiting for transfers between devices: 75.6 us -> 82.5 us
  starting transfers between devices: 54.1 us -> 50.4 us
    all_gather x1, waiting for transfers between devices: 11.8 us -> 15.8 us  [shards(): wall = lax.all_gather(stream_ffn, 'dev', axis=0, tiled=True)]
    ppermute x35, starting transfers between devices: 50.2 us -> 46.5 us  [swapped(): return lax.ppermute(value, 'dev', [(i, i ^ mask) for i in range(count)])]
    ppermute x35, waiting for transfers between devices: 63.4 us -> 66.1 us  [swapped(): return lax.ppermute(value, 'dev', [(i, i ^ mask) for i in range(count)])]
  transfers between devices with their start and end apart: 38 -> 38, of which waited for: 18 -> 22; matrix products, arithmetic and copies ran while one was open for 11% -> 11% of each run, Pallas kernels for 13% -> 12%
where the time goes in v5:
time: 251 us; the launch traced here: 247 us
  waiting for transfers between devices  82.5 us (33%)
  Pallas kernels  66.1 us (26%)
  starting transfers between devices  50.4 us (20%)
  local copies, waits for them, and re-layouts  20.6 us (8%)
  between operations  14.8 us (6%)
  other arithmetic  12.6 us (5%)
    ppermute x35, waiting for transfers between devices, swapped(): return lax.ppermute(value, 'dev', [(i, i ^ mask) for i in range(count)])  66.1 us
    pallas_call x7, Pallas kernels, call_whole(): pl.pallas_call(kernel, out_shape=[jax.ShapeDtypeStruct(s, d) for s, d in...  66.1 us
    ppermute x35, starting transfers between devices, swapped(): return lax.ppermute(value, 'dev', [(i, i ^ mask) for i in range(count)])  46.5 us
    all_gather x1, waiting for transfers between devices, shards(): wall = lax.all_gather(stream_ffn, 'dev', axis=0, tiled=True)  15.8 us
    convert_element_type x20, other arithmetic, step_halve(): high.append((k[half:].astype(f32) + g[half:].astype(f32)).astype(bf16))  8.67 us
  transfers between devices with their start and end apart: 38, of which 22 were waited for; matrix products, arithmetic and copies ran while one was open for 11% of the time, Pallas kernels for 12%

profile of v5, /device:TPU:0, one launch (start us, length us, event | category | flops | bytes accessed | tf_op | source)
XLA Modules:
  0.0 247.0 jit_solution(402039327546712933)
XLA Ops:
  7.3 0.9 reshape.332
  8.3 1.0 reshape.331
  11.0 3.1 %collective-permute-start.2 = (bf16[24,768]{1,0:T(8,128)(2,1)S(1)}, bf16[24,768]{1,0:T(8,128)(2,1)S(1)}, u32[]{:S(2)}, u32[]{:S(2)}) collective-permute-start(bf16[24,768]{1,0:T(8,128)(2,1)S(1)} %fusion.38), channel_id=1, source_target_pairs={{0,8},{1,9},{2,10},{3,11},{4,12},{5,13},{6,14},{7,15},{8,0},{9,1},... | collective-permute-start | bytes 110600 | tf_op jit(solution)/shard_map/ppermute | solution.py:37
  14.2 1.5 collective-permute-start
  15.9 0.9 multiply_sine_fusion
  19.6 2.5 %collective-permute-start.3 = (bf16[48,768]{1,0:T(8,128)(2,1)S(1)}, bf16[48,768]{1,0:T(8,128)(2,1)S(1)}, u32[]{:S(2)}, u32[]{:S(2)}) collective-permute-start(bf16[48,768]{1,0:T(8,128)(2,1)S(1)} %pad_maximum_fusion.6), channel_id=1, source_target_pairs={{0,24},{1,25},{2,26},{3,27},{4,28},{5,29},{6,30},{7,31},{8,16},{9,... | collective-permute-start | bytes 221192 | tf_op jit(solution)/shard_map/ppermute | solution.py:37
  22.1 1.6 collective-permute-start.1
  23.7 2.1 collective-permute-done.3
  25.8 2.0 collective-permute-done.1
  28.1 5.0 %collective-permute-done.7 = bf16[96,768]{1,0:T(8,128)(2,1)S(1)} collective-permute-done((bf16[96,768]{1,0:T(8,128)(2,1)S(1)}, bf16[96,768]{1,0:T(8,128)(2,1)S(1)}, u32[]{:S(2)}, u32[]{:S(2)}) %collective-permute-start.7) | collective-permute-done | bytes 147488 | tf_op jit(solution)/shard_map/ppermute | solution.py:37
  34.0 1.9 collective-permute-start.5
  35.9 4.0 %collective-permute-done.8 = bf16[192,768]{1,0:T(8,128)(2,1)S(1)} collective-permute-done((bf16[192,768]{1,0:T(8,128)(2,1)S(1)}, bf16[192,768]{1,0:T(8,128)(2,1)S(1)}, u32[]{:S(2)}, u32[]{:S(2)}) %collective-permute-start.8) | collective-permute-done | bytes 294944 | tf_op jit(solution)/shard_map/ppermute | solution.py:37
  40.0 2.6 %collective-permute-done.5 = bf16[192,768]{1,0:T(8,128)(2,1)S(1)} collective-permute-done((bf16[192,768]{1,0:T(8,128)(2,1)S(1)}, bf16[192,768]{1,0:T(8,128)(2,1)S(1)}, u32[]{:S(2)}, u32[]{:S(2)}) %collective-permute-start.5) | collective-permute-done | bytes 294944 | tf_op jit(solution)/shard_map/ppermute | solution.py:37
  42.8 0.9 copy.33.gain.gain_in
  43.7 1.1 collective-permute-done.6.wa1
  44.8 0.8 copy-done.3
  45.6 4.7 %shard_map.214 = (bf16[576,384]{1,0:T(8,128)(2,1)}, bf16[384,384]{1,0:T(8,128)(2,1)}) custom-call(bf16[576,384]{1,0:T(8,128)(2,1)} %bitcast.8, f32[576,1]{1,0:T(8,128)} %copy.33.gain.gain_in, f32[32,384]{1,0:T(8,128)} %get-tuple-element.56.cos, f32[32,384]{1,0:T(8,128)} %get-tuple-element.57.sin, s32[1,768]{1,0:T(1,128)} %select_n.87.src_a, ...), custom_call_target="tpu_custom_call" | custom-call | tf_op jit(solution)/shard_map/pallas_call | solution.py:668
  50.3 2.6 %collective-permute-start.10 = (bf16[384,384]{1,0:T(8,128)(2,1)}, bf16[384,384]{1,0:T(8,128)(2,1)S(1)}, u32[]{:S(2)}, u32[]{:S(2)}) collective-permute-start(bf16[384,384]{1,0:T(8,128)(2,1)} %get-tuple-element.63.own), channel_id=1, source_target_pairs={{0,1},{1,2},{2,3},{3,4},{4,5},{5,6},{6,7},{7,8},{8,9},{9,10},{10,1... | collective-permute-start | bytes 884744 | tf_op jit(solution)/shard_map/ppermute | solution.py:25
  54.1 0.9 copy.35.tall_a
  55.0 0.9 copy.36.tall_b
  56.0 1.0 copy.37.tall_g
  56.9 1.0 copy.38.tall_u
  58.6 12.2 %shard_map.215 = (bf16[3,3,512,384]{3,2,1,0:T(8,128)(2,1)}, bf16[576,384]{1,0:T(8,128)(2,1)}) custom-call(bf16[576,384]{1,0:T(8,128)(2,1)} %get-tuple-element.62.q, bf16[384,384]{1,0:T(8,128)(2,1)} %copy-done.6, bf16[384,384]{1,0:T(8,128)(2,1)} %get-tuple-element.63.own, s32[1,384]{1,0:T(1,128)} %broadcast_in_dim.57.pos), custom_call_target="tpu_custom_call" | custom-call | tf_op jit(solution)/shard_map/pallas_call | solution.py:668
  70.8 4.3 %shard_map.216 = (bf16[768,384]{1,0:T(8,128)(2,1)}, bf16[768,384]{1,0:T(8,128)(2,1)}, bf16[768,384]{1,0:T(8,128)(2,1)}) custom-call(bf16[576,384]{1,0:T(8,128)(2,1)} %get-tuple-element.70.att, bf16[576,384]{1,0:T(8,128)(2,1)} %bitcast.9, f32[576,1]{1,0:T(8,128)} %copy.33.gain.gain_in, s32[768,1]{1,0:T(8,128)} %copy.35.tall_a, s32[768,1]{1,0:T(8,128)} %copy.36.tall_b), custom_call_target="tpu_custom_call" | custom-call | tf_op jit(solution)/shard_map/pallas_call | solution.py:668
  75.2 15.8 %all-gather.2.cloned.1.call-done.wall = bf16[768,4352]{1,0:T(8,128)(2,1)} async-done(((bf16[24,4352]{1,0:T(8,128)(2,1)}), bf16[768,4352]{1,0:T(8,128)(2,1)}) %all-gather.2.cloned.1.call-update) | async-done | bytes 6684688 | tf_op jit(solution)/shard_map/all_gather | solution.py:739
  91.0 17.7 %shard_map.217 = (bf16[576,384]{1,0:T(8,128)(2,1)}, f32[384,576]{1,0:T(8,128)}, bf16[384,1536]{1,0:T(8,128)(2,1)}, bf16[384,1536]{1,0:T(8,128)(2,1)}, bf16[384,1...) custom-call(s32[32]{0:T(128)} %broadcast_xor_fusion.slots, ...), custom_call_target="tpu_custom_call" | custom-call | tf_op jit(solution)/shard_map/pallas_call | solution.py:668
  108.7 10.4 %shard_map.218 = (f32[576,384]{1,0:T(8,128)}, bf16[576,384]{1,0:T(8,128)(2,1)}, f32[1,576]{1,0:T(1,128)}) custom-call(f32[384,576]{1,0:T(8,128)} %get-tuple-element.76.residual_in, bf16[576,384]{1,0:T(8,128)(2,1)} %bitcast.13, f32[1,576]{1,0:T(1,128)} %broadcast_in_dim.58.gain, s32[1,768]{1,0:T(1,128)} %select_n.89.src_b.row_b, ...), custom_call_target="tpu_custom_call" | custom-call | tf_op jit(solution)/shard_map/pallas_call | solution.py:668
  119.1 8.6 %shard_map.219 = (bf16[576,384]{1,0:T(8,128)(2,1)}, bf16[384,384]{1,0:T(8,128)(2,1)}, f32[384,384]{1,0:T(8,128)}) custom-call(bf16[576,384]{1,0:T(8,128)(2,1)} %get-tuple-element.62.q, bf16[384,384]{1,0:T(8,128)(2,1)} %copy-done.6, bf16[384,384]{1,0:T(8,128)(2,1)} %get-tuple-element.63.own, bf16[3,3,512,384]{3,2,1,0:T(8,128)(2,1)} %get-tuple-element.75.prob, ...), custom_call_target="tpu_custom_call" | custom-call | tf_op jit(solution)/shard_map/pallas_call | solution.py:668
  127.7 1.3 collective-permute-start.11
  129.7 1.2 collective-permute-start.32
  132.1 8.1 %shard_map.220 = (f32[576,384]{1,0:T(8,128)}, bf16[384,768]{1,0:T(8,128)(2,1)}, bf16[384,768]{1,0:T(8,128)(2,1)}, bf16[384,768]{1,0:T(8,128)(2,1)}, bf16[384,768]{1,0:T(8,128)(2,1)}) custom-call(bf16[576,384]{1,0:T(8,128)(2,1)} %get-tuple-element.80.dq, f32[384,384]{1,0:T(8,128)} %get-tuple-element.81.own, bf16[384,384]{1,0:T(8,128)(2,1)} %copy-done.10, ...), custom_call_target="tpu_custom_call" | custom-call | tf_op jit(solution)/shard_map/pallas_call | solution.py:668
  140.2 4.9 %collective-permute-start.17 = (bf16[384,768]{1,0:T(8,128)(2,1)}, bf16[384,768]{1,0:T(8,128)(2,1)S(1)}, u32[]{:S(2)}, u32[]{:S(2)}) collective-permute-start(bf16[384,768]{1,0:T(8,128)(2,1)} %get-tuple-element.92), channel_id=1, source_target_pairs={{0,1},{1,0},{2,3},{3,2},{4,5},{5,4},{6,7},{7,6},{8,9},{9,8},{10,11... | collective-permute-start | bytes 1769480 | tf_op jit(solution)/shard_map/ppermute | solution.py:37
  145.7 1.1 convert_reduce-precision_fusion
  147.0 1.2 fusion.41
  148.8 1.5 collective-permute-start.18
  150.4 0.9 collective-permute-done.12
  151.3 1.2 fusion.4
  152.4 2.4 collective-permute-start.13
  155.3 2.9 %collective-permute-done.18 = bf16[192,768]{1,0:T(8,128)(2,1)S(1)} collective-permute-done((bf16[192,768]{1,0:T(8,128)(2,1)S(1)}, bf16[192,768]{1,0:T(8,128)(2,1)S(1)}, u32[]{:S(2)}, u32[]{:S(2)}) %collective-permute-start.18) | collective-permute-done | bytes 294944 | tf_op jit(solution)/shard_map/ppermute | solution.py:37
  158.3 2.4 collective-permute-start.19
  160.7 3.5 %collective-permute-done.13 = bf16[192,768]{1,0:T(8,128)(2,1)S(1)} collective-permute-done((bf16[192,768]{1,0:T(8,128)(2,1)S(1)}, bf16[192,768]{1,0:T(8,128)(2,1)S(1)}, u32[]{:S(2)}, u32[]{:S(2)}) %collective-permute-start.13) | collective-permute-done | bytes 294944 | tf_op jit(solution)/shard_map/ppermute | solution.py:37
  164.3 5.4 %collective-permute-start.14 = (bf16[96,768]{1,0:T(8,128)(2,1)S(1)}, bf16[96,768]{1,0:T(8,128)(2,1)S(1)}, u32[]{:S(2)}, u32[]{:S(2)}) collective-permute-start(bf16[96,768]{1,0:T(8,128)(2,1)S(1)} %get-tuple-element.123), channel_id=1, source_target_pairs={{0,8},{1,9},{2,10},{3,11},{4,12},{5,13},{6,14},{7,15},{8,0},{9,1},... | collective-permute-start | bytes 442376 | tf_op jit(solution)/shard_map/ppermute | solution.py:37
  169.7 2.4 add_convert_fusion.1
  172.2 2.3 collective-permute-start.23
  174.5 2.3 add_convert_fusion
  176.8 1.4 collective-permute-start.28
  179.0 1.9 collective-permute-start.20
  180.9 0.9 collective-permute-start.15
  181.8 3.4 %collective-permute-done.20 = bf16[48,768]{1,0:T(8,128)(2,1)S(1)} collective-permute-done((bf16[48,768]{1,0:T(8,128)(2,1)S(1)}, bf16[48,768]{1,0:T(8,128)(2,1)S(1)}, u32[]{:S(2)}, u32[]{:S(2)}) %collective-permute-start.20) | collective-permute-done | bytes 73760 | tf_op jit(solution)/shard_map/ppermute | solution.py:37
  185.3 12.7 %collective-permute-done.15 = bf16[48,768]{1,0:T(8,128)(2,1)S(1)} collective-permute-done((bf16[48,768]{1,0:T(8,128)(2,1)S(1)}, bf16[48,768]{1,0:T(8,128)(2,1)S(1)}, u32[]{:S(2)}, u32[]{:S(2)}) %collective-permute-start.15) | collective-permute-done | bytes 73760 | tf_op jit(solution)/shard_map/ppermute | solution.py:37
  199.0 3.3 %collective-permute-done.16 = bf16[24,768]{1,0:T(8,128)(2,1)S(1)} collective-permute-done((bf16[24,768]{1,0:T(8,128)(2,1)S(1)}, bf16[24,768]{1,0:T(8,128)(2,1)S(1)}, u32[]{:S(2)}, u32[]{:S(2)}) %collective-permute-start.16) | collective-permute-done | bytes 36896 | tf_op jit(solution)/shard_map/ppermute | solution.py:37
  203.3 4.1 %collective-permute-done.35 = bf16[96,576]{1,0:T(8,128)(2,1)S(1)} collective-permute-done((bf16[96,576]{1,0:T(8,128)(2,1)S(1)}, bf16[96,576]{1,0:T(8,128)(2,1)S(1)}, u32[]{:S(2)}, u32[]{:S(2)}) %collective-permute-start.35) | collective-permute-done | bytes 110624 | tf_op jit(solution)/shard_map/ppermute | solution.py:37
  208.1 1.8 collective-permute-start.36
  212.0 2.4 collective-permute-done.36
  214.4 0.7 reshape.337
  215.2 1.2 fusion.1
  216.3 1.8 collective-permute-start.24
  218.4 9.0 %collective-permute-done.24 = bf16[96,1536]{1,0:T(8,128)(2,1)S(1)} collective-permute-done((bf16[96,1536]{1,0:T(8,128)(2,1)S(1)}, bf16[96,1536]{1,0:T(8,128)(2,1)S(1)}, u32[]{:S(2)}, u32[]{:S(2)}) %collective-permute-start.24) | collective-permute-done | bytes 294944 | tf_op jit(solution)/shard_map/ppermute | solution.py:37
  227.6 1.6 collective-permute-start.30
  229.2 3.7 %collective-permute-done.25 = bf16[48,1536]{1,0:T(8,128)(2,1)S(1)} collective-permute-done((bf16[48,1536]{1,0:T(8,128)(2,1)S(1)}, bf16[48,1536]{1,0:T(8,128)(2,1)S(1)}, u32[]{:S(2)}, u32[]{:S(2)}) %collective-permute-start.25) | collective-permute-done | bytes 147488 | tf_op jit(solution)/shard_map/ppermute | solution.py:37
  233.0 1.5 collective-permute-start.26
  234.7 1.7 collective-permute-start.31
  236.5 0.9 collective-permute-done.26
  237.4 1.7 collective-permute-done.31
  (150 shorter events, 18.9 us)
Async XLA Ops:
  7.2 8.6 %copy-start.18 = (s32[32]{0:T(128)S(1)}, s32[32]{0:T(128)}, u32[]{:S(2)}) copy-start(s32[32]{0:T(128)} %constant.22.clone) | copy-start | bytes 388
  7.2 8.6 %copy-start.16 = (s32[32]{0:T(128)S(1)}, s32[32]{0:T(128)}, u32[]{:S(2)}) copy-start(s32[32]{0:T(128)} %constant.23.clone) | copy-start | bytes 388
  7.2 8.6 %copy-start.17 = (s32[32]{0:T(128)S(1)}, s32[32]{0:T(128)}, u32[]{:S(2)}) copy-start(s32[32]{0:T(128)} %constant.24.clone) | copy-start | bytes 388
  7.2 9.6 %copy-start.19 = (s32[32]{0:T(128)S(1)}, s32[32]{0:T(128)}, u32[]{:S(2)}) copy-start(s32[32]{0:T(128)} %constant.25.clone) | copy-start | bytes 388
  7.2 3.5 %copy-start.11 = (bf16[10368]{0:T(1024)(128)(2,1)S(1)}, bf16[10368]{0:T(1024)(128)(2,1)}, u32[]{:S(2)}) copy-start(bf16[10368]{0:T(1024)(128)(2,1)} %param.20) | copy-start | bytes 62212
  7.2 6.8 %copy-start.12 = (bf16[10368]{0:T(1024)(128)(2,1)S(1)}, bf16[10368]{0:T(1024)(128)(2,1)}, u32[]{:S(2)}) copy-start(bf16[10368]{0:T(1024)(128)(2,1)} %param.18) | copy-start | bytes 62212
  7.2 8.5 %copy-start.13 = (s32[384]{0:T(512)S(1)}, s32[384]{0:T(512)}, u32[]{:S(2)}) copy-start(s32[384]{0:T(512)} %param.16) | copy-start | bytes 4612
  7.3 12.3 %copy-start.14 = (f32[576]{0:T(1024)S(1)}, f32[576]{0:T(1024)}, u32[]{:S(2)}) copy-start(f32[576]{0:T(1024)} %param.17) | copy-start | bytes 6916
  7.3 83.8 %all-gather.2.cloned.1.call-start = ((), (), s32[]{:S(2)}) async-start(), calls=%async_computation | async-start | bytes 6893568 | tf_op jit(solution)/shard_map/all_gather | solution.py:739
  11.0 8.6 %collective-permute-start.2 = (bf16[24,768]{1,0:T(8,128)(2,1)S(1)}, bf16[24,768]{1,0:T(8,128)(2,1)S(1)}, u32[]{:S(2)}, u32[]{:S(2)}) collective-permute-start(bf16[24,768]{1,0:T(8,128)(2,1)S(1)} %fusion.38), channel_id=1, source_target_pairs={{0,8},{1,9},{2,10},{3,11},{4,12},{5,13},{6,14},{7,15},{8,0},{9,1},... | collective-permute-start | bytes 110600 | tf_op jit(solution)/shard_map/ppermute | solution.py:37
  14.2 7.9 %collective-permute-start = (bf16[24,768]{1,0:T(8,128)(2,1)S(1)}, bf16[24,768]{1,0:T(8,128)(2,1)S(1)}, u32[]{:S(2)}, u32[]{:S(2)}) collective-permute-start(bf16[24,768]{1,0:T(8,128)(2,1)S(1)} %fusion.37), channel_id=1, source_target_pairs={{0,2},{1,3},{2,0},{3,1},{4,6},{5,7},{6,4},{7,5},{8,10},{9,11},{10,... | collective-permute-start | bytes 110600 | tf_op jit(solution)/shard_map/ppermute | solution.py:37
  19.6 6.2 %collective-permute-start.3 = (bf16[48,768]{1,0:T(8,128)(2,1)S(1)}, bf16[48,768]{1,0:T(8,128)(2,1)S(1)}, u32[]{:S(2)}, u32[]{:S(2)}) collective-permute-start(bf16[48,768]{1,0:T(8,128)(2,1)S(1)} %pad_maximum_fusion.6), channel_id=1, source_target_pairs={{0,24},{1,25},{2,26},{3,27},{4,28},{5,29},{6,30},{7,31},{8,16},{9,... | collective-permute-start | bytes 221192 | tf_op jit(solution)/shard_map/ppermute | solution.py:37
  22.1 5.7 %collective-permute-start.1 = (bf16[48,768]{1,0:T(8,128)(2,1)S(1)}, bf16[48,768]{1,0:T(8,128)(2,1)S(1)}, u32[]{:S(2)}, u32[]{:S(2)}) collective-permute-start(bf16[48,768]{1,0:T(8,128)(2,1)S(1)} %pad_maximum_fusion.5), channel_id=1, source_target_pairs={{0,4},{1,5},{2,6},{3,7},{4,0},{5,1},{6,2},{7,3},{8,12},{9,13},{10,... | collective-permute-start | bytes 221192 | tf_op jit(solution)/shard_map/ppermute | solution.py:37
  27.9 5.2 %collective-permute-start.7 = (bf16[96,768]{1,0:T(8,128)(2,1)S(1)}, bf16[96,768]{1,0:T(8,128)(2,1)S(1)}, u32[]{:S(2)}, u32[]{:S(2)}) collective-permute-start(bf16[96,768]{1,0:T(8,128)(2,1)S(1)} %pad_maximum_fusion.4), channel_id=1, source_target_pairs={{0,2},{1,3},{2,0},{3,1},{4,6},{5,7},{6,4},{7,5},{8,10},{9,11},{10,... | collective-permute-start | bytes 442376 | tf_op jit(solution)/shard_map/ppermute | solution.py:37
  28.0 6.0 %collective-permute-start.4 = (bf16[96,768]{1,0:T(8,128)(2,1)S(1)}, bf16[96,768]{1,0:T(8,128)(2,1)S(1)}, u32[]{:S(2)}, u32[]{:S(2)}) collective-permute-start(bf16[96,768]{1,0:T(8,128)(2,1)S(1)} %pad_maximum_fusion.3), channel_id=1, source_target_pairs={{0,8},{1,9},{2,10},{3,11},{4,12},{5,13},{6,14},{7,15},{8,0},{9,1},... | collective-permute-start | bytes 442376 | tf_op jit(solution)/shard_map/ppermute | solution.py:37
  33.1 6.8 %collective-permute-start.8 = (bf16[192,768]{1,0:T(8,128)(2,1)S(1)}, bf16[192,768]{1,0:T(8,128)(2,1)S(1)}, u32[]{:S(2)}, u32[]{:S(2)}) collective-permute-start(bf16[192,768]{1,0:T(8,128)(2,1)S(1)} %pad_maximum_fusion.1), channel_id=1, source_target_pairs={{0,4},{1,5},{2,6},{3,7},{4,0},{5,1},{6,2},{7,3},{8,12},{9,13},{10,... | collective-permute-start | bytes 884744 | tf_op jit(solution)/shard_map/ppermute | solution.py:37
  34.0 8.7 %collective-permute-start.5 = (bf16[192,768]{1,0:T(8,128)(2,1)S(1)}, bf16[192,768]{1,0:T(8,128)(2,1)S(1)}, u32[]{:S(2)}, u32[]{:S(2)}) collective-permute-start(bf16[192,768]{1,0:T(8,128)(2,1)S(1)} %pad_maximum_fusion), channel_id=1, source_target_pairs={{0,24},{1,25},{2,26},{3,27},{4,28},{5,29},{6,30},{7,31},{8,16},{9,... | collective-permute-start | bytes 884744 | tf_op jit(solution)/shard_map/ppermute | solution.py:37
  39.9 4.8 %copy-start = (bf16[384,768]{1,0:T(8,128)(2,1)}, bf16[384,768]{1,0:T(8,128)(2,1)S(1)}, u32[]{:S(2)}) copy-start(bf16[384,768]{1,0:T(8,128)(2,1)S(1)} %constant_dynamic-update-slice_fusion.3.wb0) | copy-start | bytes 1769476
  39.9 3.7 %collective-permute-start.9 = (bf16[384,768]{1,0:T(8,128)(2,1)S(1)}, bf16[384,768]{1,0:T(8,128)(2,1)S(1)}, u32[]{:S(2)}, u32[]{:S(2)}) collective-permute-start(bf16[384,768]{1,0:T(8,128)(2,1)S(1)} %constant_dynamic-update-slice_fusion.3.wb0), channel_id=1, source_target_pairs={{0,1},{1,0},{2,3},{3,2},{4,5},{5,4},{6,7},{7,6},{8,9},{9,8},{10,11... | collective-permute-start | bytes 1769480 | tf_op jit(solution)/shard_map/ppermute | solution.py:37
  42.7 2.1 copy-start.2
  42.7 2.1 collective-permute-start.6
  43.7 1.1 copy-start.1
  44.8 0.8 copy-start.3
  45.6 7.9 %copy-start.15 = (f32[576]{0:T(1024)S(1)}, f32[576]{0:T(1024)}, u32[]{:S(2)}) copy-start(f32[576]{0:T(1024)} %param.21) | copy-start | bytes 6916
  50.3 7.6 %collective-permute-start.10 = (bf16[384,384]{1,0:T(8,128)(2,1)}, bf16[384,384]{1,0:T(8,128)(2,1)S(1)}, u32[]{:S(2)}, u32[]{:S(2)}) collective-permute-start(bf16[384,384]{1,0:T(8,128)(2,1)} %get-tuple-element.63.own), channel_id=1, source_target_pairs={{0,1},{1,2},{2,3},{3,4},{4,5},{5,6},{6,7},{7,8},{8,9},{9,10},{10,1... | collective-permute-start | bytes 884744 | tf_op jit(solution)/shard_map/ppermute | solution.py:25
  57.9 0.7 copy-start.6
  119.1 9.9 %copy-start.7 = (bf16[768,576]{1,0:T(8,128)(2,1)S(1)}, bf16[768,576]{1,0:T(8,128)(2,1)}, u32[]{:S(2)}) copy-start(bf16[768,576]{1,0:T(8,128)(2,1)} %get-tuple-element.98) | copy-start | bytes 2654212
  127.7 3.7 %collective-permute-start.11 = (bf16[384,384]{1,0:T(8,128)(2,1)}, bf16[384,384]{1,0:T(8,128)(2,1)S(1)}, u32[]{:S(2)}, u32[]{:S(2)}) collective-permute-start(bf16[384,384]{1,0:T(8,128)(2,1)} %get-tuple-element.82), channel_id=1, source_target_pairs={{1,0},{2,1},{3,2},{4,3},{5,4},{6,5},{7,6},{8,7},{9,8},{10,9},{11,1... | collective-permute-start | bytes 884744 | tf_op jit(solution)/shard_map/ppermute | solution.py:25
  129.7 17.4 %collective-permute-start.32 = (bf16[768,576]{0,1:T(8,128)(2,1)S(1)}, bf16[768,576]{0,1:T(8,128)(2,1)}, u32[]{:S(2)}, u32[]{:S(2)}) collective-permute-start(bf16[768,576]{0,1:T(8,128)(2,1)S(1)} %copy.42), channel_id=1, source_target_pairs={{0,1},{1,0},{2,3},{3,2},{4,5},{5,4},{6,7},{7,6},{8,9},{9,8},{10,11... | collective-permute-start | bytes 2654216 | tf_op jit(solution)/shard_map/ppermute | solution.py:37
  131.4 0.7 copy-start.10
  140.2 6.6 %copy-start.9 = (bf16[384,768]{1,0:T(8,128)(2,1)S(1)}, bf16[384,768]{1,0:T(8,128)(2,1)}, u32[]{:S(2)}) copy-start(bf16[384,768]{1,0:T(8,128)(2,1)} %get-tuple-element.89) | copy-start | bytes 1769476
  140.2 6.7 %collective-permute-start.17 = (bf16[384,768]{1,0:T(8,128)(2,1)}, bf16[384,768]{1,0:T(8,128)(2,1)S(1)}, u32[]{:S(2)}, u32[]{:S(2)}) collective-permute-start(bf16[384,768]{1,0:T(8,128)(2,1)} %get-tuple-element.92), channel_id=1, source_target_pairs={{0,1},{1,0},{2,3},{3,2},{4,5},{5,4},{6,7},{7,6},{8,9},{9,8},{10,11... | collective-permute-start | bytes 1769480 | tf_op jit(solution)/shard_map/ppermute | solution.py:37
  145.1 24.7 %collective-permute-start.22 = (bf16[384,1536]{1,0:T(8,128)(2,1)}, bf16[384,1536]{1,0:T(8,128)(2,1)}, u32[]{:S(2)}, u32[]{:S(2)}) collective-permute-start(bf16[384,1536]{1,0:T(8,128)(2,1)} %get-tuple-element.94), channel_id=1, source_target_pairs={{0,1},{1,0},{2,3},{3,2},{4,5},{5,4},{6,7},{7,6},{8,9},{9,8},{10,11... | collective-permute-start | bytes 3538952 | tf_op jit(solution)/shard_map/ppermute | solution.py:37
  145.1 29.3 %collective-permute-start.27 = (bf16[384,1536]{1,0:T(8,128)(2,1)}, bf16[384,1536]{1,0:T(8,128)(2,1)}, u32[]{:S(2)}, u32[]{:S(2)}) collective-permute-start(bf16[384,1536]{1,0:T(8,128)(2,1)} %get-tuple-element.96), channel_id=1, source_target_pairs={{0,1},{1,0},{2,3},{3,2},{4,5},{5,4},{6,7},{7,6},{8,9},{9,8},{10,11... | collective-permute-start | bytes 3538952 | tf_op jit(solution)/shard_map/ppermute | solution.py:37
  145.6 5.7 %collective-permute-start.12 = (bf16[384,768]{1,0:T(8,128)(2,1)}, bf16[384,768]{1,0:T(8,128)(2,1)}, u32[]{:S(2)}, u32[]{:S(2)}) collective-permute-start(bf16[384,768]{1,0:T(8,128)(2,1)} %get-tuple-element.90), channel_id=1, source_target_pairs={{0,1},{1,0},{2,3},{3,2},{4,5},{5,4},{6,7},{7,6},{8,9},{9,8},{10,11... | collective-permute-start | bytes 1769480 | tf_op jit(solution)/shard_map/ppermute | solution.py:37
  148.8 6.0 %copy-start.8 = (bf16[768,576]{1,0:T(8,128)(2,1)S(1)}, bf16[768,576]{1,0:T(8,128)(2,1)}, u32[]{:S(2)}) copy-start(bf16[768,576]{1,0:T(8,128)(2,1)} %get-tuple-element.97) | copy-start | bytes 2654212
  148.8 9.4 %collective-permute-start.18 = (bf16[192,768]{1,0:T(8,128)(2,1)S(1)}, bf16[192,768]{1,0:T(8,128)(2,1)S(1)}, u32[]{:S(2)}, u32[]{:S(2)}) collective-permute-start(bf16[192,768]{1,0:T(8,128)(2,1)S(1)} %get-tuple-element.107), channel_id=1, source_target_pairs={{0,4},{1,5},{2,6},{3,7},{4,0},{5,1},{6,2},{7,3},{8,12},{9,13},{10,... | collective-permute-start | bytes 884744 | tf_op jit(solution)/shard_map/ppermute | solution.py:37
  152.4 11.8 %collective-permute-start.13 = (bf16[192,768]{1,0:T(8,128)(2,1)S(1)}, bf16[192,768]{1,0:T(8,128)(2,1)S(1)}, u32[]{:S(2)}, u32[]{:S(2)}) collective-permute-start(bf16[192,768]{1,0:T(8,128)(2,1)S(1)} %get-tuple-element.109), channel_id=1, source_target_pairs={{0,24},{1,25},{2,26},{3,27},{4,28},{5,29},{6,30},{7,31},{8,16},{9,... | collective-permute-start | bytes 884744 | tf_op jit(solution)/shard_map/ppermute | solution.py:37
  155.0 23.2 %collective-permute-start.33 = (bf16[384,576]{1,0:T(8,128)(2,1)S(1)}, bf16[384,576]{1,0:T(8,128)(2,1)S(1)}, u32[]{:S(2)}, u32[]{:S(2)}) collective-permute-start(bf16[384,576]{1,0:T(8,128)(2,1)S(1)} %get-tuple-element.113), channel_id=1, source_target_pairs={{0,8},{1,9},{2,10},{3,11},{4,12},{5,13},{6,14},{7,15},{8,0},{9,1},... | collective-permute-start | bytes 1327112 | tf_op jit(solution)/shard_map/ppermute | solution.py:37
  158.2 11.5 %copy-start.5 = (bf16[384,1536]{1,0:T(8,128)(2,1)S(1)}, bf16[384,1536]{1,0:T(8,128)(2,1)}, u32[]{:S(2)}) copy-start(bf16[384,1536]{1,0:T(8,128)(2,1)} %get-tuple-element.93) | copy-start | bytes 3538948
  158.3 20.7 %collective-permute-start.19 = (bf16[96,768]{1,0:T(8,128)(2,1)S(1)}, bf16[96,768]{1,0:T(8,128)(2,1)S(1)}, u32[]{:S(2)}, u32[]{:S(2)}) collective-permute-start(bf16[96,768]{1,0:T(8,128)(2,1)S(1)} %get-tuple-element.121), channel_id=1, source_target_pairs={{0,2},{1,3},{2,0},{3,1},{4,6},{5,7},{6,4},{7,5},{8,10},{9,11},{10,... | collective-permute-start | bytes 442376 | tf_op jit(solution)/shard_map/ppermute | solution.py:37
  164.3 16.6 %collective-permute-start.14 = (bf16[96,768]{1,0:T(8,128)(2,1)S(1)}, bf16[96,768]{1,0:T(8,128)(2,1)S(1)}, u32[]{:S(2)}, u32[]{:S(2)}) collective-permute-start(bf16[96,768]{1,0:T(8,128)(2,1)S(1)} %get-tuple-element.123), channel_id=1, source_target_pairs={{0,8},{1,9},{2,10},{3,11},{4,12},{5,13},{6,14},{7,15},{8,0},{9,1},... | collective-permute-start | bytes 442376 | tf_op jit(solution)/shard_map/ppermute | solution.py:37
  169.7 4.7 %copy-start.4 = (bf16[384,1536]{1,0:T(8,128)(2,1)S(1)}, bf16[384,1536]{1,0:T(8,128)(2,1)}, u32[]{:S(2)}) copy-start(bf16[384,1536]{1,0:T(8,128)(2,1)} %get-tuple-element.95) | copy-start | bytes 3538948
  172.2 43.0 %collective-permute-start.23 = (bf16[192,1536]{1,0:T(8,128)(2,1)}, bf16[192,1536]{1,0:T(8,128)(2,1)}, u32[]{:S(2)}, u32[]{:S(2)}) collective-permute-start(bf16[192,1536]{1,0:T(8,128)(2,1)} %get-tuple-element.99), channel_id=1, source_target_pairs={{0,2},{1,3},{2,0},{3,1},{4,6},{5,7},{6,4},{7,5},{8,10},{9,11},{10,... | collective-permute-start | bytes 1769480 | tf_op jit(solution)/shard_map/ppermute | solution.py:37
  176.8 41.4 %collective-permute-start.28 = (bf16[192,1536]{1,0:T(8,128)(2,1)}, bf16[192,1536]{1,0:T(8,128)(2,1)S(1)}, u32[]{:S(2)}, u32[]{:S(2)}) collective-permute-start(bf16[192,1536]{1,0:T(8,128)(2,1)} %get-tuple-element.101), channel_id=1, source_target_pairs={{0,4},{1,5},{2,6},{3,7},{4,0},{5,1},{6,2},{7,3},{8,12},{9,13},{10,... | collective-permute-start | bytes 1769480 | tf_op jit(solution)/shard_map/ppermute | solution.py:37
  178.3 24.1 %collective-permute-start.34 = (bf16[192,576]{1,0:T(8,128)(2,1)S(1)}, bf16[192,576]{1,0:T(8,128)(2,1)S(1)}, u32[]{:S(2)}, u32[]{:S(2)}) collective-permute-start(bf16[192,576]{1,0:T(8,128)(2,1)S(1)} %get-tuple-element.111), channel_id=1, source_target_pairs={{0,4},{1,5},{2,6},{3,7},{4,0},{5,1},{6,2},{7,3},{8,12},{9,13},{10,... | collective-permute-start | bytes 663560 | tf_op jit(solution)/shard_map/ppermute | solution.py:37
  179.0 6.2 %collective-permute-start.20 = (bf16[48,768]{1,0:T(8,128)(2,1)S(1)}, bf16[48,768]{1,0:T(8,128)(2,1)S(1)}, u32[]{:S(2)}, u32[]{:S(2)}) collective-permute-start(bf16[48,768]{1,0:T(8,128)(2,1)S(1)} %get-tuple-element.127), channel_id=1, source_target_pairs={{0,24},{1,25},{2,26},{3,27},{4,28},{5,29},{6,30},{7,31},{8,16},{9,... | collective-permute-start | bytes 221192 | tf_op jit(solution)/shard_map/ppermute | solution.py:37
  180.9 17.1 %collective-permute-start.15 = (bf16[48,768]{1,0:T(8,128)(2,1)S(1)}, bf16[48,768]{1,0:T(8,128)(2,1)S(1)}, u32[]{:S(2)}, u32[]{:S(2)}) collective-permute-start(bf16[48,768]{1,0:T(8,128)(2,1)S(1)} %get-tuple-element.129), channel_id=1, source_target_pairs={{0,4},{1,5},{2,6},{3,7},{4,0},{5,1},{6,2},{7,3},{8,12},{9,13},{10,... | collective-permute-start | bytes 221192 | tf_op jit(solution)/shard_map/ppermute | solution.py:37
  185.3 13.2 %collective-permute-start.21 = (bf16[24,768]{1,0:T(8,128)(2,1)S(1)}, bf16[24,768]{1,0:T(8,128)(2,1)S(1)}, u32[]{:S(2)}, u32[]{:S(2)}) collective-permute-start(bf16[24,768]{1,0:T(8,128)(2,1)S(1)} %fusion.27), channel_id=1, source_target_pairs={{0,8},{1,9},{2,10},{3,11},{4,12},{5,13},{6,14},{7,15},{8,0},{9,1},... | collective-permute-start | bytes 110600 | tf_op jit(solution)/shard_map/ppermute | solution.py:37
  198.1 4.3 %collective-permute-start.16 = (bf16[24,768]{1,0:T(8,128)(2,1)S(1)}, bf16[24,768]{1,0:T(8,128)(2,1)S(1)}, u32[]{:S(2)}, u32[]{:S(2)}) collective-permute-start(bf16[24,768]{1,0:T(8,128)(2,1)S(1)} %fusion.30), channel_id=1, source_target_pairs={{0,2},{1,3},{2,0},{3,1},{4,6},{5,7},{6,4},{7,5},{8,10},{9,11},{10,... | collective-permute-start | bytes 110600 | tf_op jit(solution)/shard_map/ppermute | solution.py:37
  202.5 4.9 %collective-permute-start.35 = (bf16[96,576]{1,0:T(8,128)(2,1)S(1)}, bf16[96,576]{1,0:T(8,128)(2,1)S(1)}, u32[]{:S(2)}, u32[]{:S(2)}) collective-permute-start(bf16[96,576]{1,0:T(8,128)(2,1)S(1)} %get-tuple-element.125), channel_id=1, source_target_pairs={{0,2},{1,3},{2,0},{3,1},{4,6},{5,7},{6,4},{7,5},{8,10},{9,11},{10,... | collective-permute-start | bytes 331784 | tf_op jit(solution)/shard_map/ppermute | solution.py:37
  208.1 6.3 %collective-permute-start.36 = (bf16[48,576]{1,0:T(8,128)(2,1)}, bf16[48,576]{1,0:T(8,128)(2,1)S(1)}, u32[]{:S(2)}, u32[]{:S(2)}) collective-permute-start(bf16[48,576]{1,0:T(8,128)(2,1)} %fusion.25), channel_id=1, source_target_pairs={{0,24},{1,25},{2,26},{3,27},{4,28},{5,29},{6,30},{7,31},{8,16},{9,... | collective-permute-start | bytes 165896 | tf_op jit(solution)/shard_map/ppermute | solution.py:37
  216.3 11.1 %collective-permute-start.24 = (bf16[96,1536]{1,0:T(8,128)(2,1)S(1)}, bf16[96,1536]{1,0:T(8,128)(2,1)S(1)}, u32[]{:S(2)}, u32[]{:S(2)}) collective-permute-start(bf16[96,1536]{1,0:T(8,128)(2,1)S(1)} %get-tuple-element.103), channel_id=1, source_target_pairs={{0,24},{1,25},{2,26},{3,27},{4,28},{5,29},{6,30},{7,31},{8,16},{9,... | collective-permute-start | bytes 884744 | tf_op jit(solution)/shard_map/ppermute | solution.py:37
  218.3 9.2 %collective-permute-start.29 = (bf16[96,1536]{1,0:T(8,128)(2,1)S(1)}, bf16[96,1536]{1,0:T(8,128)(2,1)S(1)}, u32[]{:S(2)}, u32[]{:S(2)}) collective-permute-start(bf16[96,1536]{1,0:T(8,128)(2,1)S(1)} %get-tuple-element.105), channel_id=1, source_target_pairs={{0,2},{1,3},{2,0},{3,1},{4,6},{5,7},{6,4},{7,5},{8,10},{9,11},{10,... | collective-permute-start | bytes 884744 | tf_op jit(solution)/shard_map/ppermute | solution.py:37
  227.4 5.5 %collective-permute-start.25 = (bf16[48,1536]{1,0:T(8,128)(2,1)S(1)}, bf16[48,1536]{1,0:T(8,128)(2,1)S(1)}, u32[]{:S(2)}, u32[]{:S(2)}) collective-permute-start(bf16[48,1536]{1,0:T(8,128)(2,1)S(1)} %get-tuple-element.117), channel_id=1, source_target_pairs={{0,8},{1,9},{2,10},{3,11},{4,12},{5,13},{6,14},{7,15},{8,0},{9,1},... | collective-permute-start | bytes 442376 | tf_op jit(solution)/shard_map/ppermute | solution.py:37
  227.6 7.1 %collective-permute-start.30 = (bf16[48,1536]{1,0:T(8,128)(2,1)S(1)}, bf16[48,1536]{1,0:T(8,128)(2,1)S(1)}, u32[]{:S(2)}, u32[]{:S(2)}) collective-permute-start(bf16[48,1536]{1,0:T(8,128)(2,1)S(1)} %get-tuple-element.119), channel_id=1, source_target_pairs={{0,24},{1,25},{2,26},{3,27},{4,28},{5,29},{6,30},{7,31},{8,16},{9,... | collective-permute-start | bytes 442376 | tf_op jit(solution)/shard_map/ppermute | solution.py:37
  233.0 4.4 %collective-permute-start.26 = (bf16[24,1536]{1,0:T(8,128)(2,1)S(1)}, bf16[24,1536]{1,0:T(8,128)(2,1)S(1)}, u32[]{:S(2)}, u32[]{:S(2)}) collective-permute-start(bf16[24,1536]{1,0:T(8,128)(2,1)S(1)} %get-tuple-element.131), channel_id=1, source_target_pairs={{0,4},{1,5},{2,6},{3,7},{4,0},{5,1},{6,2},{7,3},{8,12},{9,13},{10,... | collective-permute-start | bytes 221192 | tf_op jit(solution)/shard_map/ppermute | solution.py:37
  234.7 4.4 %collective-permute-start.31 = (bf16[24,1536]{1,0:T(8,128)(2,1)S(1)}, bf16[24,1536]{1,0:T(8,128)(2,1)S(1)}, u32[]{:S(2)}, u32[]{:S(2)}) collective-permute-start(bf16[24,1536]{1,0:T(8,128)(2,1)S(1)} %get-tuple-element.133), channel_id=1, source_target_pairs={{0,8},{1,9},{2,10},{3,11},{4,12},{5,13},{6,14},{7,15},{8,0},{9,1},... | collective-permute-start | bytes 221192 | tf_op jit(solution)/shard_map/ppermute | solution.py:37
Sparse Core Ops, SparseCore 0:
  11.5 79.4 all-gather.1
